TPU v7x, 32 devices: a whole 2x2x4 slice. The times are simulated.
32 devices in a mesh: dp: 8 (over z, y), tensor: 4 (over x, core).
Axes of the slice: x: 2, y: 2, z: 4, core: 2. Of those that a mesh axis runs over, the one named last changes fastest.
Arguments:
- tokens: bfloat16 [8, 2048, 768], P('dp', 'tensor'), may hold values from -6 to 6
- segment_ids: int32 [8, 2048], P('dp'), may hold values from 0 to 7, never falling along the last dimension, each value on 1 to 1024 neighbouring positions
- cotangent: bfloat16 [8, 2048, 768], P('dp', 'tensor'), may hold values from -6 to 6
- attention_norm1_gain: bfloat16 [768], replicated, may hold values from 0.5 to 1.5
- attention_norm1_bias: bfloat16 [768], replicated, may hold values from -3 to 3
- feedforward_norm2_gain: bfloat16 [768], replicated, may hold values from 0.5 to 1.5
- feedforward_norm2_bias: bfloat16 [768], replicated, may hold values from -3 to 3
- qkv_weight: bfloat16 [768, 2304], P(None, 'tensor'), may hold values from -0.21875 to 0.21875
- qkv_bias: bfloat16 [2304], P('tensor'), may hold values from -3 to 3
- dense_weight: bfloat16 [768, 768], P('tensor'), may hold values from -2.5 to 2.5
- dense_bias: bfloat16 [768], replicated, may hold values from -3 to 3
- fc_in_weight: bfloat16 [768, 3072], P(None, 'tensor'), may hold values from -0.21875 to 0.21875
- fc_in_bias: bfloat16 [3072], P('tensor'), may hold values from -3 to 3
- fc_out_weight: bfloat16 [3072, 768], P('tensor'), may hold values from -0.109375 to 0.109375
- fc_out_bias: bfloat16 [768], replicated, may hold values from -3 to 3
Outputs:
- result: bfloat16 [8, 2048, 768], P('dp', 'tensor')
- tokens_grad: float32 [8, 2048, 768], P('dp', 'tensor')
- ln1_gain_grad: float32 [768], replicated
- ln1_bias_grad: float32 [768], replicated
- ln2_gain_grad: float32 [768], replicated
- ln2_bias_grad: float32 [768], replicated
- qkv_weight_grad: float32 [768, 2304], P(None, 'tensor')
- qkv_bias_grad: float32 [2304], P('tensor')
- dense_weight_grad: float32 [768, 768], P('tensor')
- dense_bias_grad: float32 [768], replicated
- fc_in_weight_grad: float32 [768, 3072], P(None, 'tensor')
- fc_in_bias_grad: float32 [3072], P('tensor')
- fc_out_weight_grad: float32 [3072, 768], P('tensor')
- fc_out_bias_grad: float32 [768], replicated
Inputs may be any that keep to these rules, and one draw needn't show every extreme that they name: `segment_ids`: along a row segment numbers never fall; each of the 8 numbers covers 1 to 1024 positions of every row, one exactly 1024.
All inputs are finite; a program needn't handle non-finite values.
Results may differ from a plain program's by a relative error of at most 0.013.
Values may be sent and summed in bfloat16 or wider, within the bound.
No kernel may reach another device: no remote copies, remote signals or barrier semaphores. Data moves between devices by JAX's collectives and lax.ppermute only.
A program may use at most 128 MiB of HBM per device.

v0:
```python
from functools import partial

import jax
import jax.numpy as jnp
import numpy as np
from jax import lax
from jax.experimental import pallas as pl
from jax.experimental.pallas import tpu as pltpu
from jax.sharding import PartitionSpec as P

HEAD_DIM = 64
ROT = 16
SEGS = 8
BLK = 256
NEG = -1e30
LOG2E = 1.4426950408889634
f32, bf16, i32 = jnp.float32, jnp.bfloat16, jnp.int32
VMEM = pl.BlockSpec(memory_space=pltpu.VMEM)
SMEM = pl.BlockSpec(memory_space=pltpu.SMEM)
MIB = 1 << 20


def dot(a, b):
    return jnp.dot(a, b, preferred_element_type=f32)


def dot_nt(a, b):
    return lax.dot_general(a, b, (((1,), (1,)), ((), ())), preferred_element_type=f32)


def dot_tn(a, b):
    return lax.dot_general(a, b, (((0,), (0,)), ((), ())), preferred_element_type=f32)


def like(shape, dtype):
    return jax.ShapeDtypeStruct(shape, dtype)


def call(kernel, name, inputs, outs, scratch=(), limit=8, flops=0, moved=1_000_000, smem=(), smem_out=()):
    return pl.pallas_call(
        kernel,
        out_shape=tuple(outs),
        in_specs=[SMEM if i in smem else VMEM for i in range(len(inputs))],
        out_specs=tuple(SMEM if i in smem_out else VMEM for i in range(len(outs))),
        scratch_shapes=list(scratch),
        compiler_params=pltpu.CompilerParams(vmem_limit_bytes=limit * MIB),
        cost_estimate=pl.CostEstimate(flops=flops, bytes_accessed=moved, transcendentals=0),
        name=name,
    )(*inputs)


def row_of(ref):
    return ref[...].astype(f32).reshape(1, -1)


def column_of(row):
    return jnp.broadcast_to(row, (128, row.shape[1])).T[:, 0:1]


def pair_rows(rows):
    rows = jnp.concatenate(rows, axis=0)
    high = rows.astype(bf16)
    return jnp.concatenate([high, (rows - high.astype(f32)).astype(bf16)], axis=0)


def segments_kernel(ids_ref, first_ref, start_ref, lo_ref):
    ids = ids_ref[...]
    start = jnp.zeros_like(ids)
    begins = []
    for s in range(SEGS):
        begin = jnp.sum(jnp.where(ids < s, 1.0, 0.0)).astype(i32)
        begins.append(begin)
        start = jnp.where(ids == s, begin, start)
    start_ref[...] = start
    for i in range(lo_ref.shape[0]):
        seg = first_ref[0, i * BLK]
        lo = begins[0]
        for s in range(1, SEGS):
            lo = jnp.where(seg == s, begins[s], lo)
        lo_ref[i] = lax.div(lo, BLK)


def front_kernel(
    place_ref, x0_ref, x1_ref, g1_ref, b1_ref, g2_ref, b2_ref, w1_ref, c1_ref, wq_ref, bq_ref,
    cos_ref, sin_ref, xh_ref, act_ref, slope_ref, qkv_ref, *, first,
):
    heads = qkv_ref.shape[0]
    half = ROT // 2
    rows = x0_ref.shape[0]
    g1, b1, g2, b2, c1 = [row_of(r) for r in (g1_ref, b1_ref, g2_ref, b2_ref, c1_ref)]
    for piece, x_ref in enumerate((x0_ref, x1_ref)):
        out = slice(piece * rows, (piece + 1) * rows)
        at = (place_ref[0] ^ (first + piece)) * rows
        here = pl.ds(pl.multiple_of(at, 128), rows)
        x = x_ref[...].astype(f32)
        c = x - jnp.mean(x, axis=1, keepdims=True)
        xh = c * lax.rsqrt(jnp.mean(c * c, axis=1, keepdims=True) + 1e-05)
        xh_ref[out, :] = xh.astype(bf16)
        h1 = (xh * g1 + b1).astype(bf16)
        h2 = (xh * g2 + b2).astype(bf16)
        pre = dot(h2, w1_ref[...]) + c1
        qkv = dot_nt(wq_ref[...], h1) + bq_ref[...]
        cosine, sine = cos_ref[:, here], sin_ref[:, here]
        for h in range(heads):
            for part in range(3):
                at = (3 * h + part) * HEAD_DIM
                v = qkv[at : at + HEAD_DIM]
                if part < 2:
                    one, two = v[:half], v[half:ROT]
                    v = jnp.concatenate(
                        [one * cosine - two * sine, two * cosine + one * sine, v[ROT:]], axis=0
                    )
                if part == 0:
                    v = v * HEAD_DIM ** (-0.5)
                qkv_ref[h, part, :, out] = v.astype(bf16)
        cdf = 0.5 + 0.5 * lax.erf(pre * 0.5**0.5)
        pdf = jnp.exp(pre * pre * -0.5) * (2.0 * np.pi) ** -0.5
        act_ref[out, :] = (pre * cdf).astype(bf16)
        slope_ref[out, :] = (cdf + pre * pdf).astype(bf16)


def halves(payload_ref, keep_ref, send_ref, side):
    rows = keep_ref.shape[0]
    keep_ref[...] = payload_ref[pl.ds(pl.multiple_of(side * rows, 16), rows), :]
    send_ref[...] = payload_ref[pl.ds(pl.multiple_of((1 - side) * rows, 16), rows), :]


def ff_back_kernel(*refs, last):
    place_ref, refs = refs[0], refs[1:]
    ins = refs[:9]
    dy0_ref, dy1_ref, act_ref, slope_ref, xh_ref, g2_ref, w1_ref, w2_ref, wd_ref = ins
    refs = refs[9:]
    if last:
        b2_ref, w1_in, w2_in, sums_in = refs[:4]
        refs = refs[4:]
        out_ref, back_ref, do_ref, k1_ref, s1_ref, k2_ref, s2_ref, sums_ref = refs[:8]
        w1g_ref, w2g_ref, pay_ref = refs[8:]
    else:
        out_ref, back_ref, do_ref, w1g_ref, w2g_ref, sums_ref = refs
    rows = dy0_ref.shape[0]
    g2 = row_of(g2_ref)
    sums = [sums_in[i : i + 1, :] for i in range(2)] if last else [0.0, 0.0]
    for piece, dy_ref in enumerate((dy0_ref, dy1_ref)):
        r = slice(piece * rows, (piece + 1) * rows)
        dy = dy_ref[...]
        act = act_ref[r, :]
        du = (dot_nt(dy, w2_ref[...]) * slope_ref[r, :].astype(f32)).astype(bf16)
        w2_part = dot_tn(act, dy)
        w1_part = dot_tn(xh_ref[r, :], du)
        if piece == 0:
            w2g_ref[...] = w2_in[...] + w2_part if last else w2_part
            w1g_ref[...] = w1_in[...] + w1_part if last else w1_part
        else:
            w2g_ref[...] += w2_part
            w1g_ref[...] += w1_part
        out_ref[r, :] = dot(act, w2_ref[...]).astype(bf16)
        back_ref[r, :] = (dot_nt(du, w1_ref[...]) * g2).astype(bf16)
        do_ref[:, r] = dot_nt(wd_ref[...], dy).astype(bf16)
        sums[0] = sums[0] + jnp.sum(du.astype(f32), axis=0, keepdims=True)
        sums[1] = sums[1] + jnp.sum(dy.astype(f32), axis=0, keepdims=True)
    sums_ref[0:1, :] = sums[0]
    sums_ref[1:2, :] = sums[1]
    if last:
        side = lax.rem(place_ref[1], 2)
        pay_ref[...] = w2g_ref[...].astype(bf16)
        halves(pay_ref, k2_ref, s2_ref, side)
        du_sum = jnp.broadcast_to(sums[0], (8, sums[0].shape[1]))
        high = du_sum.astype(bf16)
        low = (du_sum - high.astype(f32)).astype(bf16)
        sums_ref[3:4, :] = (dot_nt(high, w1_ref[...]) + dot_nt(low, w1_ref[...]))[0:1]
        raw = w1g_ref[...]
        gain = jnp.sum(raw * w1_ref[...].astype(f32), axis=1, keepdims=True)
        sums_ref[2:3, :] = jnp.broadcast_to(gain, (gain.shape[0], 128)).T[0:1, :]
        pay_ref[...] = (raw * column_of(g2) + column_of(row_of(b2_ref)) * sums[0]).astype(bf16)
        halves(pay_ref, k1_ref, s1_ref, side)


def blocks(place_ref, count, per):
    def phys(j):
        return pl.ds(
            pl.multiple_of(((lax.div(j, per) ^ place_ref[0]) * per + lax.rem(j, per)) * BLK, BLK),
            BLK,
        )

    return phys


def attend_kernel(
    place_ref, lo_ref, start_ref, left_ref, right_ref, outl_ref, outr_ref,
    dy0_ref, dy1_ref, dy2_ref, dy3_ref, wd_ref,
    qkv_ref, o_ref, lse_ref, keep0_ref, keep2_ref, send_ref, wdg_ref, kn_ref,
):
    heads, seq = qkv_ref.shape[0], qkv_ref.shape[3]
    count, rows = seq // BLK, keep0_ref.shape[0]
    phys = blocks(place_ref, count, rows // BLK)
    qkv_ref[:, :, :, : seq // 2] = left_ref[...]
    qkv_ref[:, :, :, seq // 2 :] = right_ref[...]
    for h in range(heads):
        for b in range(count):
            r = slice(b * BLK, (b + 1) * BLK)
            kn_ref[h, r, :] = qkv_ref[h, 1, :, r].T
    ik = lax.broadcasted_iota(i32, (BLK, BLK), 0)
    iq = lax.broadcasted_iota(i32, (BLK, BLK), 1)

    @pl.loop(0, count)
    def _(i):
        qs = phys(i)
        start = start_ref[0:1, pl.ds(pl.multiple_of(i * BLK, BLK), BLK)]

        def step(ks, mask, carry):
            scores = [
                jnp.where(mask, dot(kn_ref[h, ks, :], qkv_ref[h, 0, :, qs]), NEG)
                for h in range(heads)
            ]
            out = []
            for h in range(heads):
                top = jnp.max(scores[h], axis=0, keepdims=True)
                if carry is not None:
                    top = jnp.maximum(top, carry[h][0])
                expo = jnp.exp2(scores[h] * LOG2E - top * LOG2E)
                total = jnp.sum(expo, axis=0, keepdims=True)
                mixed = dot(qkv_ref[h, 2, :, ks], expo.astype(bf16))
                if carry is not None:
                    fade = jnp.exp2((carry[h][0] - top) * LOG2E)
                    total = total + carry[h][1] * fade
                    mixed = mixed + carry[h][2] * fade
                out.append((top, total, mixed))
            return tuple(out)

        carry = step(qs, (ik <= iq) & (ik >= start - i * BLK), None)
        carry = lax.fori_loop(
            lo_ref[i], i, lambda j, c: step(phys(j), ik >= start - j * BLK, c), carry
        )
        for h in range(heads):
            top, total, mixed = carry[h]
            at = slice(h * HEAD_DIM, (h + 1) * HEAD_DIM)
            o_ref[at, qs] = (mixed * (1.0 / total)).astype(bf16)
            lse_ref[h, 0:1, qs] = top * LOG2E + jnp.log2(total)

    dys = (dy0_ref, dy1_ref, dy2_ref, dy3_ref)
    wdg = None
    for k in range(4):
        r = slice(k * rows, (k + 1) * rows)
        o = o_ref[:, r]
        side = outl_ref if k < 2 else outr_ref
        at = slice((k % 2) * rows, (k % 2 + 1) * rows)
        total = side[at, :].astype(f32) + dot_tn(o, wd_ref[...])
        if k == 0:
            keep0_ref[...] = total
        elif k == 2:
            keep2_ref[...] = total
        else:
            send_ref[(k // 2) * rows : (k // 2 + 1) * rows, :] = total.astype(bf16)
        part = dot(o, dys[k][...])
        wdg = part if k == 0 else wdg + part
    wdg_ref[...] = wdg.astype(bf16)


def attend_back_kernel(
    place_ref, lo_ref, start_ref, qkv_ref, o_ref, dol_ref, dor_ref, lse_ref, cos_ref, sin_ref,
    xhl_ref, xhr_ref, wq_ref, g1_ref, b1_ref, wdg_ref, sums_ref,
    dqkv_ref, keep_ref, send_ref, do_ref, kn_ref, vn_ref, dk_ref, dv_ref, pay_ref,
):
    heads, seq = qkv_ref.shape[0], qkv_ref.shape[3]
    count = seq // BLK
    phys = blocks(place_ref, count, count // 4)
    half = ROT // 2
    do_ref[:, : seq // 2] = dol_ref[...]
    do_ref[:, seq // 2 :] = dor_ref[...]
    for h in range(heads):
        for b in range(count):
            r = slice(b * BLK, (b + 1) * BLK)
            kn_ref[h, r, :] = qkv_ref[h, 1, :, r].T
            vn_ref[h, r, :] = qkv_ref[h, 2, :, r].T
    dk_ref[...] = jnp.zeros_like(dk_ref)
    dv_ref[...] = jnp.zeros_like(dv_ref)
    ik = lax.broadcasted_iota(i32, (BLK, BLK), 0)
    iq = lax.broadcasted_iota(i32, (BLK, BLK), 1)

    def unrotate(grad, cosine, sine):
        one, two = grad[:half], grad[half:ROT]
        return jnp.concatenate(
            [one * cosine + two * sine, two * cosine - one * sine, grad[ROT:]], axis=0
        )

    @pl.loop(0, count)
    def _(i):
        qs = phys(i)
        here = pl.ds(pl.multiple_of(i * BLK, BLK), BLK)
        start = start_ref[0:1, here]
        dos = [do_ref[h * HEAD_DIM : (h + 1) * HEAD_DIM, qs] for h in range(heads)]
        delta = [
            jnp.sum(
                dos[h].astype(f32) * o_ref[h * HEAD_DIM : (h + 1) * HEAD_DIM, qs].astype(f32),
                axis=0, keepdims=True,
            )
            for h in range(heads)
        ]
        lse = [lse_ref[h, 0:1, qs] for h in range(heads)]

        def step(ks, mask, carry):
            scores = [
                jnp.where(mask, dot(kn_ref[h, ks, :], qkv_ref[h, 0, :, qs]), NEG)
                for h in range(heads)
            ]
            dprobs = [dot(vn_ref[h, ks, :], dos[h]) for h in range(heads)]
            probs = [jnp.exp2(scores[h] * LOG2E - lse[h]) for h in range(heads)]
            dscores = [(probs[h] * (dprobs[h] - delta[h])).astype(bf16) for h in range(heads)]
            out = []
            for h in range(heads):
                dv_ref[h, :, ks] += dot_nt(dos[h], probs[h].astype(bf16))
                dk_ref[h, :, ks] += dot_nt(qkv_ref[h, 0, :, qs], dscores[h])
                dq = dot(qkv_ref[h, 1, :, ks], dscores[h])
                out.append(dq if carry is None else carry[h] + dq)
            return tuple(out)

        carry = step(qs, (ik <= iq) & (ik >= start - i * BLK), None)
        carry = lax.fori_loop(
            lo_ref[i], i, lambda j, c: step(phys(j), ik >= start - j * BLK, c), carry
        )
        for h in range(heads):
            dq = unrotate(carry[h] * HEAD_DIM ** (-0.5), cos_ref[:, here], sin_ref[:, here])
            dqkv_ref[h, 0, :, qs] = dq.astype(bf16)

    @pl.loop(0, count)
    def _(i):
        qs = phys(i)
        here = pl.ds(pl.multiple_of(i * BLK, BLK), BLK)
        for h in range(heads):
            dk = unrotate(dk_ref[h, :, qs], cos_ref[:, here], sin_ref[:, here])
            dqkv_ref[h, 1, :, qs] = dk.astype(bf16)
            dqkv_ref[h, 2, :, qs] = dv_ref[h, :, qs].astype(bf16)

    g1, b1 = row_of(g1_ref), row_of(b1_ref)
    cols = 3 * HEAD_DIM
    gain, bias, bq = 0.0, 0.0, []
    for h in range(heads):
        grad = dqkv_ref[h].reshape(cols, seq)
        raw = dot(grad[:, : seq // 2], xhl_ref[...]) + dot(grad[:, seq // 2 :], xhr_ref[...])
        total = jnp.sum(grad.astype(f32), axis=1, keepdims=True)
        bq.append(jnp.broadcast_to(total, (cols, 128)).T[0:1, :])
        pay_ref[h * cols : (h + 1) * cols, :] = (raw * g1 + total * b1).astype(bf16)
        weight = wq_ref[h * cols : (h + 1) * cols, :].astype(f32)
        gain = gain + jnp.sum(weight * raw, axis=0, keepdims=True)
        bias = bias + jnp.sum(weight * total, axis=0, keepdims=True)
    pay_ref[heads * cols :, :] = wdg_ref[...]
    width = pay_ref.shape[1]
    zeros = jnp.zeros((1, width - heads * cols), f32)
    vectors = pair_rows(
        [
            gain, bias, sums_ref[2:3, :], sums_ref[3:4, :], sums_ref[1:2, :], sums_ref[0:1, :],
            jnp.concatenate(bq + [zeros], axis=1), jnp.zeros((1, width), f32),
        ]
    )
    side = lax.rem(place_ref[1], 2)
    rows = pay_ref.shape[0] // 2
    halves(pay_ref, keep_ref.at[0:rows], send_ref.at[0:rows], side)
    keep_ref[rows:, :] = vectors
    send_ref[rows:, :] = vectors


def tokens_back_kernel(
    dqkv_ref, backl_ref, backr_ref, wq_ref, g1_ref, keep0_ref, keep2_ref, send_ref
):
    rows = keep0_ref.shape[0]
    g1 = row_of(g1_ref)
    cols, seq = wq_ref.shape[0], dqkv_ref.shape[3]
    for k in range(4):
        grad = dqkv_ref[:, :, :, k * rows : (k + 1) * rows].reshape(cols, rows)
        side = backl_ref if k < 2 else backr_ref
        at = slice((k % 2) * rows, (k % 2 + 1) * rows)
        total = side[at, :].astype(f32) + dot_tn(grad, wq_ref[...]) * g1
        if k == 0:
            keep0_ref[...] = total
        elif k == 2:
            keep2_ref[...] = total
        else:
            send_ref[(k // 2) * rows : (k // 2 + 1) * rows, :] = total.astype(bf16)


def forward_kernel(keep2_ref, got_ref, sent_ref):
    rows = keep2_ref.shape[0]
    sent_ref[...] = (keep2_ref[...] + got_ref[rows:, :].astype(f32)).astype(bf16)


def result_kernel(x_ref, keep0_ref, got_ref, far_ref, bd_ref, c2_ref, out_ref):
    rows = x_ref.shape[0]
    summed = keep0_ref[...] + got_ref[:rows, :].astype(f32) + far_ref[...].astype(f32)
    out_ref[...] = (x_ref[...].astype(f32) + summed + (row_of(bd_ref) + row_of(c2_ref))).astype(bf16)


def tokens_grad_kernel(x_ref, dy_ref, keep0_ref, got_ref, far_ref, out_ref):
    rows = x_ref.shape[0]
    grad = keep0_ref[...] + got_ref[:rows, :].astype(f32) + far_ref[...].astype(f32)
    x = x_ref[...].astype(f32)
    c = x - jnp.mean(x, axis=1, keepdims=True)
    inverse = lax.rsqrt(jnp.mean(c * c, axis=1, keepdims=True) + 1e-05)
    xh = c * inverse
    term = grad - jnp.mean(grad, axis=1, keepdims=True)
    term = term - xh * jnp.mean(grad * xh, axis=1, keepdims=True)
    out_ref[...] = dy_ref[...].astype(f32) + inverse * term


def swap(value, axis, size, distance):
    return lax.ppermute(value, axis, [(i, i ^ distance) for i in range(size)])


def shifted(value, size, stride, factor, shift):
    pairs = []
    for i in range(size):
        digit = (i // stride) % factor
        pairs.append((i, i + ((digit + shift) % factor - digit) * stride))
    return lax.ppermute(value, "dp", pairs)


def unpair(rows):
    return rows[0:8, :].astype(f32) + rows[8:16, :].astype(f32)


def split_kernel(place_ref, keep_ref, got_ref, *out_refs, stride, tail):
    factor = len(out_refs)
    digit = lax.rem(lax.div(place_ref[1], stride), factor)
    rows = (keep_ref.shape[0] - tail) // factor
    for s in range(factor):
        at = pl.ds(pl.multiple_of(lax.rem(digit + s, factor) * rows, 8), rows)
        out_refs[s][0:rows, :] = (keep_ref[at, :].astype(f32) + got_ref[at, :].astype(f32)).astype(bf16)
        if tail:
            total = unpair(keep_ref[factor * rows :, :]) + unpair(got_ref[factor * rows :, :])
            out_refs[s][rows:, :] = pair_rows([total])


def total_kernel(*refs, tail):
    ins = refs[:-2] if tail else refs[:-1]
    out_ref = refs[len(ins)]
    rows = out_ref.shape[0]
    total = ins[0][0:rows, :].astype(f32)
    for r in ins[1:]:
        total = total + r[0:rows, :].astype(f32)
    out_ref[...] = total.astype(bf16)
    if tail:
        vectors = unpair(ins[0][rows:, :])
        for r in ins[1:]:
            vectors = vectors + unpair(r[rows:, :])
        refs[-1][...] = vectors


def place_kernel(place_ref, mine_ref, got_ref, *out_refs, stride, factor):
    digit = lax.rem(lax.div(place_ref[1], stride), factor)
    side = lax.rem(place_ref[1], 2)
    rows = mine_ref.shape[0] // factor
    out_ref = out_refs[-1]
    for s in range(factor):
        chunk = lax.rem(digit + factor - s, factor)
        for part, ref in ((side, mine_ref), (1 - side, got_ref)):
            at = pl.ds(pl.multiple_of((part * factor + chunk) * rows, 8), rows)
            out_ref[at, :] = ref[s * rows : (s + 1) * rows, :].astype(f32)
    if len(out_refs) > 1:
        split = out_refs[0].shape[0]
        out_refs[0][...] = out_ref[:split, :]
        out_refs[1][...] = out_ref[split:, :]


def reduce_pieces(place, keep, got, dp, tail):
    stride, factor = 2, 4
    rows = (keep.shape[0] - tail) // factor
    width = keep.shape[1]
    pieces = call(
        partial(split_kernel, stride=stride, tail=tail), "split", [place, keep, got],
        [like((rows + tail, width), bf16)] * factor, smem=(0,),
    )
    parts = [pieces[0]] + [
        shifted(pieces[s], dp, stride, factor, s) for s in range(1, factor)
    ]
    outs = [like((rows, width), bf16)] + ([like((8, width), f32)] if tail else [])
    return call(partial(total_kernel, tail=tail), "total", parts, outs)


def spread_pieces(total, dp):
    stride, factor = 2, 4
    pieces = [total] + [shifted(total, dp, stride, factor, s) for s in range(1, factor)]
    return jnp.concatenate(pieces, axis=0)


def settle(place, mine, got, outs, limit=8):
    scratch = [pltpu.VMEM((2 * mine.shape[0], mine.shape[1]), f32)] if len(outs) > 1 else []
    return call(
        partial(place_kernel, stride=2, factor=4), "place", [place, mine, got], outs, scratch,
        smem=(0,), limit=limit,
    )


def rest_sum(value, dp):
    if dp == 8:
        return value
    groups = [[i + 8 * j for j in range(dp // 8)] for i in range(8)]
    return lax.psum(value, "dp", axis_index_groups=groups)


def rotary_tables(length):
    half = ROT // 2
    freq = np.float32(10000.0) ** (-(np.arange(half, dtype=np.float32) * 2.0) / ROT)
    angle = freq.astype(np.float32)[:, None] * np.arange(length, dtype=np.float32)[None, :]
    return np.cos(angle).astype(np.float32), np.sin(angle).astype(np.float32)


def body(dp, tp, tokens, segment_ids, cotangent, gain1, bias1, gain2, bias2,
         qkv_weight, qkv_bias, dense_weight, dense_bias, fc_in_weight, fc_in_bias,
         fc_out_weight, fc_out_bias):
    assert tp == 4 and dp % 8 == 0
    x0, dy0 = tokens[0], cotangent[0]
    rows, width = x0.shape
    seq = rows * tp
    count = seq // BLK
    wq = qkv_weight.T
    heads = wq.shape[0] // (3 * HEAD_DIM)
    cosine, sine = rotary_tables(seq)
    place = jnp.stack([lax.axis_index("tensor"), lax.axis_index("dp")]).astype(i32)

    x1 = swap(x0, "tensor", tp, 1)
    x2 = swap(x0, "tensor", tp, 2)
    dy1 = swap(dy0, "tensor", tp, 1)
    dy2 = swap(dy0, "tensor", tp, 2)
    x3 = swap(x2, "tensor", tp, 1)
    dy3 = swap(dy2, "tensor", tp, 1)

    start, lo = call(
        segments_kernel, "segments", [segment_ids, segment_ids],
        [like((1, seq), i32), like((count,), i32)], smem=(1,), smem_out=(1,),
    )
    bq_column = qkv_bias.astype(f32)[:, None]
    pair = 2 * rows
    hidden = fc_in_weight.shape[1]

    def front(xa, xb, first):
        return call(
            partial(front_kernel, first=first), "front",
            [place, xa, xb, gain1, bias1, gain2, bias2, fc_in_weight, fc_in_bias, wq, bq_column,
             cosine, sine],
            [like((pair, width), bf16), like((pair, hidden), bf16), like((pair, hidden), bf16),
             like((heads, 3, HEAD_DIM, pair), bf16)],
            smem=(0,), limit=16, flops=2 * pair * width * (hidden + wq.shape[0]),
        )

    def ff_back(da, db, act, slope, xh, carry):
        inner = dense_weight.shape[0]
        outs = [like((pair, width), bf16), like((pair, width), bf16), like((inner, pair), bf16)]
        full = [like((width, hidden), f32), like((hidden, width), f32)]
        sums = like((8, width), f32)
        half = [like((width // 2, hidden), bf16)] * 2 + [like((hidden // 2, width), bf16)] * 2
        inputs = [place, da, db, act, slope, xh, gain2, fc_in_weight, fc_out_weight, dense_weight]
        scratch = []
        if carry is None:
            outs = outs + full + [sums]
        else:
            inputs = inputs + [bias2] + list(carry)
            outs = outs + half + [sums]
            scratch = [
                pltpu.VMEM((width, hidden), f32), pltpu.VMEM((hidden, width), f32),
                pltpu.VMEM((width, hidden), bf16),
            ]
        return call(
            partial(ff_back_kernel, last=carry is not None), "ff_back", inputs, outs, scratch,
            smem=(0,), limit=22, flops=2 * pair * width * (5 * hidden + inner),
        )

    xh_l, act_l, slope_l, qkv_l = front(x0, x1, 0)
    out_l, back_l, do_l, w1_part, w2_part, sums_l = ff_back(dy0, dy1, act_l, slope_l, xh_l, None)
    xh_r, act_r, slope_r, qkv_r = front(x2, x3, 2)
    out_r, back_r, do_r, k1, s1, k2, s2, sums = ff_back(
        dy2, dy3, act_r, slope_r, xh_r, (w1_part, w2_part, sums_l)
    )
    inner = heads * HEAD_DIM
    qkv, mixed, lse, keep0, keep2, send, dense_grad = call(
        attend_kernel, "attend",
        [place, lo, start, qkv_l, qkv_r, out_l, out_r, dy0, dy1, dy2, dy3, dense_weight],
        [like((heads, 3, HEAD_DIM, seq), bf16), like((inner, seq), bf16), like((heads, 1, seq), f32),
         like((rows, width), f32), like((rows, width), f32), like((pair, width), bf16),
         like((inner, width), bf16)],
        [pltpu.VMEM((heads, seq, HEAD_DIM), bf16)],
        smem=(0, 1), limit=12, flops=15_000_000_000,
    )
    got = swap(send, "tensor", tp, 1)
    far = swap(call(forward_kernel, "forward", [keep2, got], [like((rows, width), bf16)])[0],
               "tensor", tp, 2)
    result = call(
        result_kernel, "result", [x0, keep0, got, far, dense_bias, fc_out_bias],
        [like((rows, width), bf16)],
    )[0]

    vectors_rows = 16
    dqkv, keep_c, send_c = call(
        attend_back_kernel, "attend_back",
        [place, lo, start, qkv, mixed, do_l, do_r, lse, cosine, sine, xh_l, xh_r, wq, gain1, bias1,
         dense_grad, sums],
        [like((heads, 3, HEAD_DIM, seq), bf16)]
        + [like((width // 2 + vectors_rows, width), bf16)] * 2,
        [
            pltpu.VMEM((inner, seq), bf16),
            pltpu.VMEM((heads, seq, HEAD_DIM), bf16), pltpu.VMEM((heads, seq, HEAD_DIM), bf16),
            pltpu.VMEM((heads, HEAD_DIM, seq), f32), pltpu.VMEM((heads, HEAD_DIM, seq), f32),
            pltpu.VMEM((wq.shape[0] + inner, width), bf16),
        ],
        smem=(0, 1), limit=20, flops=22_000_000_000,
    )
    keep0b, keep2b, sendb = call(
        tokens_back_kernel, "tokens_back", [dqkv, back_l, back_r, wq, gain1],
        [like((rows, width), f32), like((rows, width), f32), like((pair, width), bf16)],
        limit=8, flops=2 * seq * width * wq.shape[0],
    )
    gotb = swap(sendb, "tensor", tp, 1)
    farb = swap(call(forward_kernel, "forward", [keep2b, gotb], [like((rows, width), bf16)])[0],
                "tensor", tp, 2)
    input_grad = call(
        tokens_grad_kernel, "tokens_grad", [x0, dy0, keep0b, gotb, farb],
        [like((rows, width), f32)],
    )[0]

    def all_sum(keep, send, tail=0):
        got = swap(send, "dp", dp, 1)
        total = reduce_pieces(place, keep, got, dp, tail)
        vectors = rest_sum(total[1], dp) if tail else None
        mine = spread_pieces(rest_sum(total[0].astype(f32), dp).astype(bf16) if dp > 8 else total[0], dp)
        return mine, swap(mine, "dp", dp, 1), vectors

    mine2, other2, _ = all_sum(k2, s2)
    mine1, other1, _ = all_sum(k1, s1)
    mine_c, other_c, vectors = all_sum(keep_c, send_c, vectors_rows)
    w2_grad = settle(place, mine2, other2, [like((hidden, width), f32)])[0]
    w1_grad = settle(place, mine1, other1, [like((width, hidden), f32)])[0]
    wq_grad, wd_grad = settle(
        place, mine_c, other_c, [like((wq.shape[0], width), f32), like((inner, width), f32)]
    )
    near = vectors + swap(vectors, "tensor", tp, 1)
    near = near + swap(near, "tensor", tp, 2)
    return (
        result[None], input_grad[None], near[0], near[1], near[2], near[3],
        wq_grad.T, vectors[6, : wq.shape[0]], wd_grad, vectors[4],
        w1_grad, vectors[5], w2_grad, vectors[4],
    )


def solution(mesh):
    split = P("dp", "tensor", None)
    columns, stacked, vector = P(None, "tensor"), P("tensor", None), P("tensor")
    whole = P()
    return jax.shard_map(
        partial(body, mesh.shape["dp"], mesh.shape["tensor"]),
        mesh=mesh,
        in_specs=(
            split, P("dp", None), split, whole, whole, whole, whole, columns, vector, stacked,
            whole, columns, vector, stacked, whole,
        ),
        out_specs=(
            split, split, whole, whole, whole, whole, columns, vector, stacked, whole, columns,
            vector, stacked, whole,
        ),
        check_vma=False,
    )
```

profile of v0, /device:TPU:0, one launch (start us, length us, event | category | flops | bytes accessed | tf_op | source)
XLA Modules:
  0.0 239.8 jit_solution(4456285016296034865)
XLA Ops:
  0.6 3.0 %collective-permute-start.1 = (bf16[512,768]{1,0:T(8,128)(2,1)}, bf16[512,768]{1,0:T(8,128)(2,1)S(1)}, u32[]{:S(2)}, u32[]{:S(2)}) collective-permute-start(bf16[512,768]{1,0:T(8,128)(2,1)} %bitcast.8), channel_id=1, source_target_pairs={{0,2},{1,3},{2,0},{3,1},{4,6},{5,7},{6,4},{7,5},{8,10},{9,11},{10,... | collective-permute-start | bytes 2359304 | tf_op jit(solution)/shard_map/ppermute | solution.py:405
  7.4 14.9 %collective-permute-done.1.x0_ref = bf16[512,768]{1,0:T(8,128)(2,1)S(1)} collective-permute-done((bf16[512,768]{1,0:T(8,128)(2,1)}, bf16[512,768]{1,0:T(8,128)(2,1)S(1)}, u32[]{:S(2)}, u32[]{:S(2)}) %collective-permute-start.1) | collective-permute-done | bytes 786464 | tf_op jit(solution)/shard_map/ppermute | solution.py:405
  22.3 16.0 %collective-permute-done.4.refs_1_.dy2_ref = bf16[512,768]{1,0:T(8,128)(2,1)S(1)} collective-permute-done((bf16[512,768]{1,0:T(8,128)(2,1)}, bf16[512,768]{1,0:T(8,128)(2,1)S(1)}, u32[]{:S(2)}, u32[]{:S(2)}) %collective-permute-start.4) | collective-permute-done | bytes 786464 | tf_op jit(solution)/shard_map/ppermute | solution.py:405
  47.0 4.4 %front.2 = (bf16[1024,768]{1,0:T(8,128)(2,1)S(1)}, bf16[1024,768]{1,0:T(8,128)(2,1)S(1)}, bf16[1024,768]{1,0:T(8,128)(2,1)S(1)}, bf16[3,3,64,1024]{3,2,1,0:T(8,128)(2,1)S(1)}) custom-call(s32[2]{0:T(128)S(1)} %pad_add_fusion.place_ref.refs_0_, bf16[512,768]{1,0:T(8,128)(2,1)S(1)} %bitcast.10, bf16[512,768]{1,0:T(8,128)(2,1)S(1)} %collective-permute-done.x1_ref, ...), custom_call_target="tpu_custom_call" | custom-call | flops 2113929216 | bytes 1000000 | tf_op jit(solution)/shard_map/front/pallas_call | solution.py:40
  51.5 7.4 %ff_back.2 = (bf16[1024,768]{1,0:T(8,128)(2,1)S(1)}, bf16[1024,768]{1,0:T(8,128)(2,1)S(1)}, bf16[192,1024]{1,0:T(8,128)(2,1)S(1)}, f32[768,768]{1,0:T(8,128)S(1)...) custom-call(s32[2]{0:T(128)S(1)} %pad_add_fusion.place_ref.refs_0_, bf16[512,768]{1,0:T(8,128)(2,1)S(1)} %bitcast.15, ...), custom_call_target="tpu_custom_call" | custom-call | flops 6341787648 | bytes 1000000 | tf_op jit(solution)/shard_map/ff_back/pallas_call | solution.py:40
  59.0 4.5 %front.3 = (bf16[1024,768]{1,0:T(8,128)(2,1)S(1)}, bf16[1024,768]{1,0:T(8,128)(2,1)S(1)}, bf16[1024,768]{1,0:T(8,128)(2,1)S(1)}, bf16[3,3,64,1024]{3,2,1,0:T(8,128)(2,1)S(1)}) custom-call(s32[2]{0:T(128)S(1)} %pad_add_fusion.place_ref.refs_0_, bf16[512,768]{1,0:T(8,128)(2,1)S(1)} %collective-permute-done.1.x0_ref, ...), custom_call_target="tpu_custom_call" | custom-call | flops 2113929216 | bytes 1000000 | tf_op jit(solution)/shard_map/front/pallas_call | solution.py:40
  63.6 8.9 %ff_back.3 = (bf16[1024,768]{1,0:T(8,128)(2,1)S(1)}, bf16[1024,768]{1,0:T(8,128)(2,1)S(1)}, bf16[192,1024]{1,0:T(8,128)(2,1)S(1)}, bf16[384,768]{1,0:T(8,128)(2,...) custom-call(s32[2]{0:T(128)S(1)} %pad_add_fusion.place_ref.refs_0_, ...), custom_call_target="tpu_custom_call" | custom-call | flops 6341787648 | bytes 1000000 | tf_op jit(solution)/shard_map/ff_back/pallas_call | solution.py:40
  74.5 15.2 %attend.1 = (bf16[3,3,64,2048]{3,2,1,0:T(8,128)(2,1)S(1)}, bf16[192,2048]{1,0:T(8,128)(2,1)S(1)}, f32[3,1,2048]{2,1,0:T(1,128)S(1)}, f32[512,768]{1,0:T(8,128)S(...) custom-call(s32[2]{0:T(128)S(1)} %pad_add_fusion.place_ref.refs_0_, ...), custom_call_target="tpu_custom_call" | custom-call | flops 15000000512 | bytes 1000000 | tf_op jit(solution)/shard_map/attend/pallas_call | solution.py:40
  89.7 19.3 %attend_back.1 = (bf16[3,3,64,2048]{3,2,1,0:T(8,128)(2,1)S(1)}, bf16[400,768]{1,0:T(8,128)(2,1)S(1)}, bf16[400,768]{1,0:T(8,128)(2,1)S(1)}) custom-call(s32[2]{0:T(128)S(1)} %pad_add_fusion.place_ref.refs_0_, s32[8]{0:T(128)S(1)} %get-tuple-element.67.lo_ref, s32[1,2048]{1,0:T(1,128)S(1)} %get-tuple-element.68.start_ref, ...), custom_call_target="tpu_custom_call" | custom-call | flops 22000001024 | bytes 1000000 | tf_op jit(solution)/shard_map/attend_back/pallas_call | solution.py:40
  109.7 2.7 %tokens_back.1 = (f32[512,768]{1,0:T(8,128)S(1)}, f32[512,768]{1,0:T(8,128)S(1)}, bf16[1024,768]{1,0:T(8,128)(2,1)S(1)}) custom-call(bf16[3,3,64,2048]{3,2,1,0:T(8,128)(2,1)S(1)} %get-tuple-element.92.dqkv_ref, bf16[1024,768]{1,0:T(8,128)(2,1)S(1)} %get-tuple-element.93.backl_ref, bf16[1024,768]{1,0:T(8,128)(2,1)S(1)} %get-tuple-element.94.backr_ref, ...), custom_call_target="tpu_custom_call" | custom-call | flops 1811939328 | bytes 1000000 | tf_op jit(solution)/shard_map/tokens_back/pallas_call | solution.py:40
  115.3 2.6 %collective-permute-start.22 = (bf16[96,768]{1,0:T(8,128)(2,1)S(1)}, bf16[96,768]{1,0:T(8,128)(2,1)S(1)}, u32[]{:S(2)}, u32[]{:S(2)}) collective-permute-start(bf16[96,768]{1,0:T(8,128)(2,1)S(1)} %get-tuple-element.112), channel_id=1, source_target_pairs={{0,16},{4,20},{8,24},{12,28},{16,0},{20,4},{24,8},{28,12},{1,17},{... | collective-permute-start | bytes 442376 | tf_op jit(solution)/shard_map/ppermute | solution.py:413
  117.9 7.0 %collective-permute-done.10.got_ref = bf16[400,768]{1,0:T(8,128)(2,1)S(1)} collective-permute-done((bf16[400,768]{1,0:T(8,128)(2,1)S(1)}, bf16[400,768]{1,0:T(8,128)(2,1)S(1)}, u32[]{:S(2)}, u32[]{:S(2)}) %collective-permute-start.10) | collective-permute-done | bytes 614432 | tf_op jit(solution)/shard_map/ppermute | solution.py:405
  133.7 2.9 %collective-permute-done.29.refs_1_ = bf16[96,768]{1,0:T(8,128)(2,1)S(1)} collective-permute-done((bf16[96,768]{1,0:T(8,128)(2,1)S(1)}, bf16[96,768]{1,0:T(8,128)(2,1)S(1)}, u32[]{:S(2)}, u32[]{:S(2)}) %collective-permute-start.29) | collective-permute-done | bytes 147488 | tf_op jit(solution)/shard_map/ppermute | solution.py:413
  140.2 8.9 %collective-permute-start.30 = (bf16[96,768]{1,0:T(8,128)(2,1)S(1)}, bf16[96,768]{1,0:T(8,128)(2,1)S(1)}, u32[]{:S(2)}, u32[]{:S(2)}) collective-permute-start(bf16[96,768]{1,0:T(8,128)(2,1)S(1)} %get-tuple-element.118), channel_id=1, source_target_pairs={{0,16},{4,20},{8,24},{12,28},{16,0},{20,4},{24,8},{28,12},{1,17},{... | collective-permute-start | bytes 442376 | tf_op jit(solution)/shard_map/ppermute | solution.py:413
  149.2 4.6 %collective-permute-start.31 = (bf16[96,768]{1,0:T(8,128)(2,1)S(1)}, bf16[96,768]{1,0:T(8,128)(2,1)S(1)}, u32[]{:S(2)}, u32[]{:S(2)}) collective-permute-start(bf16[96,768]{1,0:T(8,128)(2,1)S(1)} %get-tuple-element.119), channel_id=1, source_target_pairs={{0,24},{4,28},{8,0},{12,4},{16,8},{20,12},{24,16},{28,20},{1,25},{... | collective-permute-start | bytes 442376 | tf_op jit(solution)/shard_map/ppermute | solution.py:413
  154.0 2.6 %collective-permute-done.30.refs_2_ = bf16[96,768]{1,0:T(8,128)(2,1)S(1)} collective-permute-done((bf16[96,768]{1,0:T(8,128)(2,1)S(1)}, bf16[96,768]{1,0:T(8,128)(2,1)S(1)}, u32[]{:S(2)}, u32[]{:S(2)}) %collective-permute-start.30) | collective-permute-done | bytes 147488 | tf_op jit(solution)/shard_map/ppermute | solution.py:413
  159.3 9.0 %collective-permute-start.24 = (bf16[96,768]{1,0:T(8,128)(2,1)S(1)}, bf16[96,768]{1,0:T(8,128)(2,1)S(1)}, u32[]{:S(2)}, u32[]{:S(2)}) collective-permute-start(bf16[96,768]{1,0:T(8,128)(2,1)S(1)} %total.4), channel_id=1, source_target_pairs={{0,8},{4,12},{8,16},{12,20},{16,24},{20,28},{24,0},{28,4},{1,9},{5... | collective-permute-start | bytes 442376 | tf_op jit(solution)/shard_map/ppermute | solution.py:413
  169.9 5.8 %collective-permute-done.24 = bf16[96,768]{1,0:T(8,128)(2,1)S(1)} collective-permute-done((bf16[96,768]{1,0:T(8,128)(2,1)S(1)}, bf16[96,768]{1,0:T(8,128)(2,1)S(1)}, u32[]{:S(2)}, u32[]{:S(2)}) %collective-permute-start.24) | collective-permute-done | bytes 147488 | tf_op jit(solution)/shard_map/ppermute | solution.py:413
  175.7 6.4 %collective-permute-start.32 = (bf16[96,768]{1,0:T(8,128)(2,1)S(1)}, bf16[96,768]{1,0:T(8,128)(2,1)S(1)}, u32[]{:S(2)}, u32[]{:S(2)}) collective-permute-start(bf16[96,768]{1,0:T(8,128)(2,1)S(1)} %total.5), channel_id=1, source_target_pairs={{0,8},{4,12},{8,16},{12,20},{16,24},{20,28},{24,0},{28,4},{1,9},{5... | collective-permute-start | bytes 442376 | tf_op jit(solution)/shard_map/ppermute | solution.py:413
  182.1 2.5 %collective-permute-start.16 = (bf16[96,768]{1,0:T(8,128)(2,1)S(1)}, bf16[96,768]{1,0:T(8,128)(2,1)S(1)}, u32[]{:S(2)}, u32[]{:S(2)}) collective-permute-start(bf16[96,768]{1,0:T(8,128)(2,1)S(1)} %get-tuple-element.105), channel_id=1, source_target_pairs={{0,8},{4,12},{8,16},{12,20},{16,24},{20,28},{24,0},{28,4},{1,9},{5... | collective-permute-start | bytes 442376 | tf_op jit(solution)/shard_map/ppermute | solution.py:413
  184.7 6.5 %collective-permute-done.33 = bf16[96,768]{1,0:T(8,128)(2,1)S(1)} collective-permute-done((bf16[96,768]{1,0:T(8,128)(2,1)S(1)}, bf16[96,768]{1,0:T(8,128)(2,1)S(1)}, u32[]{:S(2)}, u32[]{:S(2)}) %collective-permute-start.33) | collective-permute-done | bytes 147488 | tf_op jit(solution)/shard_map/ppermute | solution.py:413
  195.4 5.9 %collective-permute-done.17 = bf16[96,768]{1,0:T(8,128)(2,1)S(1)} collective-permute-done((bf16[96,768]{1,0:T(8,128)(2,1)S(1)}, bf16[96,768]{1,0:T(8,128)(2,1)S(1)}, u32[]{:S(2)}, u32[]{:S(2)}) %collective-permute-start.17) | collective-permute-done | bytes 147488 | tf_op jit(solution)/shard_map/ppermute | solution.py:413
  206.8 15.0 %collective-permute-done.35.got_ref = bf16[384,768]{1,0:T(8,128)(2,1)S(1)} collective-permute-done((bf16[384,768]{1,0:T(8,128)(2,1)S(1)}, bf16[384,768]{1,0:T(8,128)(2,1)S(1)}, u32[]{:S(2)}, u32[]{:S(2)}) %collective-permute-start.35) | collective-permute-done | bytes 589856 | tf_op jit(solution)/shard_map/ppermute | solution.py:405
  226.1 7.2 %collective-permute-done.19.got_ref = bf16[384,768]{1,0:T(8,128)(2,1)S(1)} collective-permute-done((bf16[384,768]{1,0:T(8,128)(2,1)S(1)}, bf16[384,768]{1,0:T(8,128)(2,1)S(1)}, u32[]{:S(2)}, u32[]{:S(2)}) %collective-permute-start.19) | collective-permute-done | bytes 589856 | tf_op jit(solution)/shard_map/ppermute | solution.py:405
  (137 shorter events, 55.4 us)
Async XLA Ops:
  0.6 21.6 %collective-permute-start.1 = (bf16[512,768]{1,0:T(8,128)(2,1)}, bf16[512,768]{1,0:T(8,128)(2,1)S(1)}, u32[]{:S(2)}, u32[]{:S(2)}) collective-permute-start(bf16[512,768]{1,0:T(8,128)(2,1)} %bitcast.8), channel_id=1, source_target_pairs={{0,2},{1,3},{2,0},{3,1},{4,6},{5,7},{6,4},{7,5},{8,10},{9,11},{10,... | collective-permute-start | bytes 2359304 | tf_op jit(solution)/shard_map/ppermute | solution.py:405
  3.7 34.6 %collective-permute-start.4 = (bf16[512,768]{1,0:T(8,128)(2,1)}, bf16[512,768]{1,0:T(8,128)(2,1)S(1)}, u32[]{:S(2)}, u32[]{:S(2)}) collective-permute-start(bf16[512,768]{1,0:T(8,128)(2,1)} %bitcast.13), channel_id=1, source_target_pairs={{0,2},{1,3},{2,0},{3,1},{4,6},{5,7},{6,4},{7,5},{8,10},{9,11},{10,... | collective-permute-start | bytes 2359304 | tf_op jit(solution)/shard_map/ppermute | solution.py:405
  3.8 34.5 %collective-permute-start = (bf16[512,768]{1,0:T(8,128)(2,1)}, bf16[512,768]{1,0:T(8,128)(2,1)S(1)}, u32[]{:S(2)}, u32[]{:S(2)}) collective-permute-start(bf16[512,768]{1,0:T(8,128)(2,1)} %bitcast.9), channel_id=1, source_target_pairs={{0,1},{1,0},{2,3},{3,2},{4,5},{5,4},{6,7},{7,6},{8,9},{9,8},{10,11... | collective-permute-start | bytes 2359304 | tf_op jit(solution)/shard_map/ppermute | solution.py:405
  3.8 47.6 %collective-permute-start.3 = (bf16[512,768]{1,0:T(8,128)(2,1)}, bf16[512,768]{1,0:T(8,128)(2,1)S(1)}, u32[]{:S(2)}, u32[]{:S(2)}) collective-permute-start(bf16[512,768]{1,0:T(8,128)(2,1)} %bitcast.14), channel_id=1, source_target_pairs={{0,1},{1,0},{2,3},{3,2},{4,5},{5,4},{6,7},{7,6},{8,9},{9,8},{10,11... | collective-permute-start | bytes 2359304 | tf_op jit(solution)/shard_map/ppermute | solution.py:405
  22.3 36.7 %collective-permute-start.2 = (bf16[512,768]{1,0:T(8,128)(2,1)S(1)}, bf16[512,768]{1,0:T(8,128)(2,1)S(1)}, u32[]{:S(2)}, u32[]{:S(2)}) collective-permute-start(bf16[512,768]{1,0:T(8,128)(2,1)S(1)} %collective-permute-done.1.x0_ref), channel_id=1, source_target_pairs={{0,1},{1,0},{2,3},{3,2},{4,5},{5,4},{6,7},{7,6},{8,9},{9,8},{10,11... | collective-permute-start | bytes 2359304 | tf_op jit(solution)/shard_map/ppermute | solution.py:405
  38.3 25.3 %collective-permute-start.5 = (bf16[512,768]{1,0:T(8,128)(2,1)S(1)}, bf16[512,768]{1,0:T(8,128)(2,1)S(1)}, u32[]{:S(2)}, u32[]{:S(2)}) collective-permute-start(bf16[512,768]{1,0:T(8,128)(2,1)S(1)} %collective-permute-done.4.refs_1_.dy2_ref), channel_id=1, source_target_pairs={{0,1},{1,0},{2,3},{3,2},{4,5},{5,4},{6,7},{7,6},{8,9},{9,8},{10,11... | collective-permute-start | bytes 2359304 | tf_op jit(solution)/shard_map/ppermute | solution.py:405
  72.5 40.5 %collective-permute-start.20 = (bf16[384,768]{1,0:T(8,128)(2,1)S(1)}, bf16[384,768]{1,0:T(8,128)(2,1)S(1)}, u32[]{:S(2)}, u32[]{:S(2)}) collective-permute-start(bf16[384,768]{1,0:T(8,128)(2,1)S(1)} %get-tuple-element.109), channel_id=1, source_target_pairs={{0,4},{4,0},{8,12},{12,8},{16,20},{20,16},{24,28},{28,24},{1,5},{5... | collective-permute-start | bytes 1769480 | tf_op jit(solution)/shard_map/ppermute | solution.py:405
  74.2 41.1 %collective-permute-start.28 = (bf16[384,768]{1,0:T(8,128)(2,1)S(1)}, bf16[384,768]{1,0:T(8,128)(2,1)S(1)}, u32[]{:S(2)}, u32[]{:S(2)}) collective-permute-start(bf16[384,768]{1,0:T(8,128)(2,1)S(1)} %get-tuple-element.115), channel_id=1, source_target_pairs={{0,4},{4,0},{8,12},{12,8},{16,20},{20,16},{24,28},{28,24},{1,5},{5... | collective-permute-start | bytes 1769480 | tf_op jit(solution)/shard_map/ppermute | solution.py:405
  109.0 15.9 %collective-permute-start.10 = (bf16[400,768]{1,0:T(8,128)(2,1)S(1)}, bf16[400,768]{1,0:T(8,128)(2,1)S(1)}, u32[]{:S(2)}, u32[]{:S(2)}) collective-permute-start(bf16[400,768]{1,0:T(8,128)(2,1)S(1)} %get-tuple-element.99), channel_id=1, source_target_pairs={{0,4},{4,0},{8,12},{12,8},{16,20},{20,16},{24,28},{28,24},{1,5},{5... | collective-permute-start | bytes 1843208 | tf_op jit(solution)/shard_map/ppermute | solution.py:405
  109.7 83.3 %collective-permute-start.6 = (bf16[1024,768]{1,0:T(8,128)(2,1)S(1)}, bf16[1024,768]{1,0:T(8,128)(2,1)S(1)}, u32[]{:S(2)}, u32[]{:S(2)}) collective-permute-start(bf16[1024,768]{1,0:T(8,128)(2,1)S(1)} %get-tuple-element.83), channel_id=1, source_target_pairs={{0,1},{1,0},{2,3},{3,2},{4,5},{5,4},{6,7},{7,6},{8,9},{9,8},{10,11... | collective-permute-start | bytes 4718600 | tf_op jit(solution)/shard_map/ppermute | solution.py:405
  112.4 82.2 %collective-permute-start.8 = (bf16[1024,768]{1,0:T(8,128)(2,1)S(1)}, bf16[1024,768]{1,0:T(8,128)(2,1)S(1)}, u32[]{:S(2)}, u32[]{:S(2)}) collective-permute-start(bf16[1024,768]{1,0:T(8,128)(2,1)S(1)} %get-tuple-element.96), channel_id=1, source_target_pairs={{0,1},{1,0},{2,3},{3,2},{4,5},{5,4},{6,7},{7,6},{8,9},{9,8},{10,11... | collective-permute-start | bytes 4718600 | tf_op jit(solution)/shard_map/ppermute | solution.py:405
  113.7 14.2 %collective-permute-start.21 = (bf16[96,768]{1,0:T(8,128)(2,1)S(1)}, bf16[96,768]{1,0:T(8,128)(2,1)S(1)}, u32[]{:S(2)}, u32[]{:S(2)}) collective-permute-start(bf16[96,768]{1,0:T(8,128)(2,1)S(1)} %get-tuple-element.111), channel_id=1, source_target_pairs={{0,8},{4,12},{8,16},{12,20},{16,24},{20,28},{24,0},{28,4},{1,9},{5... | collective-permute-start | bytes 442376 | tf_op jit(solution)/shard_map/ppermute | solution.py:413
  131.4 17.8 %collective-permute-start.12 = (bf16[112,768]{1,0:T(8,128)(2,1)S(1)}, bf16[112,768]{1,0:T(8,128)(2,1)S(1)}, u32[]{:S(2)}, u32[]{:S(2)}) collective-permute-start(bf16[112,768]{1,0:T(8,128)(2,1)S(1)} %get-tuple-element.102), channel_id=1, source_target_pairs={{0,16},{4,20},{8,24},{12,28},{16,0},{20,4},{24,8},{28,12},{1,17},{... | collective-permute-start | bytes 516104 | tf_op jit(solution)/shard_map/ppermute | solution.py:413
  136.6 17.3 %collective-permute-start.13 = (bf16[112,768]{1,0:T(8,128)(2,1)S(1)}, bf16[112,768]{1,0:T(8,128)(2,1)S(1)}, u32[]{:S(2)}, u32[]{:S(2)}) collective-permute-start(bf16[112,768]{1,0:T(8,128)(2,1)S(1)} %get-tuple-element.103), channel_id=1, source_target_pairs={{0,24},{4,28},{8,0},{12,4},{16,8},{20,12},{24,16},{28,20},{1,25},{... | collective-permute-start | bytes 516104 | tf_op jit(solution)/shard_map/ppermute | solution.py:413
  140.2 16.4 %collective-permute-start.30 = (bf16[96,768]{1,0:T(8,128)(2,1)S(1)}, bf16[96,768]{1,0:T(8,128)(2,1)S(1)}, u32[]{:S(2)}, u32[]{:S(2)}) collective-permute-start(bf16[96,768]{1,0:T(8,128)(2,1)S(1)} %get-tuple-element.118), channel_id=1, source_target_pairs={{0,16},{4,20},{8,24},{12,28},{16,0},{20,4},{24,8},{28,12},{1,17},{... | collective-permute-start | bytes 442376 | tf_op jit(solution)/shard_map/ppermute | solution.py:413
  153.9 14.5 %collective-permute-start.26 = (bf16[96,768]{1,0:T(8,128)(2,1)S(1)}, bf16[96,768]{1,0:T(8,128)(2,1)S(1)}, u32[]{:S(2)}, u32[]{:S(2)}) collective-permute-start(bf16[96,768]{1,0:T(8,128)(2,1)S(1)} %total.4), channel_id=1, source_target_pairs={{0,24},{4,28},{8,0},{12,4},{16,8},{20,12},{24,16},{28,20},{1,25},{... | collective-permute-start | bytes 442376 | tf_op jit(solution)/shard_map/ppermute | solution.py:413
  159.3 16.4 %collective-permute-start.24 = (bf16[96,768]{1,0:T(8,128)(2,1)S(1)}, bf16[96,768]{1,0:T(8,128)(2,1)S(1)}, u32[]{:S(2)}, u32[]{:S(2)}) collective-permute-start(bf16[96,768]{1,0:T(8,128)(2,1)S(1)} %total.4), channel_id=1, source_target_pairs={{0,8},{4,12},{8,16},{12,20},{16,24},{20,28},{24,0},{28,4},{1,9},{5... | collective-permute-start | bytes 442376 | tf_op jit(solution)/shard_map/ppermute | solution.py:413
  169.1 22.1 %collective-permute-start.33 = (bf16[96,768]{1,0:T(8,128)(2,1)S(1)}, bf16[96,768]{1,0:T(8,128)(2,1)S(1)}, u32[]{:S(2)}, u32[]{:S(2)}) collective-permute-start(bf16[96,768]{1,0:T(8,128)(2,1)S(1)} %total.5), channel_id=1, source_target_pairs={{0,16},{4,20},{8,24},{12,28},{16,0},{20,4},{24,8},{28,12},{1,17},{... | collective-permute-start | bytes 442376 | tf_op jit(solution)/shard_map/ppermute | solution.py:413
  175.7 15.5 %collective-permute-start.32 = (bf16[96,768]{1,0:T(8,128)(2,1)S(1)}, bf16[96,768]{1,0:T(8,128)(2,1)S(1)}, u32[]{:S(2)}, u32[]{:S(2)}) collective-permute-start(bf16[96,768]{1,0:T(8,128)(2,1)S(1)} %total.5), channel_id=1, source_target_pairs={{0,8},{4,12},{8,16},{12,20},{16,24},{20,28},{24,0},{28,4},{1,9},{5... | collective-permute-start | bytes 442376 | tf_op jit(solution)/shard_map/ppermute | solution.py:413
  193.0 31.0 %collective-permute-start.27 = (bf16[384,768]{1,0:T(8,128)(2,1)S(1)}, bf16[384,768]{1,0:T(8,128)(2,1)S(1)}, u32[]{:S(2)}, u32[]{:S(2)}) collective-permute-start(bf16[384,768]{1,0:T(8,128)(2,1)S(1)} %pad_maximum_fusion.mine_ref), channel_id=1, source_target_pairs={{0,4},{4,0},{8,12},{12,8},{16,20},{20,16},{24,28},{28,24},{1,5},{5... | collective-permute-start | bytes 1769480 | tf_op jit(solution)/shard_map/ppermute | solution.py:405
  194.7 43.2 %collective-permute-start.7 = (bf16[512,768]{1,0:T(8,128)(2,1)S(1)}, bf16[512,768]{1,0:T(8,128)(2,1)S(1)}, u32[]{:S(2)}, u32[]{:S(2)}) collective-permute-start(bf16[512,768]{1,0:T(8,128)(2,1)S(1)} %forward.2), channel_id=1, source_target_pairs={{0,2},{1,3},{2,0},{3,1},{4,6},{5,7},{6,4},{7,5},{8,10},{9,11},{10,... | collective-permute-start | bytes 2359304 | tf_op jit(solution)/shard_map/ppermute | solution.py:405
  201.2 34.3 %collective-permute-start.9 = (bf16[512,768]{1,0:T(8,128)(2,1)S(1)}, bf16[512,768]{1,0:T(8,128)(2,1)S(1)}, u32[]{:S(2)}, u32[]{:S(2)}) collective-permute-start(bf16[512,768]{1,0:T(8,128)(2,1)S(1)} %forward.3), channel_id=1, source_target_pairs={{0,2},{1,3},{2,0},{3,1},{4,6},{5,7},{6,4},{7,5},{8,10},{9,11},{10,... | collective-permute-start | bytes 2359304 | tf_op jit(solution)/shard_map/ppermute | solution.py:405
  202.8 19.1 %collective-permute-start.35 = (bf16[384,768]{1,0:T(8,128)(2,1)S(1)}, bf16[384,768]{1,0:T(8,128)(2,1)S(1)}, u32[]{:S(2)}, u32[]{:S(2)}) collective-permute-start(bf16[384,768]{1,0:T(8,128)(2,1)S(1)} %pad_maximum_fusion.1.mine_ref), channel_id=1, source_target_pairs={{0,4},{4,0},{8,12},{12,8},{16,20},{20,16},{24,28},{28,24},{1,5},{5... | collective-permute-start | bytes 1769480 | tf_op jit(solution)/shard_map/ppermute | solution.py:405
  204.3 29.0 %collective-permute-start.19 = (bf16[384,768]{1,0:T(8,128)(2,1)S(1)}, bf16[384,768]{1,0:T(8,128)(2,1)S(1)}, u32[]{:S(2)}, u32[]{:S(2)}) collective-permute-start(bf16[384,768]{1,0:T(8,128)(2,1)S(1)} %constant_dynamic-update-slice_fusion.mine_ref), channel_id=1, source_target_pairs={{0,4},{4,0},{8,12},{12,8},{16,20},{20,16},{24,28},{28,24},{1,5},{5... | collective-permute-start | bytes 1769480 | tf_op jit(solution)/shard_map/ppermute | solution.py:405
  (39 other events, 254.4 us)
where the time goes:
time: 239 us; the launch traced here: 240 us
  waiting for transfers between devices  90.3 us (38%)
  Pallas kernels  76.7 us (32%)
  starting transfers between devices  58.8 us (25%)
  local copies, waits for them, and re-layouts  12.7 us (5%)
    pallas_call x21, Pallas kernels, call(): pl.pallas_call(kernel, out_shape=tuple(outs), in_specs=[SMEM if i in smem...  76.7 us
    ppermute x18, waiting for transfers between devices, swap(): return lax.ppermute(value, axis, [(i, i ^ distance) for i in range(size)])  60.2 us
    ppermute x18, starting transfers between devices, shifted(): return lax.ppermute(value, 'dp', pairs)  44.5 us
    ppermute x18, waiting for transfers between devices, shifted(): return lax.ppermute(value, 'dp', pairs)  30.1 us
    ppermute x18, starting transfers between devices, swap(): return lax.ppermute(value, axis, [(i, i ^ distance) for i in range(size)])  14.3 us
    unnamed x58, local copies, waits for them, and re-layouts  10.1 us
  transfers between devices with their start and end apart: 36, of which 13 were waited for; matrix products, arithmetic and copies ran while one was open for 1% of the time, Pallas kernels for 28%

commit v1 on v0

v1 whole, which is shorter than its diff:
```python
from functools import partial

import jax
import jax.numpy as jnp
import numpy as np
from jax import lax
from jax.experimental import pallas as pl
from jax.experimental.pallas import tpu as pltpu
from jax.sharding import PartitionSpec as P

HEAD_DIM = 64
ROT = 16
SEGS = 8
BLK = 256
NEG = -1e30
LOG2E = 1.4426950408889634
f32, bf16, i32 = jnp.float32, jnp.bfloat16, jnp.int32
VMEM = pl.BlockSpec(memory_space=pltpu.VMEM)
SMEM = pl.BlockSpec(memory_space=pltpu.SMEM)
MIB = 1 << 20
UNIT = 500_000_000
ORDER_A, ORDER_B = (0, 1, 2), (1, 0, 2)


def dot(a, b):
    return jnp.dot(a, b, preferred_element_type=f32)


def dot_nt(a, b):
    return lax.dot_general(a, b, (((1,), (1,)), ((), ())), preferred_element_type=f32)


def dot_tn(a, b):
    return lax.dot_general(a, b, (((0,), (0,)), ((), ())), preferred_element_type=f32)


def like(shape, dtype):
    return jax.ShapeDtypeStruct(shape, dtype)


def call(kernel, name, inputs, outs, scratch=(), limit=8, smem=(), smem_out=(), flops=1000):
    return pl.pallas_call(
        kernel,
        out_shape=tuple(outs),
        in_specs=[SMEM if i in smem else VMEM for i in range(len(inputs))],
        out_specs=tuple(SMEM if i in smem_out else VMEM for i in range(len(outs))),
        scratch_shapes=list(scratch),
        compiler_params=pltpu.CompilerParams(vmem_limit_bytes=limit * MIB),
        cost_estimate=pl.CostEstimate(flops=flops, bytes_accessed=1000, transcendentals=0),
        name=name,
    )(*inputs)


def after(token, *values):
    return lax.optimization_barrier((token, *values))[1:]


def row_of(ref):
    return ref[...].astype(f32).reshape(1, -1)


def column_of(row):
    return jnp.broadcast_to(row, (128, row.shape[1])).T[:, 0:1]


def pair_rows(rows):
    rows = jnp.concatenate(rows, axis=0)
    high = rows.astype(bf16)
    return jnp.concatenate([high, (rows - high.astype(f32)).astype(bf16)], axis=0)


def segments_kernel(ids_ref, first_ref, start_ref, lo_ref):
    ids = ids_ref[...]
    start = jnp.zeros_like(ids)
    begins = []
    for s in range(SEGS):
        begin = jnp.sum(jnp.where(ids < s, 1.0, 0.0)).astype(i32)
        begins.append(begin)
        start = jnp.where(ids == s, begin, start)
    start_ref[...] = start
    for i in range(lo_ref.shape[0]):
        seg = first_ref[0, i * BLK]
        lo = begins[0]
        for s in range(1, SEGS):
            lo = jnp.where(seg == s, begins[s], lo)
        lo_ref[i] = lax.div(lo, BLK)


def front_kernel(place_ref, *refs, first, pieces):
    x_refs, refs = refs[:pieces], refs[pieces:]
    g1_ref, b1_ref, g2_ref, b2_ref, w1_ref, c1_ref, wq_ref, bq_ref, cos_ref, sin_ref = refs[:10]
    xh_ref, act_ref, slope_ref, qkv_ref = refs[10:]
    heads = qkv_ref.shape[0]
    half = ROT // 2
    rows = x_refs[0].shape[0]
    g1, b1, g2, b2, c1 = [row_of(r) for r in (g1_ref, b1_ref, g2_ref, b2_ref, c1_ref)]
    for piece, x_ref in enumerate(x_refs):
        out = slice(piece * rows, (piece + 1) * rows)
        at = (place_ref[0] ^ (first + piece)) * rows
        here = pl.ds(pl.multiple_of(at, 128), rows)
        x = x_ref[...].astype(f32)
        c = x - jnp.mean(x, axis=1, keepdims=True)
        xh = c * lax.rsqrt(jnp.mean(c * c, axis=1, keepdims=True) + 1e-05)
        xh_ref[out, :] = xh.astype(bf16)
        h1 = (xh * g1 + b1).astype(bf16)
        h2 = (xh * g2 + b2).astype(bf16)
        pre = dot(h2, w1_ref[...]) + c1
        qkv = dot_nt(wq_ref[...], h1) + bq_ref[...]
        cosine, sine = cos_ref[:, here], sin_ref[:, here]
        for h in range(heads):
            for part in range(3):
                at = (3 * h + part) * HEAD_DIM
                v = qkv[at : at + HEAD_DIM]
                if part < 2:
                    one, two = v[:half], v[half:ROT]
                    v = jnp.concatenate(
                        [one * cosine - two * sine, two * cosine + one * sine, v[ROT:]], axis=0
                    )
                if part == 0:
                    v = v * HEAD_DIM ** (-0.5)
                qkv_ref[h, part, :, out] = v.astype(bf16)
        cdf = 0.5 + 0.5 * lax.erf(pre * 0.5**0.5)
        pdf = jnp.exp(pre * pre * -0.5) * (2.0 * np.pi) ** -0.5
        act_ref[out, :] = (pre * cdf).astype(bf16)
        slope_ref[out, :] = (cdf + pre * pdf).astype(bf16)


def halves(payload_ref, keep_ref, send_ref, side):
    rows = keep_ref.shape[0]
    keep_ref[...] = payload_ref[pl.ds(pl.multiple_of(side * rows, 16), rows), :]
    send_ref[...] = payload_ref[pl.ds(pl.multiple_of((1 - side) * rows, 16), rows), :]


def bit_of(place_ref, bit):
    return lax.rem(lax.div(place_ref[1], 1 << bit), 2)


def ff_back_kernel(place_ref, *refs, pieces, carried, last):
    dy_refs, refs = refs[:pieces], refs[pieces:]
    act_ref, slope_ref, xh_ref, g2_ref, b2_ref, w1_ref, w2_ref, wd_ref = refs[:8]
    refs = refs[8:]
    if carried:
        w1_in, w2_in, sums_in = refs[:3]
        refs = refs[3:]
    if last:
        out_ref, back_ref, do_ref, k1_ref, s1_ref, k2_ref, s2_ref, sums_ref = refs[:8]
        w1g_ref, w2g_ref, pay_ref = refs[8:]
    else:
        out_ref, back_ref, do_ref, w1g_ref, w2g_ref, sums_ref = refs
    rows = dy_refs[0].shape[0]
    g2 = row_of(g2_ref)
    sums = [sums_in[i : i + 1, :] for i in range(2)] if carried else [0.0, 0.0]
    for piece, dy_ref in enumerate(dy_refs):
        r = slice(piece * rows, (piece + 1) * rows)
        dy = dy_ref[...]
        act = act_ref[r, :]
        du = (dot_nt(dy, w2_ref[...]) * slope_ref[r, :].astype(f32)).astype(bf16)
        w2_part = dot_tn(act, dy)
        w1_part = dot_tn(xh_ref[r, :], du)
        if piece == 0:
            w2g_ref[...] = w2_in[...] + w2_part if carried else w2_part
            w1g_ref[...] = w1_in[...] + w1_part if carried else w1_part
        else:
            w2g_ref[...] += w2_part
            w1g_ref[...] += w1_part
        out_ref[r, :] = dot(act, w2_ref[...]).astype(bf16)
        back_ref[r, :] = (dot_nt(du, w1_ref[...]) * g2).astype(bf16)
        do_ref[:, r] = dot_nt(wd_ref[...], dy).astype(bf16)
        sums[0] = sums[0] + jnp.sum(du.astype(f32), axis=0, keepdims=True)
        sums[1] = sums[1] + jnp.sum(dy.astype(f32), axis=0, keepdims=True)
    sums_ref[0:1, :] = sums[0]
    sums_ref[1:2, :] = sums[1]
    if last:
        pay_ref[...] = w2g_ref[...].astype(bf16)
        halves(pay_ref, k2_ref, s2_ref, bit_of(place_ref, ORDER_A[0]))
        du_sum = jnp.broadcast_to(sums[0], (8, sums[0].shape[1]))
        high = du_sum.astype(bf16)
        low = (du_sum - high.astype(f32)).astype(bf16)
        sums_ref[3:4, :] = (dot_nt(high, w1_ref[...]) + dot_nt(low, w1_ref[...]))[0:1]
        raw = w1g_ref[...]
        gain = jnp.sum(raw * w1_ref[...].astype(f32), axis=1, keepdims=True)
        sums_ref[2:3, :] = jnp.broadcast_to(gain, (gain.shape[0], 128)).T[0:1, :]
        pay_ref[...] = (raw * column_of(g2) + column_of(row_of(b2_ref)) * sums[0]).astype(bf16)
        halves(pay_ref, k1_ref, s1_ref, bit_of(place_ref, ORDER_B[0]))


def blocks(place_ref, count, per):
    def phys(j):
        return pl.ds(
            pl.multiple_of(((lax.div(j, per) ^ place_ref[0]) * per + lax.rem(j, per)) * BLK, BLK),
            BLK,
        )

    return phys


def spans(refs, axis):
    at = 0
    for ref in refs:
        size = ref.shape[axis]
        yield slice(at, at + size), ref
        at += size


def attend_kernel(
    place_ref, lo_ref, start_ref, part0_ref, part1_ref, part2_ref,
    qkv_ref, o_ref, lse_ref, kn_ref,
):
    heads, seq = qkv_ref.shape[0], qkv_ref.shape[3]
    count = seq // BLK
    phys = blocks(place_ref, count, count // 4)
    for at, ref in spans((part0_ref, part1_ref, part2_ref), 3):
        qkv_ref[:, :, :, at] = ref[...]
    for h in range(heads):
        for b in range(count):
            r = slice(b * BLK, (b + 1) * BLK)
            kn_ref[h, r, :] = qkv_ref[h, 1, :, r].T
    ik = lax.broadcasted_iota(i32, (BLK, BLK), 0)
    iq = lax.broadcasted_iota(i32, (BLK, BLK), 1)

    @pl.loop(0, count)
    def _(i):
        qs = phys(i)
        start = start_ref[0:1, pl.ds(pl.multiple_of(i * BLK, BLK), BLK)]

        def step(ks, mask, carry):
            scores = [
                jnp.where(mask, dot(kn_ref[h, ks, :], qkv_ref[h, 0, :, qs]), NEG)
                for h in range(heads)
            ]
            out = []
            for h in range(heads):
                top = jnp.max(scores[h], axis=0, keepdims=True)
                if carry is not None:
                    top = jnp.maximum(top, carry[h][0])
                expo = jnp.exp2(scores[h] * LOG2E - top * LOG2E)
                total = jnp.sum(expo, axis=0, keepdims=True)
                mixed = dot(qkv_ref[h, 2, :, ks], expo.astype(bf16))
                if carry is not None:
                    fade = jnp.exp2((carry[h][0] - top) * LOG2E)
                    total = total + carry[h][1] * fade
                    mixed = mixed + carry[h][2] * fade
                out.append((top, total, mixed))
            return tuple(out)

        carry = step(qs, (ik <= iq) & (ik >= start - i * BLK), None)
        carry = lax.fori_loop(
            lo_ref[i], i, lambda j, c: step(phys(j), ik >= start - j * BLK, c), carry
        )
        for h in range(heads):
            top, total, mixed = carry[h]
            at = slice(h * HEAD_DIM, (h + 1) * HEAD_DIM)
            o_ref[at, qs] = (mixed * (1.0 / total)).astype(bf16)
            lse_ref[h, 0:1, qs] = top * LOG2E + jnp.log2(total)


def chunk(refs, k, rows):
    for at, ref in spans(refs, 0):
        if at.start <= k * rows < at.stop:
            return ref[k * rows - at.start : (k + 1) * rows - at.start, :]


def deal(k, total, keep0_ref, keep2_ref, send_ref):
    rows = keep0_ref.shape[0]
    if k == 0:
        keep0_ref[...] = total
    elif k == 2:
        keep2_ref[...] = total
    else:
        send_ref[(k // 2) * rows : (k // 2 + 1) * rows, :] = total.astype(bf16)


def attend_end_kernel(
    o_ref, dy0_ref, dy1_ref, dy2_ref, dy3_ref, wd_ref, out0_ref, out1_ref, out2_ref,
    keep0_ref, keep2_ref, send_ref, wdg_ref,
):
    rows = keep0_ref.shape[0]
    wdg = None
    for k, dy_ref in enumerate((dy0_ref, dy1_ref, dy2_ref, dy3_ref)):
        o = o_ref[:, k * rows : (k + 1) * rows]
        out = chunk((out0_ref, out1_ref, out2_ref), k, rows).astype(f32)
        deal(k, out + dot_tn(o, wd_ref[...]), keep0_ref, keep2_ref, send_ref)
        part = dot(o, dy_ref[...])
        wdg = part if k == 0 else wdg + part
    wdg_ref[...] = wdg.astype(bf16)


def attend_back_kernel(
    place_ref, lo_ref, start_ref, qkv_ref, o_ref, do0_ref, do1_ref, do2_ref, lse_ref, cos_ref,
    sin_ref, dqkv_ref, do_ref, kn_ref, vn_ref, dk_ref, dv_ref,
):
    heads, seq = qkv_ref.shape[0], qkv_ref.shape[3]
    count = seq // BLK
    phys = blocks(place_ref, count, count // 4)
    half = ROT // 2
    for at, ref in spans((do0_ref, do1_ref, do2_ref), 1):
        do_ref[:, at] = ref[...]
    for h in range(heads):
        for b in range(count):
            r = slice(b * BLK, (b + 1) * BLK)
            kn_ref[h, r, :] = qkv_ref[h, 1, :, r].T
            vn_ref[h, r, :] = qkv_ref[h, 2, :, r].T
    dk_ref[...] = jnp.zeros_like(dk_ref)
    dv_ref[...] = jnp.zeros_like(dv_ref)
    ik = lax.broadcasted_iota(i32, (BLK, BLK), 0)
    iq = lax.broadcasted_iota(i32, (BLK, BLK), 1)

    def unrotate(grad, cosine, sine):
        one, two = grad[:half], grad[half:ROT]
        return jnp.concatenate(
            [one * cosine + two * sine, two * cosine - one * sine, grad[ROT:]], axis=0
        )

    @pl.loop(0, count)
    def _(i):
        qs = phys(i)
        here = pl.ds(pl.multiple_of(i * BLK, BLK), BLK)
        start = start_ref[0:1, here]
        dos = [do_ref[h * HEAD_DIM : (h + 1) * HEAD_DIM, qs] for h in range(heads)]
        delta = [
            jnp.sum(
                dos[h].astype(f32) * o_ref[h * HEAD_DIM : (h + 1) * HEAD_DIM, qs].astype(f32),
                axis=0, keepdims=True,
            )
            for h in range(heads)
        ]
        lse = [lse_ref[h, 0:1, qs] for h in range(heads)]

        def step(ks, mask, carry):
            scores = [
                jnp.where(mask, dot(kn_ref[h, ks, :], qkv_ref[h, 0, :, qs]), NEG)
                for h in range(heads)
            ]
            dprobs = [dot(vn_ref[h, ks, :], dos[h]) for h in range(heads)]
            probs = [jnp.exp2(scores[h] * LOG2E - lse[h]) for h in range(heads)]
            dscores = [(probs[h] * (dprobs[h] - delta[h])).astype(bf16) for h in range(heads)]
            out = []
            for h in range(heads):
                dv_ref[h, :, ks] += dot_nt(dos[h], probs[h].astype(bf16))
                dk_ref[h, :, ks] += dot_nt(qkv_ref[h, 0, :, qs], dscores[h])
                dq = dot(qkv_ref[h, 1, :, ks], dscores[h])
                out.append(dq if carry is None else carry[h] + dq)
            return tuple(out)

        carry = step(qs, (ik <= iq) & (ik >= start - i * BLK), None)
        carry = lax.fori_loop(
            lo_ref[i], i, lambda j, c: step(phys(j), ik >= start - j * BLK, c), carry
        )
        for h in range(heads):
            dq = unrotate(carry[h] * HEAD_DIM ** (-0.5), cos_ref[:, here], sin_ref[:, here])
            dqkv_ref[h, 0, :, qs] = dq.astype(bf16)

    @pl.loop(0, count)
    def _(i):
        qs = phys(i)
        here = pl.ds(pl.multiple_of(i * BLK, BLK), BLK)
        for h in range(heads):
            dk = unrotate(dk_ref[h, :, qs], cos_ref[:, here], sin_ref[:, here])
            dqkv_ref[h, 1, :, qs] = dk.astype(bf16)
            dqkv_ref[h, 2, :, qs] = dv_ref[h, :, qs].astype(bf16)


def qkv_end_kernel(
    place_ref, dqkv_ref, xh0_ref, xh1_ref, xh2_ref, wq_ref, g1_ref, b1_ref, wdg_ref, sums_ref,
    keep_ref, send_ref, pay_ref,
):
    heads, seq = dqkv_ref.shape[0], dqkv_ref.shape[3]
    g1, b1 = row_of(g1_ref), row_of(b1_ref)
    cols = 3 * HEAD_DIM
    gain, bias, bq = 0.0, 0.0, []
    for h in range(heads):
        grad = dqkv_ref[h].reshape(cols, seq)
        raw = None
        for at, ref in spans((xh0_ref, xh1_ref, xh2_ref), 0):
            part = dot(grad[:, at], ref[...])
            raw = part if raw is None else raw + part
        total = jnp.sum(grad.astype(f32), axis=1, keepdims=True)
        bq.append(jnp.broadcast_to(total, (cols, 128)).T[0:1, :])
        pay_ref[h * cols : (h + 1) * cols, :] = (raw * g1 + total * b1).astype(bf16)
        weight = wq_ref[h * cols : (h + 1) * cols, :].astype(f32)
        gain = gain + jnp.sum(weight * raw, axis=0, keepdims=True)
        bias = bias + jnp.sum(weight * total, axis=0, keepdims=True)
    pay_ref[heads * cols :, :] = wdg_ref[...]
    width = pay_ref.shape[1]
    zeros = jnp.zeros((1, width - heads * cols), f32)
    vectors = pair_rows(
        [
            gain, bias, sums_ref[2:3, :], sums_ref[3:4, :], sums_ref[1:2, :], sums_ref[0:1, :],
            jnp.concatenate(bq + [zeros], axis=1), jnp.zeros((1, width), f32),
        ]
    )
    side = bit_of(place_ref, ORDER_A[0])
    rows = pay_ref.shape[0] // 2
    halves(pay_ref, keep_ref.at[0:rows], send_ref.at[0:rows], side)
    keep_ref[rows:, :] = vectors
    send_ref[rows:, :] = vectors


def tokens_back_kernel(
    dqkv_ref, back0_ref, back1_ref, back2_ref, wq_ref, g1_ref, keep0_ref, keep2_ref, send_ref
):
    rows = keep0_ref.shape[0]
    g1 = row_of(g1_ref)
    cols = wq_ref.shape[0]
    for k in range(4):
        grad = dqkv_ref[:, :, :, k * rows : (k + 1) * rows].reshape(cols, rows)
        back = chunk((back0_ref, back1_ref, back2_ref), k, rows).astype(f32)
        deal(k, back + dot_tn(grad, wq_ref[...]) * g1, keep0_ref, keep2_ref, send_ref)


def forward_kernel(keep2_ref, got_ref, sent_ref):
    rows = keep2_ref.shape[0]
    sent_ref[...] = (keep2_ref[...] + got_ref[rows:, :].astype(f32)).astype(bf16)


def result_kernel(x_ref, keep0_ref, got_ref, far_ref, bd_ref, c2_ref, out_ref):
    rows = x_ref.shape[0]
    summed = keep0_ref[...] + got_ref[:rows, :].astype(f32) + far_ref[...].astype(f32)
    out_ref[...] = (x_ref[...].astype(f32) + summed + (row_of(bd_ref) + row_of(c2_ref))).astype(bf16)


def tokens_grad_kernel(x_ref, dy_ref, keep0_ref, got_ref, far_ref, out_ref):
    rows = x_ref.shape[0]
    grad = keep0_ref[...] + got_ref[:rows, :].astype(f32) + far_ref[...].astype(f32)
    x = x_ref[...].astype(f32)
    c = x - jnp.mean(x, axis=1, keepdims=True)
    inverse = lax.rsqrt(jnp.mean(c * c, axis=1, keepdims=True) + 1e-05)
    xh = c * inverse
    term = grad - jnp.mean(grad, axis=1, keepdims=True)
    term = term - xh * jnp.mean(grad * xh, axis=1, keepdims=True)
    out_ref[...] = dy_ref[...].astype(f32) + inverse * term


def swap(value, axis, size, distance):
    return lax.ppermute(value, axis, [(i, i ^ distance) for i in range(size)])


def unpair(rows):
    return rows[0:8, :].astype(f32) + rows[8:16, :].astype(f32)


def fold_kernel(place_ref, keep_ref, got_ref, next_ref, send_ref, *, bit, tail):
    rows = (keep_ref.shape[0] - tail) // 2
    side = bit_of(place_ref, bit)
    for half, out_ref in ((side, next_ref), (1 - side, send_ref)):
        at = pl.ds(pl.multiple_of(half * rows, 16), rows)
        out_ref[0:rows, :] = (keep_ref[at, :].astype(f32) + got_ref[at, :].astype(f32)).astype(bf16)
    if tail:
        vectors = pair_rows([unpair(keep_ref[2 * rows :, :]) + unpair(got_ref[2 * rows :, :])])
        next_ref[rows:, :] = vectors
        send_ref[rows:, :] = vectors


def total_kernel(keep_ref, got_ref, out_ref, *vector_ref):
    rows = out_ref.shape[0]
    total = keep_ref[0:rows, :].astype(f32) + got_ref[0:rows, :].astype(f32)
    out_ref[...] = total.astype(bf16)
    if vector_ref:
        vector_ref[0][...] = unpair(keep_ref[rows:, :]) + unpair(got_ref[rows:, :])


def join_kernel(place_ref, mine_ref, got_ref, *out_refs, bit):
    side = bit_of(place_ref, bit)
    rows = mine_ref.shape[0]
    out_ref = out_refs[-1]
    for part, ref in ((side, mine_ref), (1 - side, got_ref)):
        at = pl.ds(pl.multiple_of(part * rows, 16), rows)
        out_ref[at, :] = ref[...].astype(out_ref.dtype)
    if len(out_refs) > 1:
        split = out_refs[0].shape[0]
        out_refs[0][...] = out_ref[:split, :]
        out_refs[1][...] = out_ref[split:, :]


def dp_swap(value, dp, bit):
    return swap(value, "dp", dp, 1 << bit)


def fold(place, keep, got, bit, tail=0):
    rows = (keep.shape[0] - tail) // 2 + tail
    return call(
        partial(fold_kernel, bit=bit, tail=tail), "fold", [place, keep, got],
        [like((rows, keep.shape[1]), bf16)] * 2, smem=(0,),
    )


def join(place, mine, got, bit, outs=None):
    width = mine.shape[1]
    if outs is None:
        outs = [like((2 * mine.shape[0], width), bf16)]
    scratch = [pltpu.VMEM((2 * mine.shape[0], width), f32)] if len(outs) > 1 else []
    return call(
        partial(join_kernel, bit=bit), "join", [place, mine, got], outs, scratch, smem=(0,),
    )


def rest_sum(value, dp):
    if dp == 8:
        return value
    groups = [[i + 8 * j for j in range(dp // 8)] for i in range(8)]
    return lax.psum(value, "dp", axis_index_groups=groups)


def rotary_tables(length):
    half = ROT // 2
    freq = np.float32(10000.0) ** (-(np.arange(half, dtype=np.float32) * 2.0) / ROT)
    angle = freq.astype(np.float32)[:, None] * np.arange(length, dtype=np.float32)[None, :]
    return np.cos(angle).astype(np.float32), np.sin(angle).astype(np.float32)


def body(dp, tp, tokens, segment_ids, cotangent, gain1, bias1, gain2, bias2,
         qkv_weight, qkv_bias, dense_weight, dense_bias, fc_in_weight, fc_in_bias,
         fc_out_weight, fc_out_bias):
    assert tp == 4 and dp % 8 == 0
    x0, dy0 = tokens[0], cotangent[0]
    rows, width = x0.shape
    seq = rows * tp
    count = seq // BLK
    wq = qkv_weight.T
    heads = wq.shape[0] // (3 * HEAD_DIM)
    cosine, sine = rotary_tables(seq)
    place = jnp.stack([lax.axis_index("tensor"), lax.axis_index("dp")]).astype(i32)

    x1 = swap(x0, "tensor", tp, 1)
    x2 = swap(x0, "tensor", tp, 2)
    dy1 = swap(dy0, "tensor", tp, 1)
    dy2 = swap(dy0, "tensor", tp, 2)

    bq_column = qkv_bias.astype(f32)[:, None]
    start, lo = call(
        segments_kernel, "segments", [segment_ids, segment_ids],
        [like((1, seq), i32), like((count,), i32)], smem=(1,), smem_out=(1,), flops=8 * UNIT,
    )
    (x1,) = after(start, x1)
    hidden, inner = fc_in_weight.shape[1], dense_weight.shape[0]

    def front(xs, first):
        size = rows * len(xs)
        return call(
            partial(front_kernel, first=first, pieces=len(xs)), "front",
            [place, *xs, gain1, bias1, gain2, bias2, fc_in_weight, fc_in_bias, wq, bq_column,
             cosine, sine],
            [like((size, width), bf16), like((size, hidden), bf16), like((size, hidden), bf16),
             like((heads, 3, HEAD_DIM, size), bf16)],
            smem=(0,), limit=16, flops=len(xs) * 2 * UNIT,
        )

    def ff_back(dys, act, slope, xh, carry=(), last=False):
        size = rows * len(dys)
        outs = [like((size, width), bf16), like((size, width), bf16), like((inner, size), bf16)]
        full = [like((width, hidden), f32), like((hidden, width), f32)]
        sums = [like((8, width), f32)]
        half = [like((width // 2, hidden), bf16)] * 2 + [like((hidden // 2, width), bf16)] * 2
        scratch = [
            pltpu.VMEM((width, hidden), f32), pltpu.VMEM((hidden, width), f32),
            pltpu.VMEM((width, hidden), bf16),
        ]
        return call(
            partial(ff_back_kernel, pieces=len(dys), carried=bool(carry), last=last), "ff_back",
            [place, *dys, act, slope, xh, gain2, bias2, fc_in_weight, fc_out_weight, dense_weight,
             *carry],
            outs + (half if last else full) + sums, scratch if last else [],
            smem=(0,), limit=22 if last else 16, flops=len(dys) * 4 * UNIT,
        )

    xh0, act0, slope0, qkv0 = front((x0, x1), 0)
    (act0,) = after(qkv0, act0)
    out0, back0, do0, *carry = ff_back((dy0, dy1), act0, slope0, xh0)
    x3 = swap(*after(carry[2], x2), "tensor", tp, 1)
    (x2,) = after(carry[2], x2)
    xh1, act1, slope1, qkv1 = front((x2,), 2)
    (x3,) = after(qkv1, x3)
    xh2, act2, slope2, qkv2 = front((x3,), 3)
    qkv, mixed, lse = call(
        attend_kernel, "attend", [place, lo, start, qkv0, qkv1, qkv2],
        [like((heads, 3, HEAD_DIM, seq), bf16), like((inner, seq), bf16), like((heads, 1, seq), f32)],
        [pltpu.VMEM((heads, seq, HEAD_DIM), bf16)],
        smem=(0, 1), limit=12, flops=10 * UNIT,
    )
    dy3 = swap(*after(lse, dy2), "tensor", tp, 1)
    (dy2,) = after(lse, dy2)
    out1, back1, do1, *carry = ff_back((dy2,), act1, slope1, xh1, carry)
    (dy3,) = after(carry[2], dy3)
    out2, back2, do2, k1, s1, k2, s2, sums = ff_back((dy3,), act2, slope2, xh2, carry, last=True)

    got2 = dp_swap(s2, dp, ORDER_A[0])
    got1 = dp_swap(s1, dp, ORDER_B[0])
    (mixed_late,) = after(sums, mixed)
    pair = 2 * rows
    keep0, keep2, send, dense_grad = call(
        attend_end_kernel, "attend_end",
        [mixed_late, dy0, dy1, dy2, dy3, dense_weight, out0, out1, out2],
        [like((rows, width), f32), like((rows, width), f32), like((pair, width), bf16),
         like((inner, width), bf16)],
        limit=12, flops=3 * UNIT,
    )
    got = swap(send, "tensor", tp, 1)
    (mixed_late,) = after(dense_grad, mixed)
    (dqkv,) = call(
        attend_back_kernel, "attend_back",
        [place, lo, start, qkv, mixed_late, do0, do1, do2, lse, cosine, sine],
        [like((heads, 3, HEAD_DIM, seq), bf16)],
        [
            pltpu.VMEM((inner, seq), bf16),
            pltpu.VMEM((heads, seq, HEAD_DIM), bf16), pltpu.VMEM((heads, seq, HEAD_DIM), bf16),
            pltpu.VMEM((heads, HEAD_DIM, seq), f32), pltpu.VMEM((heads, HEAD_DIM, seq), f32),
        ],
        smem=(0, 1), limit=20, flops=14 * UNIT,
    )
    keep2, got, got1, got2 = after(dqkv, keep2, got, got1, got2)
    far = swap(call(forward_kernel, "forward", [keep2, got], [like((rows, width), bf16)])[0],
               "tensor", tp, 2)
    k2, s2 = fold(place, k2, got2, ORDER_A[1])
    got2 = dp_swap(s2, dp, ORDER_A[1])
    k1, s1 = fold(place, k1, got1, ORDER_B[1])
    got1 = dp_swap(s1, dp, ORDER_B[1])

    tail = 16
    (dqkv,) = after((k1, k2), dqkv)
    keep_c, send_c = call(
        qkv_end_kernel, "qkv_end",
        [place, dqkv, xh0, xh1, xh2, wq, gain1, bias1, dense_grad, sums],
        [like((width // 2 + tail, width), bf16)] * 2,
        [pltpu.VMEM((wq.shape[0] + inner, width), bf16)],
        smem=(0,), limit=12, flops=3 * UNIT,
    )
    got_c = dp_swap(send_c, dp, ORDER_A[0])
    (dqkv,) = after(keep_c, dqkv)
    keep0b, keep2b, sendb = call(
        tokens_back_kernel, "tokens_back", [dqkv, back0, back1, back2, wq, gain1],
        [like((rows, width), f32), like((rows, width), f32), like((pair, width), bf16)],
        limit=8, flops=3 * UNIT,
    )
    gotb = swap(sendb, "tensor", tp, 1)

    def finish_sum(keep, got, vector=0):
        size = keep.shape[0] - vector
        outs = [like((size, width), bf16)] + ([like((8, width), f32)] if vector else [])
        total = call(total_kernel, "total", [keep, got], outs)
        if dp == 8:
            return total
        return [rest_sum(total[0].astype(f32), dp).astype(bf16)] + [
            rest_sum(t, dp) for t in total[1:]
        ]

    k2, s2 = fold(place, k2, got2, ORDER_A[2])
    got2 = dp_swap(s2, dp, ORDER_A[2])
    k1, s1 = fold(place, k1, got1, ORDER_B[2])
    got1 = dp_swap(s1, dp, ORDER_B[2])
    farb = swap(call(forward_kernel, "forward", [keep2b, gotb], [like((rows, width), bf16)])[0],
                "tensor", tp, 2)
    keep_c, send_c = fold(place, keep_c, got_c, ORDER_A[1], tail)
    got_c = dp_swap(send_c, dp, ORDER_A[1])

    (mine2,) = finish_sum(k2, got2)
    (mine1,) = finish_sum(k1, got1)
    for step in (2, 1):
        mine2 = join(place, mine2, dp_swap(mine2, dp, ORDER_A[step]), ORDER_A[step])[0]
        mine1 = join(place, mine1, dp_swap(mine1, dp, ORDER_B[step]), ORDER_B[step])[0]
    w2_grad = join(place, mine2, dp_swap(mine2, dp, ORDER_A[0]), ORDER_A[0],
                   [like((hidden, width), f32)])[0]
    w1_grad = join(place, mine1, dp_swap(mine1, dp, ORDER_B[0]), ORDER_B[0],
                   [like((width, hidden), f32)])[0]

    keep_c, send_c = fold(place, keep_c, got_c, ORDER_A[2], tail)
    got_c = dp_swap(send_c, dp, ORDER_A[2])
    mine_c, vectors = finish_sum(keep_c, got_c, tail)
    for step in (2, 1):
        mine_c = join(place, mine_c, dp_swap(mine_c, dp, ORDER_A[step]), ORDER_A[step])[0]
    wq_grad, wd_grad = join(
        place, mine_c, dp_swap(mine_c, dp, ORDER_A[0]), ORDER_A[0],
        [like((wq.shape[0], width), f32), like((inner, width), f32)],
    )
    near = vectors + swap(vectors, "tensor", tp, 1)
    near = near + swap(near, "tensor", tp, 2)
    result = call(
        result_kernel, "result", [x0, keep0, got, far, dense_bias, fc_out_bias],
        [like((rows, width), bf16)],
    )[0]
    input_grad = call(
        tokens_grad_kernel, "tokens_grad", [x0, dy0, keep0b, gotb, farb],
        [like((rows, width), f32)],
    )[0]
    return (
        result[None], input_grad[None], near[0], near[1], near[2], near[3],
        wq_grad.T, vectors[6, : wq.shape[0]], wd_grad, vectors[4],
        w1_grad, vectors[5], w2_grad, vectors[4],
    )


def solution(mesh):
    split = P("dp", "tensor", None)
    columns, stacked, vector = P(None, "tensor"), P("tensor", None), P("tensor")
    whole = P()
    return jax.shard_map(
        partial(body, mesh.shape["dp"], mesh.shape["tensor"]),
        mesh=mesh,
        in_specs=(
            split, P("dp", None), split, whole, whole, whole, whole, columns, vector, stacked,
            whole, columns, vector, stacked, whole,
        ),
        out_specs=(
            split, split, whole, whole, whole, whole, columns, vector, stacked, whole, columns,
            vector, stacked, whole,
        ),
        check_vma=False,
    )
```

time: 239 us -> 193 us (0.81)
  starting transfers between devices: 58.8 us -> 30.3 us
  waiting for transfers between devices: 90.3 us -> 72.4 us
  local copies, waits for them, and re-layouts: 12.7 us -> 3.34 us
  Pallas kernels: 76.7 us -> 85.3 us
    ppermute x18 -> x0, starting transfers between devices: 44.5 us -> none  [shifted(): return lax.ppermute(value, 'dp', pairs)]
    ppermute x18 -> x0, waiting for transfers between devices: 30.1 us -> none  [shifted(): return lax.ppermute(value, 'dp', pairs)]
    ppermute x18 -> x30, starting transfers between devices: 14.3 us -> 30.3 us  [swap(): return lax.ppermute(value, axis, [(i, i ^ distance) for i in range(size)])]
    ppermute x18 -> x30, waiting for transfers between devices: 60.2 us -> 72.4 us  [swap(): return lax.ppermute(value, axis, [(i, i ^ distance) for i in range(size)])]
    unnamed x58 -> x37, local copies, waits for them, and re-layouts: 10.1 us -> 1.37 us
    pallas_call x21 -> x34, Pallas kernels: 76.7 us -> 85.3 us  [call(): pl.pallas_call(kernel, out_shape=tuple(outs), in_specs=[SMEM if i in smem...]
  transfers between devices with their start and end apart: 36 -> 30, of which waited for: 13 -> 15; matrix products, arithmetic and copies ran while one was open for 1% -> 1% of each run, Pallas kernels for 28% -> 35%
where the time goes in v1:
time: 193 us
  Pallas kernels  85.3 us (44%)
  waiting for transfers between devices  72.4 us (38%)
  starting transfers between devices  30.3 us (16%)
  local copies, waits for them, and re-layouts  3.34 us (2%)
    pallas_call x34, Pallas kernels, call(): pl.pallas_call(kernel, out_shape=tuple(outs), in_specs=[SMEM if i in smem...  85.3 us
    ppermute x30, waiting for transfers between devices, swap(): return lax.ppermute(value, axis, [(i, i ^ distance) for i in range(size)])  72.4 us
    ppermute x30, starting transfers between devices, swap(): return lax.ppermute(value, axis, [(i, i ^ distance) for i in range(size)])  30.3 us
  transfers between devices with their start and end apart: 30, of which 15 were waited for; matrix products, arithmetic and copies ran while one was open for 1% of the time, Pallas kernels for 35%

profile of v1, /device:TPU:0, one launch (start us, length us, event | category | flops | bytes accessed | tf_op | source)
XLA Modules:
  0.0 192.6 jit_solution(16894743005650055431)
XLA Ops:
  1.4 2.9 %collective-permute-start.2 = (bf16[512,768]{1,0:T(8,128)(2,1)}, bf16[512,768]{1,0:T(8,128)(2,1)}, u32[]{:S(2)}, u32[]{:S(2)}) collective-permute-start(bf16[512,768]{1,0:T(8,128)(2,1)} %bitcast.14), channel_id=1, source_target_pairs={{0,2},{1,3},{2,0},{3,1},{4,6},{5,7},{6,4},{7,5},{8,10},{9,11},{10,... | collective-permute-start | bytes 2359304 | tf_op jit(solution)/shard_map/ppermute | solution.py:435
  6.9 5.1 %front.3 = (bf16[1024,768]{1,0:T(8,128)(2,1)S(1)}, bf16[1024,768]{1,0:T(8,128)(2,1)S(1)}, bf16[1024,768]{1,0:T(8,128)(2,1)S(1)}, bf16[3,3,64,1024]{3,2,1,0:T(8,128)(2,1)S(1)}) custom-call(s32[2]{0:T(128)S(1)} %pad_add_fusion.place_ref, bf16[512,768]{1,0:T(8,128)(2,1)S(1)} %bitcast.15, bf16[512,768]{1,0:T(8,128)(2,1)} %collective-permute-done.refs_1_, ...), custom_call_target="tpu_custom_call" | custom-call | flops 2000000000 | bytes 1000 | tf_op jit(solution)/shard_map/front/pallas_call | solution.py:42
  12.0 8.0 %ff_back.3 = (bf16[1024,768]{1,0:T(8,128)(2,1)S(1)}, bf16[1024,768]{1,0:T(8,128)(2,1)S(1)}, bf16[192,1024]{1,0:T(8,128)(2,1)S(1)}, f32[768,768]{1,0:T(8,128)S(1)...) custom-call(s32[2]{0:T(128)S(1)} %pad_add_fusion.place_ref, bf16[512,768]{1,0:T(8,128)(2,1)S(1)} %bitcast.19, ...), custom_call_target="tpu_custom_call" | custom-call | flops 4000000000 | bytes 1000 | tf_op jit(solution)/shard_map/ff_back/pallas_call | solution.py:42
  24.1 3.0 %front.4 = (bf16[512,768]{1,0:T(8,128)(2,1)S(1)}, bf16[512,768]{1,0:T(8,128)(2,1)S(1)}, bf16[512,768]{1,0:T(8,128)(2,1)S(1)}, bf16[3,3,64,512]{3,2,1,0:T(8,128)(2,1)S(1)}) custom-call(s32[2]{0:T(128)S(1)} %pad_add_fusion.place_ref, bf16[512,768]{1,0:T(8,128)(2,1)} %collective-permute-done.2.refs_0_, bf16[768]{0:T(1024)(128)(2,1)S(1)} %copy-done.6, ...), custom_call_target="tpu_custom_call" | custom-call | flops 1000000000 | bytes 1000 | tf_op jit(solution)/shard_map/front/pallas_call | solution.py:42
  27.1 2.6 %front.5 = (bf16[512,768]{1,0:T(8,128)(2,1)S(1)}, bf16[512,768]{1,0:T(8,128)(2,1)S(1)}, bf16[512,768]{1,0:T(8,128)(2,1)S(1)}, bf16[3,3,64,512]{3,2,1,0:T(8,128)(2,1)S(1)}) custom-call(s32[2]{0:T(128)S(1)} %pad_add_fusion.place_ref, bf16[512,768]{1,0:T(8,128)(2,1)S(1)} %collective-permute-done.3.refs_0_, bf16[768]{0:T(1024)(128)(2,1)S(1)} %copy-done.6, ...), custom_call_target="tpu_custom_call" | custom-call | flops 1000000000 | bytes 1000 | tf_op jit(solution)/shard_map/front/pallas_call | solution.py:42
  29.7 12.7 %attend.1 = (bf16[3,3,64,2048]{3,2,1,0:T(8,128)(2,1)S(1)}, bf16[192,2048]{1,0:T(8,128)(2,1)S(1)}, f32[3,1,2048]{2,1,0:T(1,128)S(1)}) custom-call(s32[2]{0:T(128)S(1)} %pad_add_fusion.place_ref, s32[8]{0:T(128)S(1)} %get-tuple-element.90.lo_ref, s32[1,2048]{1,0:T(1,128)S(1)} %get-tuple-element.91.start_ref, ...), custom_call_target="tpu_custom_call" | custom-call | flops 5000000000 | bytes 1000 | tf_op jit(solution)/shard_map/attend/pallas_call | solution.py:42
  42.8 4.1 %ff_back.4 = (bf16[512,768]{1,0:T(8,128)(2,1)S(1)}, bf16[512,768]{1,0:T(8,128)(2,1)S(1)}, bf16[192,512]{1,0:T(8,128)(2,1)S(1)}, f32[768,768]{1,0:T(8,128)S(1)}, ...) custom-call(s32[2]{0:T(128)S(1)} %pad_add_fusion.place_ref, bf16[512,768]{1,0:T(8,128)(2,1)S(1)} %collective-permute-done.4.refs_0_.dy2_ref, ...), custom_call_target="tpu_custom_call" | custom-call | flops 2000000000 | bytes 1000 | tf_op jit(solution)/shard_map/ff_back/pallas_call | solution.py:42
  46.9 5.4 %ff_back.5 = (bf16[512,768]{1,0:T(8,128)(2,1)S(1)}, bf16[512,768]{1,0:T(8,128)(2,1)S(1)}, bf16[192,512]{1,0:T(8,128)(2,1)S(1)}, bf16[384,768]{1,0:T(8,128)(2,1)S...) custom-call(s32[2]{0:T(128)S(1)} %pad_add_fusion.place_ref, ...), custom_call_target="tpu_custom_call" | custom-call | flops 2000000000 | bytes 1000 | tf_op jit(solution)/shard_map/ff_back/pallas_call | solution.py:42
  52.3 2.9 %attend_end.1 = (f32[512,768]{1,0:T(8,128)S(1)}, f32[512,768]{1,0:T(8,128)S(1)}, bf16[1024,768]{1,0:T(8,128)(2,1)S(1)}, bf16[192,768]{1,0:T(8,128)(2,1)S(1)}) custom-call(bf16[192,2048]{1,0:T(8,128)(2,1)S(1)} %get-tuple-element.126.o_ref, bf16[512,768]{1,0:T(8,128)(2,1)S(1)} %bitcast.21, bf16[512,768]{1,0:T(8,128)(2,1)} %collective-permute-done.1.refs_1_.dy1_ref, ...), custom_call_target="tpu_custom_call" | custom-call | flops 1500000000 | bytes 1000 | tf_op jit(solution)/shard_map/attend_end/pallas_call | solution.py:42
  59.2 16.2 %attend_back.1.dqkv_ref = bf16[3,3,64,2048]{3,2,1,0:T(8,128)(2,1)S(1)} custom-call(s32[2]{0:T(128)S(1)} %pad_add_fusion.place_ref, s32[8]{0:T(128)S(1)} %get-tuple-element.90.lo_ref, s32[1,2048]{1,0:T(1,128)S(1)} %get-tuple-element.91.start_ref, bf16[3,3,64,2048]{3,2,1,0:T(8,128)(2,1)S(1)} %get-tuple-element.124.qkv_ref, ...), custom_call_target="tpu_custom_call" | custom-call | flops 7000000000 | bytes 1000 | tf_op jit(solution)/shard_map/attend_back/pallas_call | solution.py:42
  76.9 3.1 %qkv_end.1 = (bf16[400,768]{1,0:T(8,128)(2,1)S(1)}, bf16[400,768]{1,0:T(8,128)(2,1)S(1)}) custom-call(s32[2]{0:T(128)S(1)} %pad_add_fusion.place_ref, bf16[3,3,64,2048]{3,2,1,0:T(8,128)(2,1)S(1)} %attend_back.1.dqkv_ref, bf16[1024,768]{1,0:T(8,128)(2,1)S(1)} %get-tuple-element.97.refs_4_.xh0_ref, bf16[512,768]{1,0:T(8,128)(2,1)S(1)} %get-tuple-element.107.refs_3_.xh1_ref, ...), custom_call_target="tpu_custom_call" | custom-call | flops 1500000000 | bytes 1000 | tf_op jit(solution)/shard_map/qkv_end/pallas_call | solution.py:42
  80.0 2.7 %tokens_back.1 = (f32[512,768]{1,0:T(8,128)S(1)}, f32[512,768]{1,0:T(8,128)S(1)}, bf16[1024,768]{1,0:T(8,128)(2,1)S(1)}) custom-call(bf16[3,3,64,2048]{3,2,1,0:T(8,128)(2,1)S(1)} %attend_back.1.dqkv_ref, bf16[1024,768]{1,0:T(8,128)(2,1)S(1)} %get-tuple-element.145.back0_ref, bf16[512,768]{1,0:T(8,128)(2,1)S(1)} %get-tuple-element.146.back1_ref, ...), custom_call_target="tpu_custom_call" | custom-call | flops 1500000000 | bytes 1000 | tf_op jit(solution)/shard_map/tokens_back/pallas_call | solution.py:42
  84.0 15.0 %collective-permute-done.12.got_ref = bf16[400,768]{1,0:T(8,128)(2,1)S(1)} collective-permute-done((bf16[400,768]{1,0:T(8,128)(2,1)S(1)}, bf16[400,768]{1,0:T(8,128)(2,1)S(1)}, u32[]{:S(2)}, u32[]{:S(2)}) %collective-permute-start.12) | collective-permute-done | bytes 614432 | tf_op jit(solution)/shard_map/ppermute | solution.py:435
  103.0 7.2 %collective-permute-done.13.got_ref = bf16[208,768]{1,0:T(8,128)(2,1)S(1)} collective-permute-done((bf16[208,768]{1,0:T(8,128)(2,1)S(1)}, bf16[208,768]{1,0:T(8,128)(2,1)S(1)}, u32[]{:S(2)}, u32[]{:S(2)}) %collective-permute-start.13) | collective-permute-done | bytes 319520 | tf_op jit(solution)/shard_map/ppermute | solution.py:435
  113.1 5.4 %collective-permute-done.25.got_ref = bf16[192,768]{1,0:T(8,128)(2,1)S(1)} collective-permute-done((bf16[192,768]{1,0:T(8,128)(2,1)S(1)}, bf16[192,768]{1,0:T(8,128)(2,1)S(1)}, u32[]{:S(2)}, u32[]{:S(2)}) %collective-permute-start.25) | collective-permute-done | bytes 294944 | tf_op jit(solution)/shard_map/ppermute | solution.py:435
  120.0 2.8 %collective-permute-start.21 = (bf16[96,768]{1,0:T(8,128)(2,1)S(1)}, bf16[96,768]{1,0:T(8,128)(2,1)S(1)}, u32[]{:S(2)}, u32[]{:S(2)}) collective-permute-start(bf16[96,768]{1,0:T(8,128)(2,1)S(1)} %get-tuple-element.162), channel_id=1, source_target_pairs={{0,16},{4,20},{8,24},{12,28},{16,0},{20,4},{24,8},{28,12},{1,17},{... | collective-permute-start | bytes 442376 | tf_op jit(solution)/shard_map/ppermute | solution.py:435
  124.4 6.4 %collective-permute-done.26.got_ref = bf16[96,768]{1,0:T(8,128)(2,1)S(1)} collective-permute-done((bf16[96,768]{1,0:T(8,128)(2,1)S(1)}, bf16[96,768]{1,0:T(8,128)(2,1)S(1)}, u32[]{:S(2)}, u32[]{:S(2)}) %collective-permute-start.26) | collective-permute-done | bytes 147488 | tf_op jit(solution)/shard_map/ppermute | solution.py:435
  130.9 9.4 %collective-permute-done.21.got_ref = bf16[96,768]{1,0:T(8,128)(2,1)S(1)} collective-permute-done((bf16[96,768]{1,0:T(8,128)(2,1)S(1)}, bf16[96,768]{1,0:T(8,128)(2,1)S(1)}, u32[]{:S(2)}, u32[]{:S(2)}) %collective-permute-start.21) | collective-permute-done | bytes 147488 | tf_op jit(solution)/shard_map/ppermute | solution.py:435
  140.4 3.0 %collective-permute-start.17 = (bf16[96,768]{1,0:T(8,128)(2,1)S(1)}, bf16[96,768]{1,0:T(8,128)(2,1)S(1)}, u32[]{:S(2)}, u32[]{:S(2)}) collective-permute-start(bf16[96,768]{1,0:T(8,128)(2,1)S(1)} %get-tuple-element.157.mine_ref), channel_id=1, source_target_pairs={{0,16},{4,20},{8,24},{12,28},{16,0},{20,4},{24,8},{28,12},{1,17},{... | collective-permute-start | bytes 442376 | tf_op jit(solution)/shard_map/ppermute | solution.py:435
  143.4 3.2 %collective-permute-done.27.got_ref = bf16[96,768]{1,0:T(8,128)(2,1)S(1)} collective-permute-done((bf16[96,768]{1,0:T(8,128)(2,1)S(1)}, bf16[96,768]{1,0:T(8,128)(2,1)S(1)}, u32[]{:S(2)}, u32[]{:S(2)}) %collective-permute-start.27) | collective-permute-done | bytes 147488 | tf_op jit(solution)/shard_map/ppermute | solution.py:435
  147.2 2.6 %collective-permute-done.22.got_ref = bf16[96,768]{1,0:T(8,128)(2,1)S(1)} collective-permute-done((bf16[96,768]{1,0:T(8,128)(2,1)S(1)}, bf16[96,768]{1,0:T(8,128)(2,1)S(1)}, u32[]{:S(2)}, u32[]{:S(2)}) %collective-permute-start.22) | collective-permute-done | bytes 147488 | tf_op jit(solution)/shard_map/ppermute | solution.py:435
  154.5 4.4 %collective-permute-done.28.got_ref = bf16[192,768]{1,0:T(8,128)(2,1)S(1)} collective-permute-done((bf16[192,768]{1,0:T(8,128)(2,1)S(1)}, bf16[192,768]{1,0:T(8,128)(2,1)S(1)}, u32[]{:S(2)}, u32[]{:S(2)}) %collective-permute-start.28) | collective-permute-done | bytes 294944 | tf_op jit(solution)/shard_map/ppermute | solution.py:435
  161.3 4.0 %collective-permute-done.18.got_ref = bf16[192,768]{1,0:T(8,128)(2,1)S(1)} collective-permute-done((bf16[192,768]{1,0:T(8,128)(2,1)S(1)}, bf16[192,768]{1,0:T(8,128)(2,1)S(1)}, u32[]{:S(2)}, u32[]{:S(2)}) %collective-permute-start.18) | collective-permute-done | bytes 294944 | tf_op jit(solution)/shard_map/ppermute | solution.py:435
  180.0 7.4 %collective-permute-done.19.got_ref = bf16[384,768]{1,0:T(8,128)(2,1)S(1)} collective-permute-done((bf16[384,768]{1,0:T(8,128)(2,1)S(1)}, bf16[384,768]{1,0:T(8,128)(2,1)S(1)}, u32[]{:S(2)}, u32[]{:S(2)}) %collective-permute-start.19) | collective-permute-done | bytes 589856 | tf_op jit(solution)/shard_map/ppermute | solution.py:435
  (114 shorter events, 52.0 us)
Async XLA Ops:
  1.2 10.7 %collective-permute-start.1 = (bf16[512,768]{1,0:T(8,128)(2,1)}, bf16[512,768]{1,0:T(8,128)(2,1)}, u32[]{:S(2)}, u32[]{:S(2)}) collective-permute-start(bf16[512,768]{1,0:T(8,128)(2,1)} %bitcast.18), channel_id=1, source_target_pairs={{0,1},{1,0},{2,3},{3,2},{4,5},{5,4},{6,7},{7,6},{8,9},{9,8},{10,11... | collective-permute-start | bytes 2359304 | tf_op jit(solution)/shard_map/ppermute | solution.py:435
  1.4 21.0 %collective-permute-start.2 = (bf16[512,768]{1,0:T(8,128)(2,1)}, bf16[512,768]{1,0:T(8,128)(2,1)}, u32[]{:S(2)}, u32[]{:S(2)}) collective-permute-start(bf16[512,768]{1,0:T(8,128)(2,1)} %bitcast.14), channel_id=1, source_target_pairs={{0,2},{1,3},{2,0},{3,1},{4,6},{5,7},{6,4},{7,5},{8,10},{9,11},{10,... | collective-permute-start | bytes 2359304 | tf_op jit(solution)/shard_map/ppermute | solution.py:435
  22.4 20.0 %collective-permute-start.4 = (bf16[512,768]{1,0:T(8,128)(2,1)S(1)}, bf16[512,768]{1,0:T(8,128)(2,1)S(1)}, u32[]{:S(2)}, u32[]{:S(2)}) collective-permute-start(bf16[512,768]{1,0:T(8,128)(2,1)S(1)} %bitcast.20), channel_id=1, source_target_pairs={{0,2},{1,3},{2,0},{3,1},{4,6},{5,7},{6,4},{7,5},{8,10},{9,11},{10,... | collective-permute-start | bytes 2359304 | tf_op jit(solution)/shard_map/ppermute | solution.py:435
  55.2 20.3 %collective-permute-start.6 = (bf16[1024,768]{1,0:T(8,128)(2,1)S(1)}, bf16[1024,768]{1,0:T(8,128)(2,1)S(1)}, u32[]{:S(2)}, u32[]{:S(2)}) collective-permute-start(bf16[1024,768]{1,0:T(8,128)(2,1)S(1)} %get-tuple-element.131), channel_id=1, source_target_pairs={{0,1},{1,0},{2,3},{3,2},{4,5},{5,4},{6,7},{7,6},{8,9},{9,8},{10,11... | collective-permute-start | bytes 4718600 | tf_op jit(solution)/shard_map/ppermute | solution.py:435
  55.5 19.9 %collective-permute-start.7 = (bf16[384,768]{1,0:T(8,128)(2,1)S(1)}, bf16[384,768]{1,0:T(8,128)(2,1)S(1)}, u32[]{:S(2)}, u32[]{:S(2)}) collective-permute-start(bf16[384,768]{1,0:T(8,128)(2,1)S(1)} %get-tuple-element.132), channel_id=1, source_target_pairs={{0,8},{4,12},{8,0},{12,4},{16,24},{20,28},{24,16},{28,20},{1,9},{5... | collective-permute-start | bytes 1769480 | tf_op jit(solution)/shard_map/ppermute | solution.py:435
  57.7 17.8 %collective-permute-start.8 = (bf16[384,768]{1,0:T(8,128)(2,1)S(1)}, bf16[384,768]{1,0:T(8,128)(2,1)S(1)}, u32[]{:S(2)}, u32[]{:S(2)}) collective-permute-start(bf16[384,768]{1,0:T(8,128)(2,1)S(1)} %get-tuple-element.133), channel_id=1, source_target_pairs={{0,4},{4,0},{8,12},{12,8},{16,20},{20,16},{24,28},{28,24},{1,5},{5... | collective-permute-start | bytes 1769480 | tf_op jit(solution)/shard_map/ppermute | solution.py:435
  82.7 70.5 %collective-permute-start.10 = (bf16[1024,768]{1,0:T(8,128)(2,1)S(1)}, bf16[1024,768]{1,0:T(8,128)(2,1)S(1)}, u32[]{:S(2)}, u32[]{:S(2)}) collective-permute-start(bf16[1024,768]{1,0:T(8,128)(2,1)S(1)} %get-tuple-element.149), channel_id=1, source_target_pairs={{0,1},{1,0},{2,3},{3,2},{4,5},{5,4},{6,7},{7,6},{8,9},{9,8},{10,11... | collective-permute-start | bytes 4718600 | tf_op jit(solution)/shard_map/ppermute | solution.py:435
  82.8 16.3 %collective-permute-start.12 = (bf16[400,768]{1,0:T(8,128)(2,1)S(1)}, bf16[400,768]{1,0:T(8,128)(2,1)S(1)}, u32[]{:S(2)}, u32[]{:S(2)}) collective-permute-start(bf16[400,768]{1,0:T(8,128)(2,1)S(1)} %get-tuple-element.151), channel_id=1, source_target_pairs={{0,4},{4,0},{8,12},{12,8},{16,20},{20,16},{24,28},{28,24},{1,5},{5... | collective-permute-start | bytes 1843208 | tf_op jit(solution)/shard_map/ppermute | solution.py:435
  99.8 10.5 %collective-permute-start.13 = (bf16[208,768]{1,0:T(8,128)(2,1)S(1)}, bf16[208,768]{1,0:T(8,128)(2,1)S(1)}, u32[]{:S(2)}, u32[]{:S(2)}) collective-permute-start(bf16[208,768]{1,0:T(8,128)(2,1)S(1)} %get-tuple-element.153), channel_id=1, source_target_pairs={{0,8},{4,12},{8,0},{12,4},{16,24},{20,28},{24,16},{28,20},{1,9},{5... | collective-permute-start | bytes 958472 | tf_op jit(solution)/shard_map/ppermute | solution.py:435
  101.0 17.5 %collective-permute-start.25 = (bf16[192,768]{1,0:T(8,128)(2,1)S(1)}, bf16[192,768]{1,0:T(8,128)(2,1)S(1)}, u32[]{:S(2)}, u32[]{:S(2)}) collective-permute-start(bf16[192,768]{1,0:T(8,128)(2,1)S(1)} %get-tuple-element.163), channel_id=1, source_target_pairs={{0,8},{4,12},{8,0},{12,4},{16,24},{20,28},{24,16},{28,20},{1,9},{5... | collective-permute-start | bytes 884744 | tf_op jit(solution)/shard_map/ppermute | solution.py:435
  101.9 17.5 %collective-permute-start.20 = (bf16[192,768]{1,0:T(8,128)(2,1)S(1)}, bf16[192,768]{1,0:T(8,128)(2,1)S(1)}, u32[]{:S(2)}, u32[]{:S(2)}) collective-permute-start(bf16[192,768]{1,0:T(8,128)(2,1)S(1)} %get-tuple-element.160), channel_id=1, source_target_pairs={{0,4},{4,0},{8,12},{12,8},{16,20},{20,16},{24,28},{28,24},{1,5},{5... | collective-permute-start | bytes 884744 | tf_op jit(solution)/shard_map/ppermute | solution.py:435
  110.9 29.5 %collective-permute-start.14 = (bf16[112,768]{1,0:T(8,128)(2,1)S(1)}, bf16[112,768]{1,0:T(8,128)(2,1)S(1)}, u32[]{:S(2)}, u32[]{:S(2)}) collective-permute-start(bf16[112,768]{1,0:T(8,128)(2,1)S(1)} %get-tuple-element.155), channel_id=1, source_target_pairs={{0,16},{4,20},{8,24},{12,28},{16,0},{20,4},{24,8},{28,12},{1,17},{... | collective-permute-start | bytes 516104 | tf_op jit(solution)/shard_map/ppermute | solution.py:435
  119.1 11.7 %collective-permute-start.26 = (bf16[96,768]{1,0:T(8,128)(2,1)S(1)}, bf16[96,768]{1,0:T(8,128)(2,1)S(1)}, u32[]{:S(2)}, u32[]{:S(2)}) collective-permute-start(bf16[96,768]{1,0:T(8,128)(2,1)S(1)} %get-tuple-element.165), channel_id=1, source_target_pairs={{0,16},{4,20},{8,24},{12,28},{16,0},{20,4},{24,8},{28,12},{1,17},{... | collective-permute-start | bytes 442376 | tf_op jit(solution)/shard_map/ppermute | solution.py:435
  120.0 20.2 %collective-permute-start.21 = (bf16[96,768]{1,0:T(8,128)(2,1)S(1)}, bf16[96,768]{1,0:T(8,128)(2,1)S(1)}, u32[]{:S(2)}, u32[]{:S(2)}) collective-permute-start(bf16[96,768]{1,0:T(8,128)(2,1)S(1)} %get-tuple-element.162), channel_id=1, source_target_pairs={{0,16},{4,20},{8,24},{12,28},{16,0},{20,4},{24,8},{28,12},{1,17},{... | collective-permute-start | bytes 442376 | tf_op jit(solution)/shard_map/ppermute | solution.py:435
  123.0 44.0 %collective-permute-start.9 = (bf16[512,768]{1,0:T(8,128)(2,1)S(1)}, bf16[512,768]{1,0:T(8,128)(2,1)S(1)}, u32[]{:S(2)}, u32[]{:S(2)}) collective-permute-start(bf16[512,768]{1,0:T(8,128)(2,1)S(1)} %forward.2), channel_id=1, source_target_pairs={{0,2},{1,3},{2,0},{3,1},{4,6},{5,7},{6,4},{7,5},{8,10},{9,11},{10,... | collective-permute-start | bytes 2359304 | tf_op jit(solution)/shard_map/ppermute | solution.py:435
  130.8 15.8 %collective-permute-start.27 = (bf16[96,768]{1,0:T(8,128)(2,1)S(1)}, bf16[96,768]{1,0:T(8,128)(2,1)S(1)}, u32[]{:S(2)}, u32[]{:S(2)}) collective-permute-start(bf16[96,768]{1,0:T(8,128)(2,1)S(1)} %total.5.mine_ref), channel_id=1, source_target_pairs={{0,16},{4,20},{8,24},{12,28},{16,0},{20,4},{24,8},{28,12},{1,17},{... | collective-permute-start | bytes 442376 | tf_op jit(solution)/shard_map/ppermute | solution.py:435
  140.4 12.2 %collective-permute-start.17 = (bf16[96,768]{1,0:T(8,128)(2,1)S(1)}, bf16[96,768]{1,0:T(8,128)(2,1)S(1)}, u32[]{:S(2)}, u32[]{:S(2)}) collective-permute-start(bf16[96,768]{1,0:T(8,128)(2,1)S(1)} %get-tuple-element.157.mine_ref), channel_id=1, source_target_pairs={{0,16},{4,20},{8,24},{12,28},{16,0},{20,4},{24,8},{28,12},{1,17},{... | collective-permute-start | bytes 442376 | tf_op jit(solution)/shard_map/ppermute | solution.py:435
  147.1 11.8 %collective-permute-start.28 = (bf16[192,768]{1,0:T(8,128)(2,1)S(1)}, bf16[192,768]{1,0:T(8,128)(2,1)S(1)}, u32[]{:S(2)}, u32[]{:S(2)}) collective-permute-start(bf16[192,768]{1,0:T(8,128)(2,1)S(1)} %join.15.mine_ref), channel_id=1, source_target_pairs={{0,8},{4,12},{8,0},{12,4},{16,24},{20,28},{24,16},{28,20},{1,9},{5... | collective-permute-start | bytes 884744 | tf_op jit(solution)/shard_map/ppermute | solution.py:435
  150.4 10.2 %collective-permute-start.23 = (bf16[192,768]{1,0:T(8,128)(2,1)S(1)}, bf16[192,768]{1,0:T(8,128)(2,1)S(1)}, u32[]{:S(2)}, u32[]{:S(2)}) collective-permute-start(bf16[192,768]{1,0:T(8,128)(2,1)S(1)} %join.12.mine_ref), channel_id=1, source_target_pairs={{0,4},{4,0},{8,12},{12,8},{16,20},{20,16},{24,28},{28,24},{1,5},{5... | collective-permute-start | bytes 884744 | tf_op jit(solution)/shard_map/ppermute | solution.py:435
  153.2 12.1 %collective-permute-start.18 = (bf16[192,768]{1,0:T(8,128)(2,1)S(1)}, bf16[192,768]{1,0:T(8,128)(2,1)S(1)}, u32[]{:S(2)}, u32[]{:S(2)}) collective-permute-start(bf16[192,768]{1,0:T(8,128)(2,1)S(1)} %join.9.mine_ref), channel_id=1, source_target_pairs={{0,8},{4,12},{8,0},{12,4},{16,24},{20,28},{24,16},{28,20},{1,9},{5... | collective-permute-start | bytes 884744 | tf_op jit(solution)/shard_map/ppermute | solution.py:435
  153.4 36.2 %collective-permute-start.11 = (bf16[512,768]{1,0:T(8,128)(2,1)S(1)}, bf16[512,768]{1,0:T(8,128)(2,1)S(1)}, u32[]{:S(2)}, u32[]{:S(2)}) collective-permute-start(bf16[512,768]{1,0:T(8,128)(2,1)S(1)} %forward.3), channel_id=1, source_target_pairs={{0,2},{1,3},{2,0},{3,1},{4,6},{5,7},{6,4},{7,5},{8,10},{9,11},{10,... | collective-permute-start | bytes 2359304 | tf_op jit(solution)/shard_map/ppermute | solution.py:435
  159.5 16.3 %collective-permute-start.29 = (bf16[384,768]{1,0:T(8,128)(2,1)S(1)}, bf16[384,768]{1,0:T(8,128)(2,1)S(1)}, u32[]{:S(2)}, u32[]{:S(2)}) collective-permute-start(bf16[384,768]{1,0:T(8,128)(2,1)S(1)} %join.16.mine_ref), channel_id=1, source_target_pairs={{0,4},{4,0},{8,12},{12,8},{16,20},{20,16},{24,28},{28,24},{1,5},{5... | collective-permute-start | bytes 1769480 | tf_op jit(solution)/shard_map/ppermute | solution.py:435
  161.2 16.7 %collective-permute-start.24 = (bf16[384,768]{1,0:T(8,128)(2,1)S(1)}, bf16[384,768]{1,0:T(8,128)(2,1)S(1)}, u32[]{:S(2)}, u32[]{:S(2)}) collective-permute-start(bf16[384,768]{1,0:T(8,128)(2,1)S(1)} %join.13.mine_ref), channel_id=1, source_target_pairs={{0,8},{4,12},{8,0},{12,4},{16,24},{20,28},{24,16},{28,20},{1,9},{5... | collective-permute-start | bytes 1769480 | tf_op jit(solution)/shard_map/ppermute | solution.py:435
  165.8 21.5 %collective-permute-start.19 = (bf16[384,768]{1,0:T(8,128)(2,1)S(1)}, bf16[384,768]{1,0:T(8,128)(2,1)S(1)}, u32[]{:S(2)}, u32[]{:S(2)}) collective-permute-start(bf16[384,768]{1,0:T(8,128)(2,1)S(1)} %join.10.mine_ref), channel_id=1, source_target_pairs={{0,4},{4,0},{8,12},{12,8},{16,20},{20,16},{24,28},{28,24},{1,5},{5... | collective-permute-start | bytes 1769480 | tf_op jit(solution)/shard_map/ppermute | solution.py:435
  (24 other events, 141.6 us)

commit v2 on v1

--- a/solution.py
+++ b/solution.py
@@ -19,6 +19,15 @@
 SMEM = pl.BlockSpec(memory_space=pltpu.SMEM)
 MIB = 1 << 20
 UNIT = 500_000_000
+SEQUENCE = (
+    "attend_back", "p1", "qkv_end", "p2", "q1", "sides", "q2", "p3",
+    "forward", "p4", "q3", "p5", "q4", "vectors", "q5", "result",
+    "tokens_grad", "p6", "q6",
+)
+COSTS = {
+    "attend": 10, "attend_back": 14, "ff_back": 4, "front": 2, "p3": 150, "p4": 60,
+    "segments": 8,
+}
 ORDER_A, ORDER_B = (0, 1, 2), (1, 0, 2)
 
 
@@ -51,8 +60,24 @@
     )(*inputs)
 
 
+def cost(name, times=1):
+    return int(COSTS.get(name, 0.002) * times * UNIT)
+
+
 def after(token, *values):
     return lax.optimization_barrier((token, *values))[1:]
+
+
+class Chain:
+    def __init__(self, token):
+        self.token = token
+
+    def __call__(self, kernel, name, inputs, outs, hold, **options):
+        inputs = list(inputs)
+        (inputs[hold],) = after(self.token, inputs[hold])
+        outs = call(kernel, name, inputs, outs, **options)
+        self.token = outs[0]
+        return outs
 
 
 def row_of(ref):
@@ -143,8 +168,8 @@
         w1_in, w2_in, sums_in = refs[:3]
         refs = refs[3:]
     if last:
-        out_ref, back_ref, do_ref, k1_ref, s1_ref, k2_ref, s2_ref, sums_ref = refs[:8]
-        w1g_ref, w2g_ref, pay_ref = refs[8:]
+        out_ref, back_ref, do_ref, k1_ref, s1_ref, k2_ref, s2_ref = refs[:7]
+        w1g_ref, w2g_ref, pay_ref = refs[7:]
     else:
         out_ref, back_ref, do_ref, w1g_ref, w2g_ref, sums_ref = refs
     rows = dy_refs[0].shape[0]
@@ -168,18 +193,23 @@
         do_ref[:, r] = dot_nt(wd_ref[...], dy).astype(bf16)
         sums[0] = sums[0] + jnp.sum(du.astype(f32), axis=0, keepdims=True)
         sums[1] = sums[1] + jnp.sum(dy.astype(f32), axis=0, keepdims=True)
-    sums_ref[0:1, :] = sums[0]
-    sums_ref[1:2, :] = sums[1]
-    if last:
+    if not last:
+        sums_ref[0:1, :] = sums[0]
+        sums_ref[1:2, :] = sums[1]
+    else:
         pay_ref[...] = w2g_ref[...].astype(bf16)
-        halves(pay_ref, k2_ref, s2_ref, bit_of(place_ref, ORDER_A[0]))
+        half = pay_ref.shape[0] // 2
+        halves(pay_ref, k2_ref.at[0:half], s2_ref.at[0:half], bit_of(place_ref, ORDER_A[0]))
         du_sum = jnp.broadcast_to(sums[0], (8, sums[0].shape[1]))
         high = du_sum.astype(bf16)
         low = (du_sum - high.astype(f32)).astype(bf16)
-        sums_ref[3:4, :] = (dot_nt(high, w1_ref[...]) + dot_nt(low, w1_ref[...]))[0:1]
+        bias = (dot_nt(high, w1_ref[...]) + dot_nt(low, w1_ref[...]))[0:1]
         raw = w1g_ref[...]
         gain = jnp.sum(raw * w1_ref[...].astype(f32), axis=1, keepdims=True)
-        sums_ref[2:3, :] = jnp.broadcast_to(gain, (gain.shape[0], 128)).T[0:1, :]
+        gain = jnp.broadcast_to(gain, (gain.shape[0], 128)).T[0:1, :]
+        vectors = pair_rows([gain, bias, sums[1], sums[0]])
+        k2_ref[half:, :] = vectors
+        s2_ref[half:, :] = vectors
         pay_ref[...] = (raw * column_of(g2) + column_of(row_of(b2_ref)) * sums[0]).astype(bf16)
         halves(pay_ref, k1_ref, s1_ref, bit_of(place_ref, ORDER_B[0]))
 
@@ -260,31 +290,6 @@
             return ref[k * rows - at.start : (k + 1) * rows - at.start, :]
 
 
-def deal(k, total, keep0_ref, keep2_ref, send_ref):
-    rows = keep0_ref.shape[0]
-    if k == 0:
-        keep0_ref[...] = total
-    elif k == 2:
-        keep2_ref[...] = total
-    else:
-        send_ref[(k // 2) * rows : (k // 2 + 1) * rows, :] = total.astype(bf16)
-
-
-def attend_end_kernel(
-    o_ref, dy0_ref, dy1_ref, dy2_ref, dy3_ref, wd_ref, out0_ref, out1_ref, out2_ref,
-    keep0_ref, keep2_ref, send_ref, wdg_ref,
-):
-    rows = keep0_ref.shape[0]
-    wdg = None
-    for k, dy_ref in enumerate((dy0_ref, dy1_ref, dy2_ref, dy3_ref)):
-        o = o_ref[:, k * rows : (k + 1) * rows]
-        out = chunk((out0_ref, out1_ref, out2_ref), k, rows).astype(f32)
-        deal(k, out + dot_tn(o, wd_ref[...]), keep0_ref, keep2_ref, send_ref)
-        part = dot(o, dy_ref[...])
-        wdg = part if k == 0 else wdg + part
-    wdg_ref[...] = wdg.astype(bf16)
-
-
 def attend_back_kernel(
     place_ref, lo_ref, start_ref, qkv_ref, o_ref, do0_ref, do1_ref, do2_ref, lse_ref, cos_ref,
     sin_ref, dqkv_ref, do_ref, kn_ref, vn_ref, dk_ref, dv_ref,
@@ -361,8 +366,8 @@
 
 
 def qkv_end_kernel(
-    place_ref, dqkv_ref, xh0_ref, xh1_ref, xh2_ref, wq_ref, g1_ref, b1_ref, wdg_ref, sums_ref,
-    keep_ref, send_ref, pay_ref,
+    place_ref, dqkv_ref, xh0_ref, xh1_ref, xh2_ref, wq_ref, g1_ref, b1_ref,
+    o_ref, dy0_ref, dy1_ref, dy2_ref, dy3_ref, ka_ref, sa_ref, kb_ref, sb_ref, pay_ref,
 ):
     heads, seq = dqkv_ref.shape[0], dqkv_ref.shape[3]
     g1, b1 = row_of(g1_ref), row_of(b1_ref)
@@ -380,48 +385,60 @@
         weight = wq_ref[h * cols : (h + 1) * cols, :].astype(f32)
         gain = gain + jnp.sum(weight * raw, axis=0, keepdims=True)
         bias = bias + jnp.sum(weight * total, axis=0, keepdims=True)
-    pay_ref[heads * cols :, :] = wdg_ref[...]
+    dense = None
+    for at, ref in spans((dy0_ref, dy1_ref, dy2_ref, dy3_ref), 0):
+        part = dot(o_ref[:, at], ref[...])
+        dense = part if dense is None else dense + part
+    pay_ref[heads * cols :, :] = dense.astype(bf16)
     width = pay_ref.shape[1]
     zeros = jnp.zeros((1, width - heads * cols), f32)
-    vectors = pair_rows(
-        [
-            gain, bias, sums_ref[2:3, :], sums_ref[3:4, :], sums_ref[1:2, :], sums_ref[0:1, :],
-            jnp.concatenate(bq + [zeros], axis=1), jnp.zeros((1, width), f32),
-        ]
-    )
-    side = bit_of(place_ref, ORDER_A[0])
-    rows = pay_ref.shape[0] // 2
-    halves(pay_ref, keep_ref.at[0:rows], send_ref.at[0:rows], side)
-    keep_ref[rows:, :] = vectors
-    send_ref[rows:, :] = vectors
-
-
-def tokens_back_kernel(
-    dqkv_ref, back0_ref, back1_ref, back2_ref, wq_ref, g1_ref, keep0_ref, keep2_ref, send_ref
+    vectors = pair_rows([gain, bias, jnp.concatenate(bq + [zeros], axis=1), jnp.zeros((1, width), f32)])
+    rows = kb_ref.shape[0]
+    top, bottom = pay_ref.at[0 : 2 * rows], pay_ref.at[2 * rows : 4 * rows]
+    halves(top, ka_ref.at[0:rows], sa_ref.at[0:rows], bit_of(place_ref, ORDER_A[0]))
+    halves(bottom, kb_ref, sb_ref, bit_of(place_ref, ORDER_B[0]))
+    ka_ref[rows:, :] = vectors
+    sa_ref[rows:, :] = vectors
+
+
+def sides_kernel(
+    dqkv_ref, back0_ref, back1_ref, back2_ref, wq_ref, g1_ref,
+    o_ref, out0_ref, out1_ref, out2_ref, wd_ref,
+    outn_ref, outf_ref, backn_ref, backf_ref, send_ref,
 ):
-    rows = keep0_ref.shape[0]
+    rows = outn_ref.shape[0]
     g1 = row_of(g1_ref)
     cols = wq_ref.shape[0]
     for k in range(4):
-        grad = dqkv_ref[:, :, :, k * rows : (k + 1) * rows].reshape(cols, rows)
+        r = slice(k * rows, (k + 1) * rows)
         back = chunk((back0_ref, back1_ref, back2_ref), k, rows).astype(f32)
-        deal(k, back + dot_tn(grad, wq_ref[...]) * g1, keep0_ref, keep2_ref, send_ref)
-
-
-def forward_kernel(keep2_ref, got_ref, sent_ref):
-    rows = keep2_ref.shape[0]
-    sent_ref[...] = (keep2_ref[...] + got_ref[rows:, :].astype(f32)).astype(bf16)
-
-
-def result_kernel(x_ref, keep0_ref, got_ref, far_ref, bd_ref, c2_ref, out_ref):
+        back = back + dot_tn(dqkv_ref[:, :, :, r].reshape(cols, rows), wq_ref[...]) * g1
+        out = chunk((out0_ref, out1_ref, out2_ref), k, rows).astype(f32)
+        out = out + dot_tn(o_ref[:, r], wd_ref[...])
+        for value, keep, place in ((out, (outn_ref, outf_ref), 0), (back, (backn_ref, backf_ref), 2)):
+            if k % 2:
+                at = (place + k // 2) * rows
+                send_ref[at : at + rows, :] = value.astype(bf16)
+            else:
+                keep[k // 2][...] = value
+
+
+def forward_kernel(outf_ref, backf_ref, got_ref, sent_ref):
+    rows = outf_ref.shape[0]
+    for i, ref in enumerate((outf_ref, backf_ref)):
+        got = got_ref[(2 * i + 1) * rows : (2 * i + 2) * rows, :].astype(f32)
+        sent_ref[i * rows : (i + 1) * rows, :] = (ref[...] + got).astype(bf16)
+
+
+def result_kernel(x_ref, keep_ref, got_ref, far_ref, bd_ref, c2_ref, out_ref):
     rows = x_ref.shape[0]
-    summed = keep0_ref[...] + got_ref[:rows, :].astype(f32) + far_ref[...].astype(f32)
+    summed = keep_ref[...] + got_ref[:rows, :].astype(f32) + far_ref[:rows, :].astype(f32)
     out_ref[...] = (x_ref[...].astype(f32) + summed + (row_of(bd_ref) + row_of(c2_ref))).astype(bf16)
 
 
-def tokens_grad_kernel(x_ref, dy_ref, keep0_ref, got_ref, far_ref, out_ref):
+def tokens_grad_kernel(x_ref, dy_ref, keep_ref, got_ref, far_ref, out_ref):
     rows = x_ref.shape[0]
-    grad = keep0_ref[...] + got_ref[:rows, :].astype(f32) + far_ref[...].astype(f32)
+    grad = keep_ref[...] + got_ref[2 * rows : 3 * rows, :].astype(f32) + far_ref[rows:, :].astype(f32)
     x = x_ref[...].astype(f32)
     c = x - jnp.mean(x, axis=1, keepdims=True)
     inverse = lax.rsqrt(jnp.mean(c * c, axis=1, keepdims=True) + 1e-05)
@@ -436,69 +453,99 @@
 
 
 def unpair(rows):
-    return rows[0:8, :].astype(f32) + rows[8:16, :].astype(f32)
-
-
-def fold_kernel(place_ref, keep_ref, got_ref, next_ref, send_ref, *, bit, tail):
-    rows = (keep_ref.shape[0] - tail) // 2
-    side = bit_of(place_ref, bit)
-    for half, out_ref in ((side, next_ref), (1 - side, send_ref)):
-        at = pl.ds(pl.multiple_of(half * rows, 16), rows)
-        out_ref[0:rows, :] = (keep_ref[at, :].astype(f32) + got_ref[at, :].astype(f32)).astype(bf16)
-    if tail:
-        vectors = pair_rows([unpair(keep_ref[2 * rows :, :]) + unpair(got_ref[2 * rows :, :])])
-        next_ref[rows:, :] = vectors
-        send_ref[rows:, :] = vectors
-
-
-def total_kernel(keep_ref, got_ref, out_ref, *vector_ref):
+    rows = rows.astype(f32)
+    return rows[0:4, :] + rows[4:8, :]
+
+
+def half_sum(keep_ref, got_ref, half, rows):
+    at = pl.ds(pl.multiple_of(half * rows, 16), rows)
+    return (keep_ref[at, :].astype(f32) + got_ref[at, :].astype(f32)).astype(bf16)
+
+
+def vector_sum(keep_ref, got_ref):
+    return unpair(keep_ref[-8:, :]) + unpair(got_ref[-8:, :])
+
+
+def fold_kernel(place_ref, ka_ref, ga_ref, kb_ref, gb_ref, *outs):
+    for keep_ref, got_ref, next_ref, send_ref, order in (
+        (ka_ref, ga_ref, outs[0], outs[1], ORDER_A), (kb_ref, gb_ref, outs[2], outs[3], ORDER_B),
+    ):
+        rows = keep_ref.shape[0] // 16 * 8
+        side = bit_of(place_ref, order[1])
+        for half, out_ref in ((side, next_ref), (1 - side, send_ref)):
+            out_ref[0:rows, :] = half_sum(keep_ref, got_ref, half, rows)
+    vectors = pair_rows([vector_sum(ka_ref, ga_ref)])
+    outs[0][-8:, :] = vectors
+    outs[1][-8:, :] = vectors
+
+
+def far_fold_kernel(place_ref, ka_ref, ga_ref, kb_ref, gb_ref, next_ref, send_ref):
+    side = bit_of(place_ref, ORDER_A[2])
+    first = 0
+    for keep_ref, got_ref in ((ka_ref, ga_ref), (kb_ref, gb_ref)):
+        rows = keep_ref.shape[0] // 16 * 8
+        for half, out_ref in ((side, next_ref), (1 - side, send_ref)):
+            out_ref[first : first + rows, :] = half_sum(keep_ref, got_ref, half, rows)
+        first += rows
+    vectors = pair_rows([vector_sum(ka_ref, ga_ref)])
+    next_ref[first:, :] = vectors
+    send_ref[first:, :] = vectors
+
+
+def total_kernel(keep_ref, got_ref, out_ref, vector_ref):
     rows = out_ref.shape[0]
     total = keep_ref[0:rows, :].astype(f32) + got_ref[0:rows, :].astype(f32)
     out_ref[...] = total.astype(bf16)
-    if vector_ref:
-        vector_ref[0][...] = unpair(keep_ref[rows:, :]) + unpair(got_ref[rows:, :])
-
-
-def join_kernel(place_ref, mine_ref, got_ref, *out_refs, bit):
-    side = bit_of(place_ref, bit)
-    rows = mine_ref.shape[0]
-    out_ref = out_refs[-1]
-    for part, ref in ((side, mine_ref), (1 - side, got_ref)):
-        at = pl.ds(pl.multiple_of(part * rows, 16), rows)
-        out_ref[at, :] = ref[...].astype(out_ref.dtype)
-    if len(out_refs) > 1:
-        split = out_refs[0].shape[0]
-        out_refs[0][...] = out_ref[:split, :]
-        out_refs[1][...] = out_ref[split:, :]
+    vector_ref[...] = vector_sum(keep_ref, got_ref)
+
+
+def put_halves(out_ref, mine, got, side):
+    rows = mine.shape[0]
+    for half, value in ((side, mine), (1 - side, got)):
+        out_ref[pl.ds(pl.multiple_of(half * rows, 16), rows), :] = value.astype(out_ref.dtype)
+
+
+def far_join_kernel(place_ref, mine_ref, got_ref, a_ref, b_ref):
+    side = bit_of(place_ref, ORDER_A[2])
+    first = 0
+    for out_ref in (a_ref, b_ref):
+        r = slice(first, first + out_ref.shape[0] // 2)
+        put_halves(out_ref, mine_ref[r, :], got_ref[r, :], side)
+        first = r.stop
+
+
+def join_kernel(place_ref, ma_ref, ga_ref, mb_ref, gb_ref, a_ref, b_ref, *, step):
+    put_halves(a_ref, ma_ref[...], ga_ref[...], bit_of(place_ref, ORDER_A[step]))
+    put_halves(b_ref, mb_ref[...], gb_ref[...], bit_of(place_ref, ORDER_B[step]))
+
+
+def spread_kernel(place_ref, ma_ref, ga_ref, mb_ref, gb_ref, wq_ref, wd_ref):
+    rows = ma_ref.shape[0]
+    put_halves(wq_ref.at[0 : 2 * rows], ma_ref[...], ga_ref[...], bit_of(place_ref, ORDER_A[0]))
+    side = bit_of(place_ref, ORDER_B[0])
+    mine, got = mb_ref[...].astype(f32), gb_ref[...].astype(f32)
+    wq_ref[2 * rows :, :] = jnp.where(side == 0, mine, got)
+    wd_ref[...] = jnp.where(side == 0, got, mine)
+
+
+def vectors_kernel(near_ref, a_ref, c_ref, *out_refs):
+    for i in range(4):
+        out_refs[i][...] = near_ref[i : i + 1, :].reshape(-1)
+    out_refs[4][...] = a_ref[2:3, :].reshape(-1)
+    out_refs[5][...] = a_ref[2:3, :].reshape(-1)
+    out_refs[6][...] = a_ref[3:4, :].reshape(-1)
+    out_refs[7][...] = c_ref[2:3, : out_refs[7].shape[0]].reshape(-1)
 
 
 def dp_swap(value, dp, bit):
     return swap(value, "dp", dp, 1 << bit)
-
-
-def fold(place, keep, got, bit, tail=0):
-    rows = (keep.shape[0] - tail) // 2 + tail
-    return call(
-        partial(fold_kernel, bit=bit, tail=tail), "fold", [place, keep, got],
-        [like((rows, keep.shape[1]), bf16)] * 2, smem=(0,),
-    )
-
-
-def join(place, mine, got, bit, outs=None):
-    width = mine.shape[1]
-    if outs is None:
-        outs = [like((2 * mine.shape[0], width), bf16)]
-    scratch = [pltpu.VMEM((2 * mine.shape[0], width), f32)] if len(outs) > 1 else []
-    return call(
-        partial(join_kernel, bit=bit), "join", [place, mine, got], outs, scratch, smem=(0,),
-    )
 
 
 def rest_sum(value, dp):
     if dp == 8:
         return value
     groups = [[i + 8 * j for j in range(dp // 8)] for i in range(8)]
-    return lax.psum(value, "dp", axis_index_groups=groups)
+    return lax.psum(value.astype(f32), "dp", axis_index_groups=groups).astype(value.dtype)
 
 
 def rotary_tables(length):
@@ -529,7 +576,7 @@
     bq_column = qkv_bias.astype(f32)[:, None]
     start, lo = call(
         segments_kernel, "segments", [segment_ids, segment_ids],
-        [like((1, seq), i32), like((count,), i32)], smem=(1,), smem_out=(1,), flops=8 * UNIT,
+        [like((1, seq), i32), like((count,), i32)], smem=(1,), smem_out=(1,), flops=cost("segments"),
     )
     (x1,) = after(start, x1)
     hidden, inner = fc_in_weight.shape[1], dense_weight.shape[0]
@@ -542,7 +589,7 @@
              cosine, sine],
             [like((size, width), bf16), like((size, hidden), bf16), like((size, hidden), bf16),
              like((heads, 3, HEAD_DIM, size), bf16)],
-            smem=(0,), limit=16, flops=len(xs) * 2 * UNIT,
+            smem=(0,), limit=16, flops=cost("front", len(xs)),
         )
 
     def ff_back(dys, act, slope, xh, carry=(), last=False):
@@ -550,7 +597,7 @@
         outs = [like((size, width), bf16), like((size, width), bf16), like((inner, size), bf16)]
         full = [like((width, hidden), f32), like((hidden, width), f32)]
         sums = [like((8, width), f32)]
-        half = [like((width // 2, hidden), bf16)] * 2 + [like((hidden // 2, width), bf16)] * 2
+        half = [like((width // 2, hidden), bf16)] * 2 + [like((hidden // 2 + 8, width), bf16)] * 2
         scratch = [
             pltpu.VMEM((width, hidden), f32), pltpu.VMEM((hidden, width), f32),
             pltpu.VMEM((width, hidden), bf16),
@@ -559,8 +606,8 @@
             partial(ff_back_kernel, pieces=len(dys), carried=bool(carry), last=last), "ff_back",
             [place, *dys, act, slope, xh, gain2, bias2, fc_in_weight, fc_out_weight, dense_weight,
              *carry],
-            outs + (half if last else full) + sums, scratch if last else [],
-            smem=(0,), limit=22 if last else 16, flops=len(dys) * 4 * UNIT,
+            outs + (half if last else full + sums), scratch if last else [],
+            smem=(0,), limit=22 if last else 16, flops=cost("ff_back", len(dys)),
         )
 
     xh0, act0, slope0, qkv0 = front((x0, x1), 0)
@@ -575,116 +622,168 @@
         attend_kernel, "attend", [place, lo, start, qkv0, qkv1, qkv2],
         [like((heads, 3, HEAD_DIM, seq), bf16), like((inner, seq), bf16), like((heads, 1, seq), f32)],
         [pltpu.VMEM((heads, seq, HEAD_DIM), bf16)],
-        smem=(0, 1), limit=12, flops=10 * UNIT,
+        smem=(0, 1), limit=12, flops=cost("attend"),
     )
     dy3 = swap(*after(lse, dy2), "tensor", tp, 1)
     (dy2,) = after(lse, dy2)
     out1, back1, do1, *carry = ff_back((dy2,), act1, slope1, xh1, carry)
     (dy3,) = after(carry[2], dy3)
-    out2, back2, do2, k1, s1, k2, s2, sums = ff_back((dy3,), act2, slope2, xh2, carry, last=True)
-
-    got2 = dp_swap(s2, dp, ORDER_A[0])
-    got1 = dp_swap(s1, dp, ORDER_B[0])
-    (mixed_late,) = after(sums, mixed)
-    pair = 2 * rows
-    keep0, keep2, send, dense_grad = call(
-        attend_end_kernel, "attend_end",
-        [mixed_late, dy0, dy1, dy2, dy3, dense_weight, out0, out1, out2],
-        [like((rows, width), f32), like((rows, width), f32), like((pair, width), bf16),
-         like((inner, width), bf16)],
-        limit=12, flops=3 * UNIT,
-    )
-    got = swap(send, "tensor", tp, 1)
-    (mixed_late,) = after(dense_grad, mixed)
-    (dqkv,) = call(
-        attend_back_kernel, "attend_back",
-        [place, lo, start, qkv, mixed_late, do0, do1, do2, lse, cosine, sine],
-        [like((heads, 3, HEAD_DIM, seq), bf16)],
-        [
-            pltpu.VMEM((inner, seq), bf16),
-            pltpu.VMEM((heads, seq, HEAD_DIM), bf16), pltpu.VMEM((heads, seq, HEAD_DIM), bf16),
-            pltpu.VMEM((heads, HEAD_DIM, seq), f32), pltpu.VMEM((heads, HEAD_DIM, seq), f32),
-        ],
-        smem=(0, 1), limit=20, flops=14 * UNIT,
-    )
-    keep2, got, got1, got2 = after(dqkv, keep2, got, got1, got2)
-    far = swap(call(forward_kernel, "forward", [keep2, got], [like((rows, width), bf16)])[0],
-               "tensor", tp, 2)
-    k2, s2 = fold(place, k2, got2, ORDER_A[1])
-    got2 = dp_swap(s2, dp, ORDER_A[1])
-    k1, s1 = fold(place, k1, got1, ORDER_B[1])
-    got1 = dp_swap(s1, dp, ORDER_B[1])
-
-    tail = 16
-    (dqkv,) = after((k1, k2), dqkv)
-    keep_c, send_c = call(
-        qkv_end_kernel, "qkv_end",
-        [place, dqkv, xh0, xh1, xh2, wq, gain1, bias1, dense_grad, sums],
-        [like((width // 2 + tail, width), bf16)] * 2,
-        [pltpu.VMEM((wq.shape[0] + inner, width), bf16)],
-        smem=(0,), limit=12, flops=3 * UNIT,
-    )
-    got_c = dp_swap(send_c, dp, ORDER_A[0])
-    (dqkv,) = after(keep_c, dqkv)
-    keep0b, keep2b, sendb = call(
-        tokens_back_kernel, "tokens_back", [dqkv, back0, back1, back2, wq, gain1],
-        [like((rows, width), f32), like((rows, width), f32), like((pair, width), bf16)],
-        limit=8, flops=3 * UNIT,
-    )
-    gotb = swap(sendb, "tensor", tp, 1)
-
-    def finish_sum(keep, got, vector=0):
-        size = keep.shape[0] - vector
-        outs = [like((size, width), bf16)] + ([like((8, width), f32)] if vector else [])
-        total = call(total_kernel, "total", [keep, got], outs)
-        if dp == 8:
-            return total
-        return [rest_sum(total[0].astype(f32), dp).astype(bf16)] + [
-            rest_sum(t, dp) for t in total[1:]
-        ]
-
-    k2, s2 = fold(place, k2, got2, ORDER_A[2])
-    got2 = dp_swap(s2, dp, ORDER_A[2])
-    k1, s1 = fold(place, k1, got1, ORDER_B[2])
-    got1 = dp_swap(s1, dp, ORDER_B[2])
-    farb = swap(call(forward_kernel, "forward", [keep2b, gotb], [like((rows, width), bf16)])[0],
-                "tensor", tp, 2)
-    keep_c, send_c = fold(place, keep_c, got_c, ORDER_A[1], tail)
-    got_c = dp_swap(send_c, dp, ORDER_A[1])
-
-    (mine2,) = finish_sum(k2, got2)
-    (mine1,) = finish_sum(k1, got1)
-    for step in (2, 1):
-        mine2 = join(place, mine2, dp_swap(mine2, dp, ORDER_A[step]), ORDER_A[step])[0]
-        mine1 = join(place, mine1, dp_swap(mine1, dp, ORDER_B[step]), ORDER_B[step])[0]
-    w2_grad = join(place, mine2, dp_swap(mine2, dp, ORDER_A[0]), ORDER_A[0],
-                   [like((hidden, width), f32)])[0]
-    w1_grad = join(place, mine1, dp_swap(mine1, dp, ORDER_B[0]), ORDER_B[0],
-                   [like((width, hidden), f32)])[0]
-
-    keep_c, send_c = fold(place, keep_c, got_c, ORDER_A[2], tail)
-    got_c = dp_swap(send_c, dp, ORDER_A[2])
-    mine_c, vectors = finish_sum(keep_c, got_c, tail)
-    for step in (2, 1):
-        mine_c = join(place, mine_c, dp_swap(mine_c, dp, ORDER_A[step]), ORDER_A[step])[0]
-    wq_grad, wd_grad = join(
-        place, mine_c, dp_swap(mine_c, dp, ORDER_A[0]), ORDER_A[0],
-        [like((wq.shape[0], width), f32), like((inner, width), f32)],
-    )
-    near = vectors + swap(vectors, "tensor", tp, 1)
-    near = near + swap(near, "tensor", tp, 2)
-    result = call(
-        result_kernel, "result", [x0, keep0, got, far, dense_bias, fc_out_bias],
-        [like((rows, width), bf16)],
-    )[0]
-    input_grad = call(
-        tokens_grad_kernel, "tokens_grad", [x0, dy0, keep0b, gotb, farb],
-        [like((rows, width), f32)],
-    )[0]
+    out2, back2, do2, k1, s1, k2, s2 = ff_back((dy3,), act2, slope2, xh2, carry, last=True)
+
+    run = Chain(do2)
+    tail = 8
+    keep, got, vectors, made = {}, {}, {}, {}
+
+    def part(count):
+        return like((count, width), bf16)
+
+    def send(name, a, b, step):
+        got[name] = [dp_swap(a, dp, ORDER_A[step]), dp_swap(b, dp, ORDER_B[step])]
+
+    def parts(name):
+        (ka, kb), (ga, gb) = keep[name], got[name]
+        return [place, ka, ga, kb, gb]
+
+    def fold(name):
+        na, nb = keep[name][0].shape[0] // 16 * 8, keep[name][1].shape[0] // 2
+        ka, sa, kb, sb = run(
+            fold_kernel, "fold", parts(name), [part(na + tail)] * 2 + [part(nb)] * 2,
+            hold=2, smem=(0,), flops=cost(f"{name}1"),
+        )
+        keep[name] = ka, kb
+        send(name, sa, sb, 1)
+
+    def far_fold(name):
+        count = sum(k.shape[0] // 16 * 8 for k in keep[name]) + tail
+        keep[name], sent = run(
+            far_fold_kernel, "far_fold", parts(name), [part(count)] * 2, hold=2, smem=(0,),
+            flops=cost(f"{name}2"),
+        )
+        got[name] = dp_swap(sent, dp, ORDER_A[2])
+
+    def complete(name):
+        total, vector = run(
+            total_kernel, "total", [keep[name], got[name]],
+            [part(keep[name].shape[0] - tail), like((4, width), f32)], hold=1,
+            flops=cost(f"{name}3"),
+        )
+        keep[name], vectors[name] = rest_sum(total, dp), rest_sum(vector, dp)
+        got[name] = dp_swap(keep[name], dp, ORDER_A[2])
+        if len(vectors) == 2:
+            near = jnp.concatenate([vectors["q"][:2], vectors["p"][:2]], axis=0)
+            near = near + swap(near, "tensor", tp, 1)
+            made["near"] = near + swap(near, "tensor", tp, 2)
+
+    def far_join(name):
+        keep[name] = run(
+            far_join_kernel, "far_join", [place, keep[name], got[name]],
+            [part(keep[name].shape[0])] * 2, hold=2, smem=(0,), flops=cost(f"{name}4"),
+        )
+        send(name, *keep[name], 1)
+
+    def join(name):
+        keep[name] = run(
+            partial(join_kernel, step=1), "join", parts(name),
+            [part(2 * k.shape[0]) for k in keep[name]], hold=2, smem=(0,), flops=cost(f"{name}5"),
+        )
+        send(name, *keep[name], 0)
+
+    def finish_p():
+        made["p"] = run(
+            partial(join_kernel, step=0), "grads", parts("p"),
+            [like((hidden, width), f32), like((width, hidden), f32)], hold=2, smem=(0,),
+            flops=cost("p6"),
+        )
+
+    def finish_q():
+        made["q"] = run(
+            spread_kernel, "spread", parts("q"),
+            [like((wq.shape[0], width), f32), like((inner, width), f32)], hold=2, smem=(0,),
+            flops=cost("q6"),
+        )
+
+    def attend_back():
+        (made["dqkv"],) = run(
+            attend_back_kernel, "attend_back",
+            [place, lo, start, qkv, mixed, do0, do1, do2, lse, cosine, sine],
+            [like((heads, 3, HEAD_DIM, seq), bf16)], hold=4,
+            scratch=[
+                pltpu.VMEM((inner, seq), bf16),
+                pltpu.VMEM((heads, seq, HEAD_DIM), bf16), pltpu.VMEM((heads, seq, HEAD_DIM), bf16),
+                pltpu.VMEM((heads, HEAD_DIM, seq), f32), pltpu.VMEM((heads, HEAD_DIM, seq), f32),
+            ],
+            smem=(0, 1), limit=20, flops=cost("attend_back"),
+        )
+
+    def qkv_end():
+        count = (wq.shape[0] + inner) // 4
+        ka, sa, kb, sb = run(
+            qkv_end_kernel, "qkv_end",
+            [place, made["dqkv"], xh0, xh1, xh2, wq, gain1, bias1, mixed, dy0, dy1, dy2, dy3],
+            [part(count + tail)] * 2 + [part(count)] * 2, hold=1,
+            scratch=[pltpu.VMEM((4 * count, width), bf16)], smem=(0,), limit=12,
+            flops=cost("qkv_end"),
+        )
+        keep["q"] = ka, kb
+        send("q", sa, sb, 0)
+
+    def sides():
+        *made["sides"], sent = run(
+            sides_kernel, "sides",
+            [made["dqkv"], back0, back1, back2, wq, gain1, mixed, out0, out1, out2, dense_weight],
+            [like((rows, width), f32)] * 4 + [like((4 * rows, width), bf16)],
+            hold=0, limit=12, flops=cost("sides"),
+        )
+        made["crossed"] = swap(sent, "tensor", tp, 1)
+
+    def forward():
+        _, far_out, _, far_back = made["sides"]
+        (sent,) = run(
+            forward_kernel, "forward", [far_out, far_back, made["crossed"]],
+            [like((2 * rows, width), bf16)], hold=2, flops=cost("forward"),
+        )
+        made["far"] = swap(sent, "tensor", tp, 2)
+
+    def result():
+        (made["result"],) = run(
+            result_kernel, "result",
+            [x0, made["sides"][0], made["crossed"], made["far"], dense_bias, fc_out_bias],
+            [like((rows, width), bf16)], hold=3, flops=cost("result"),
+        )
+
+    def tokens_grad():
+        (made["tokens_grad"],) = run(
+            tokens_grad_kernel, "tokens_grad",
+            [x0, dy0, made["sides"][2], made["crossed"], made["far"]],
+            [like((rows, width), f32)], hold=4, flops=cost("tokens_grad"),
+        )
+
+    def finish_vectors():
+        flat = like((width,), f32)
+        made["vectors"] = run(
+            vectors_kernel, "vectors", [made["near"], vectors["p"], vectors["q"]],
+            [flat] * 7 + [like((wq.shape[0],), f32)], hold=0, flops=cost("vectors"),
+        )
+
+    steps = {
+        "attend_back": attend_back, "qkv_end": qkv_end, "sides": sides, "forward": forward,
+        "result": result, "tokens_grad": tokens_grad, "vectors": finish_vectors,
+        "p6": finish_p, "q6": finish_q,
+    }
+    for name in "pq":
+        for step, act in enumerate((fold, far_fold, complete, far_join, join)):
+            steps[f"{name}{step + 1}"] = partial(act, name)
+    keep["p"] = k2, k1
+    send("p", s2, s1, 0)
+    for step in SEQUENCE:
+        steps[step]()
+    *vectors, bq_grad = made["vectors"]
+    (w2_grad, w1_grad), (wq_grad, wd_grad) = made["p"], made["q"]
+    result, input_grad = made["result"], made["tokens_grad"]
+    gain1_grad, bias1_grad, gain2_grad, bias2_grad, dense_sum, out_sum, du_sum = vectors
     return (
-        result[None], input_grad[None], near[0], near[1], near[2], near[3],
-        wq_grad.T, vectors[6, : wq.shape[0]], wd_grad, vectors[4],
-        w1_grad, vectors[5], w2_grad, vectors[4],
+        result[None], input_grad[None], gain1_grad, bias1_grad, gain2_grad, bias2_grad,
+        wq_grad.T, bq_grad, wd_grad, dense_sum, w1_grad, du_sum, w2_grad, out_sum,
     )
 
 

time: 193 us -> 165 us (0.85)
  waiting for transfers between devices: 72.4 us -> 51.9 us
  starting transfers between devices: 30.3 us -> 27.5 us
  Pallas kernels: 85.3 us -> 82.8 us
  local copies, waits for them, and re-layouts: 3.34 us -> 0.91 us
    ppermute x30, waiting for transfers between devices: 72.4 us -> 51.9 us  [swap(): return lax.ppermute(value, axis, [(i, i ^ distance) for i in range(size)])]
    ppermute x30, starting transfers between devices: 30.3 us -> 27.5 us  [swap(): return lax.ppermute(value, axis, [(i, i ^ distance) for i in range(size)])]
    pallas_call x34 -> x27, Pallas kernels: 85.3 us -> 82.8 us  [call(): pl.pallas_call(kernel, out_shape=tuple(outs), in_specs=[SMEM if i in smem...]
  transfers between devices with their start and end apart: 30 -> 30, of which waited for: 15 -> 14; matrix products, arithmetic and copies ran while one was open for 1% -> 0% of each run, Pallas kernels for 35% -> 45%
where the time goes in v2:
time: 165 us; the launch traced here: 164 us
  Pallas kernels  82.8 us (50%)
  waiting for transfers between devices  51.9 us (31%)
  starting transfers between devices  27.5 us (17%)
    pallas_call x27, Pallas kernels, call(): pl.pallas_call(kernel, out_shape=tuple(outs), in_specs=[SMEM if i in smem...  82.8 us
    ppermute x30, waiting for transfers between devices, swap(): return lax.ppermute(value, axis, [(i, i ^ distance) for i in range(size)])  51.9 us
    ppermute x30, starting transfers between devices, swap(): return lax.ppermute(value, axis, [(i, i ^ distance) for i in range(size)])  27.5 us
  transfers between devices with their start and end apart: 30, of which 14 were waited for; matrix products, arithmetic and copies ran while one was open for 0% of the time, Pallas kernels for 45%

profile of v2, /device:TPU:0, one launch (start us, length us, event | category | flops | bytes accessed | tf_op | source)
XLA Modules:
  0.0 164.3 jit_solution(14496703758220631627)
XLA Ops:
  1.4 2.9 %collective-permute-start.2 = (bf16[512,768]{1,0:T(8,128)(2,1)}, bf16[512,768]{1,0:T(8,128)(2,1)}, u32[]{:S(2)}, u32[]{:S(2)}) collective-permute-start(bf16[512,768]{1,0:T(8,128)(2,1)} %bitcast.14), channel_id=1, source_target_pairs={{0,2},{1,3},{2,0},{3,1},{4,6},{5,7},{6,4},{7,5},{8,10},{9,11},{10,... | collective-permute-start | bytes 2359304 | tf_op jit(solution)/shard_map/ppermute | solution.py:452
  6.9 5.1 %front.3 = (bf16[1024,768]{1,0:T(8,128)(2,1)S(1)}, bf16[1024,768]{1,0:T(8,128)(2,1)S(1)}, bf16[1024,768]{1,0:T(8,128)(2,1)S(1)}, bf16[3,3,64,1024]{3,2,1,0:T(8,128)(2,1)S(1)}) custom-call(s32[2]{0:T(128)S(1)} %pad_add_fusion.place_ref, bf16[512,768]{1,0:T(8,128)(2,1)S(1)} %bitcast.15, bf16[512,768]{1,0:T(8,128)(2,1)} %collective-permute-done.refs_1_, ...), custom_call_target="tpu_custom_call" | custom-call | flops 2000000000 | bytes 1000 | tf_op jit(solution)/shard_map/front/pallas_call | solution.py:51
  12.0 8.0 %ff_back.3 = (bf16[1024,768]{1,0:T(8,128)(2,1)S(1)}, bf16[1024,768]{1,0:T(8,128)(2,1)S(1)}, bf16[192,1024]{1,0:T(8,128)(2,1)S(1)}, f32[768,768]{1,0:T(8,128)S(1)...) custom-call(s32[2]{0:T(128)S(1)} %pad_add_fusion.place_ref, bf16[512,768]{1,0:T(8,128)(2,1)S(1)} %bitcast.19, ...), custom_call_target="tpu_custom_call" | custom-call | flops 4000000000 | bytes 1000 | tf_op jit(solution)/shard_map/ff_back/pallas_call | solution.py:51
  20.0 2.4 %collective-permute-done.2.refs_0_ = bf16[512,768]{1,0:T(8,128)(2,1)} collective-permute-done((bf16[512,768]{1,0:T(8,128)(2,1)}, bf16[512,768]{1,0:T(8,128)(2,1)}, u32[]{:S(2)}, u32[]{:S(2)}) %collective-permute-start.2) | collective-permute-done | bytes 786464 | tf_op jit(solution)/shard_map/ppermute | solution.py:452
  24.1 3.0 %front.4 = (bf16[512,768]{1,0:T(8,128)(2,1)S(1)}, bf16[512,768]{1,0:T(8,128)(2,1)S(1)}, bf16[512,768]{1,0:T(8,128)(2,1)S(1)}, bf16[3,3,64,512]{3,2,1,0:T(8,128)(2,1)S(1)}) custom-call(s32[2]{0:T(128)S(1)} %pad_add_fusion.place_ref, bf16[512,768]{1,0:T(8,128)(2,1)} %collective-permute-done.2.refs_0_, bf16[768]{0:T(1024)(128)(2,1)S(1)} %copy-done.6, ...), custom_call_target="tpu_custom_call" | custom-call | flops 1000000000 | bytes 1000 | tf_op jit(solution)/shard_map/front/pallas_call | solution.py:51
  27.1 2.6 %front.5 = (bf16[512,768]{1,0:T(8,128)(2,1)S(1)}, bf16[512,768]{1,0:T(8,128)(2,1)S(1)}, bf16[512,768]{1,0:T(8,128)(2,1)S(1)}, bf16[3,3,64,512]{3,2,1,0:T(8,128)(2,1)S(1)}) custom-call(s32[2]{0:T(128)S(1)} %pad_add_fusion.place_ref, bf16[512,768]{1,0:T(8,128)(2,1)S(1)} %collective-permute-done.3.refs_0_, bf16[768]{0:T(1024)(128)(2,1)S(1)} %copy-done.6, ...), custom_call_target="tpu_custom_call" | custom-call | flops 1000000000 | bytes 1000 | tf_op jit(solution)/shard_map/front/pallas_call | solution.py:51
  29.7 13.3 %attend.1 = (bf16[3,3,64,2048]{3,2,1,0:T(8,128)(2,1)S(1)}, bf16[192,2048]{1,0:T(8,128)(2,1)S(1)}, f32[3,1,2048]{2,1,0:T(1,128)S(1)}) custom-call(s32[2]{0:T(128)S(1)} %pad_add_fusion.place_ref, s32[8]{0:T(128)S(1)} %get-tuple-element.120.lo_ref, s32[1,2048]{1,0:T(1,128)S(1)} %get-tuple-element.121.start_ref, ...), custom_call_target="tpu_custom_call" | custom-call | flops 5000000000 | bytes 1000 | tf_op jit(solution)/shard_map/attend/pallas_call | solution.py:51
  43.3 4.1 %ff_back.4 = (bf16[512,768]{1,0:T(8,128)(2,1)S(1)}, bf16[512,768]{1,0:T(8,128)(2,1)S(1)}, bf16[192,512]{1,0:T(8,128)(2,1)S(1)}, f32[768,768]{1,0:T(8,128)S(1)}, ...) custom-call(s32[2]{0:T(128)S(1)} %pad_add_fusion.place_ref, bf16[512,768]{1,0:T(8,128)(2,1)S(1)} %collective-permute-done.4.refs_0_.dy2_ref, ...), custom_call_target="tpu_custom_call" | custom-call | flops 2000000000 | bytes 1000 | tf_op jit(solution)/shard_map/ff_back/pallas_call | solution.py:51
  47.4 5.5 %ff_back.5 = (bf16[512,768]{1,0:T(8,128)(2,1)S(1)}, bf16[512,768]{1,0:T(8,128)(2,1)S(1)}, bf16[192,512]{1,0:T(8,128)(2,1)S(1)}, bf16[384,768]{1,0:T(8,128)(2,1)S...) custom-call(s32[2]{0:T(128)S(1)} %pad_add_fusion.place_ref, ...), custom_call_target="tpu_custom_call" | custom-call | flops 2000000000 | bytes 1000 | tf_op jit(solution)/shard_map/ff_back/pallas_call | solution.py:51
  53.8 2.2 %collective-permute-start.6 = (bf16[392,768]{1,0:T(8,128)(2,1)S(1)}, bf16[392,768]{1,0:T(8,128)(2,1)S(1)}, u32[]{:S(2)}, u32[]{:S(2)}) collective-permute-start(bf16[392,768]{1,0:T(8,128)(2,1)S(1)} %get-tuple-element.154), channel_id=1, source_target_pairs={{0,4},{4,0},{8,12},{12,8},{16,20},{20,16},{24,28},{28,24},{1,5},{5... | collective-permute-start | bytes 1806344 | tf_op jit(solution)/shard_map/ppermute | solution.py:452
  56.1 16.9 %attend_back.1.dqkv_ref = bf16[3,3,64,2048]{3,2,1,0:T(8,128)(2,1)S(1)} custom-call(s32[2]{0:T(128)S(1)} %pad_add_fusion.place_ref, s32[8]{0:T(128)S(1)} %get-tuple-element.120.lo_ref, s32[1,2048]{1,0:T(1,128)S(1)} %get-tuple-element.121.start_ref, bf16[3,3,64,2048]{3,2,1,0:T(8,128)(2,1)S(1)} %get-tuple-element.148.qkv_ref, ...), custom_call_target="tpu_custom_call" | custom-call | flops 7000000000 | bytes 1000 | tf_op jit(solution)/shard_map/attend_back/pallas_call | solution.py:51
  74.8 4.4 %qkv_end.1 = (bf16[200,768]{1,0:T(8,128)(2,1)S(1)}, bf16[200,768]{1,0:T(8,128)(2,1)S(1)}, bf16[192,768]{1,0:T(8,128)(2,1)S(1)}, bf16[192,768]{1,0:T(8,128)(2,1)S(1)}) custom-call(s32[2]{0:T(128)S(1)} %pad_add_fusion.place_ref, bf16[3,3,64,2048]{3,2,1,0:T(8,128)(2,1)S(1)} %attend_back.1.dqkv_ref, bf16[1024,768]{1,0:T(8,128)(2,1)S(1)} %get-tuple-element.127.refs_4_.xh0_ref, ...), custom_call_target="tpu_custom_call" | custom-call | flops 1000000 | bytes 1000 | tf_op jit(solution)/shard_map/qkv_end/pallas_call | solution.py:51
  86.4 2.8 %collective-permute-done.10.ga_ref = bf16[200,768]{1,0:T(8,128)(2,1)S(1)} collective-permute-done((bf16[200,768]{1,0:T(8,128)(2,1)S(1)}, bf16[200,768]{1,0:T(8,128)(2,1)S(1)}, u32[]{:S(2)}, u32[]{:S(2)}) %collective-permute-start.10) | collective-permute-done | bytes 307232 | tf_op jit(solution)/shard_map/ppermute | solution.py:452
  89.2 4.1 %collective-permute-done.11.gb_ref = bf16[192,768]{1,0:T(8,128)(2,1)S(1)} collective-permute-done((bf16[192,768]{1,0:T(8,128)(2,1)S(1)}, bf16[192,768]{1,0:T(8,128)(2,1)S(1)}, u32[]{:S(2)}, u32[]{:S(2)}) %collective-permute-start.11) | collective-permute-done | bytes 294944 | tf_op jit(solution)/shard_map/ppermute | solution.py:452
  94.5 3.6 %sides.1 = (f32[512,768]{1,0:T(8,128)S(1)}, f32[512,768]{1,0:T(8,128)S(1)}, f32[512,768]{1,0:T(8,128)S(1)}, f32[512,768]{1,0:T(8,128)S(1)}, bf16[2048,768]{1,0:T(8,128)(2,1)S(1)}) custom-call(bf16[3,3,64,2048]{3,2,1,0:T(8,128)(2,1)S(1)} %attend_back.1.dqkv_ref, bf16[1024,768]{1,0:T(8,128)(2,1)S(1)} %get-tuple-element.172.back0_ref, ...), custom_call_target="tpu_custom_call" | custom-call | flops 1000000 | bytes 1000 | tf_op jit(solution)/shard_map/sides/pallas_call | solution.py:51
  98.1 3.2 %collective-permute-done.13.ga_ref = bf16[104,768]{1,0:T(8,128)(2,1)S(1)} collective-permute-done((bf16[104,768]{1,0:T(8,128)(2,1)S(1)}, bf16[104,768]{1,0:T(8,128)(2,1)S(1)}, u32[]{:S(2)}, u32[]{:S(2)}) %collective-permute-start.13) | collective-permute-done | bytes 159776 | tf_op jit(solution)/shard_map/ppermute | solution.py:452
  105.5 11.5 %collective-permute-done.16.got_ref = bf16[192,768]{1,0:T(8,128)(2,1)S(1)} collective-permute-done((bf16[192,768]{1,0:T(8,128)(2,1)S(1)}, bf16[192,768]{1,0:T(8,128)(2,1)S(1)}, u32[]{:S(2)}, u32[]{:S(2)}) %collective-permute-start.16) | collective-permute-done | bytes 294944 | tf_op jit(solution)/shard_map/ppermute | solution.py:452
  118.0 2.3 %collective-permute-start.17 = (bf16[104,768]{1,0:T(8,128)(2,1)S(1)}, bf16[104,768]{1,0:T(8,128)(2,1)S(1)}, u32[]{:S(2)}, u32[]{:S(2)}) collective-permute-start(bf16[104,768]{1,0:T(8,128)(2,1)S(1)} %get-tuple-element.193), channel_id=1, source_target_pairs={{0,16},{4,20},{8,24},{12,28},{16,0},{20,4},{24,8},{28,12},{1,17},{... | collective-permute-start | bytes 479240 | tf_op jit(solution)/shard_map/ppermute | solution.py:452
  120.3 7.5 %collective-permute-done.17.got_ref = bf16[104,768]{1,0:T(8,128)(2,1)S(1)} collective-permute-done((bf16[104,768]{1,0:T(8,128)(2,1)S(1)}, bf16[104,768]{1,0:T(8,128)(2,1)S(1)}, u32[]{:S(2)}, u32[]{:S(2)}) %collective-permute-start.17) | collective-permute-done | bytes 159776 | tf_op jit(solution)/shard_map/ppermute | solution.py:452
  127.9 3.4 %collective-permute-start.20 = (bf16[96,768]{1,0:T(8,128)(2,1)S(1)}, bf16[96,768]{1,0:T(8,128)(2,1)S(1)}, u32[]{:S(2)}, u32[]{:S(2)}) collective-permute-start(bf16[96,768]{1,0:T(8,128)(2,1)S(1)} %get-tuple-element.195.mine_ref), channel_id=1, source_target_pairs={{0,16},{4,20},{8,24},{12,28},{16,0},{20,4},{24,8},{28,12},{1,17},{... | collective-permute-start | bytes 442376 | tf_op jit(solution)/shard_map/ppermute | solution.py:452
  134.1 5.0 %collective-permute-done.20.got_ref = bf16[96,768]{1,0:T(8,128)(2,1)S(1)} collective-permute-done((bf16[96,768]{1,0:T(8,128)(2,1)S(1)}, bf16[96,768]{1,0:T(8,128)(2,1)S(1)}, u32[]{:S(2)}, u32[]{:S(2)}) %collective-permute-start.20) | collective-permute-done | bytes 147488 | tf_op jit(solution)/shard_map/ppermute | solution.py:452
  143.2 10.1 %collective-permute-done.23.ga_ref = bf16[96,768]{1,0:T(8,128)(2,1)S(1)} collective-permute-done((bf16[96,768]{1,0:T(8,128)(2,1)S(1)}, bf16[96,768]{1,0:T(8,128)(2,1)S(1)}, u32[]{:S(2)}, u32[]{:S(2)}) %collective-permute-start.23) | collective-permute-done | bytes 147488 | tf_op jit(solution)/shard_map/ppermute | solution.py:452
  155.4 2.3 %tokens_grad.1 = f32[512,768]{1,0:T(8,128)} custom-call(bf16[512,768]{1,0:T(8,128)(2,1)S(1)} %bitcast.17, bf16[512,768]{1,0:T(8,128)(2,1)S(1)} %bitcast.22, f32[512,768]{1,0:T(8,128)S(1)} %get-tuple-element.209.keep_ref, bf16[2048,768]{1,0:T(8,128)(2,1)S(1)} %collective-permute-done.12.got_ref, bf16[1024,768]{1,0:T(8,128)(2,1)S(1)} %collective-permute-done.25.far_ref), custom_call_target="tpu_custom_call" | custom-call | flops 1000000 | bytes 1000 | tf_op jit(solution)/shard_map/tokens_grad/pallas_call | solution.py:51
  157.8 3.0 %grads.1 = (f32[768,768]{1,0:T(8,128)}, f32[768,768]{1,0:T(8,128)}) custom-call(s32[2]{0:T(128)S(1)} %pad_add_fusion.place_ref, bf16[384,768]{1,0:T(8,128)(2,1)S(1)} %get-tuple-element.198.ma_ref, bf16[384,768]{1,0:T(8,128)(2,1)S(1)} %collective-permute-done.26.ga_ref, bf16[384,768]{1,0:T(8,128)(2,1)S(1)} %get-tuple-element.215.mb_ref, ...), custom_call_target="tpu_custom_call" | custom-call | flops 1000000 | bytes 1000 | tf_op jit(solution)/shard_map/grads/pallas_call | solution.py:51
  (104 shorter events, 34.2 us)
Async XLA Ops:
  1.2 10.7 %collective-permute-start.1 = (bf16[512,768]{1,0:T(8,128)(2,1)}, bf16[512,768]{1,0:T(8,128)(2,1)}, u32[]{:S(2)}, u32[]{:S(2)}) collective-permute-start(bf16[512,768]{1,0:T(8,128)(2,1)} %bitcast.18), channel_id=1, source_target_pairs={{0,1},{1,0},{2,3},{3,2},{4,5},{5,4},{6,7},{7,6},{8,9},{9,8},{10,11... | collective-permute-start | bytes 2359304 | tf_op jit(solution)/shard_map/ppermute | solution.py:452
  1.4 21.0 %collective-permute-start.2 = (bf16[512,768]{1,0:T(8,128)(2,1)}, bf16[512,768]{1,0:T(8,128)(2,1)}, u32[]{:S(2)}, u32[]{:S(2)}) collective-permute-start(bf16[512,768]{1,0:T(8,128)(2,1)} %bitcast.14), channel_id=1, source_target_pairs={{0,2},{1,3},{2,0},{3,1},{4,6},{5,7},{6,4},{7,5},{8,10},{9,11},{10,... | collective-permute-start | bytes 2359304 | tf_op jit(solution)/shard_map/ppermute | solution.py:452
  22.4 20.6 %collective-permute-start.4 = (bf16[512,768]{1,0:T(8,128)(2,1)S(1)}, bf16[512,768]{1,0:T(8,128)(2,1)S(1)}, u32[]{:S(2)}, u32[]{:S(2)}) collective-permute-start(bf16[512,768]{1,0:T(8,128)(2,1)S(1)} %bitcast.20), channel_id=1, source_target_pairs={{0,2},{1,3},{2,0},{3,1},{4,6},{5,7},{6,4},{7,5},{8,10},{9,11},{10,... | collective-permute-start | bytes 2359304 | tf_op jit(solution)/shard_map/ppermute | solution.py:452
  52.9 20.1 %collective-permute-start.7 = (bf16[384,768]{1,0:T(8,128)(2,1)S(1)}, bf16[384,768]{1,0:T(8,128)(2,1)S(1)}, u32[]{:S(2)}, u32[]{:S(2)}) collective-permute-start(bf16[384,768]{1,0:T(8,128)(2,1)S(1)} %get-tuple-element.157), channel_id=1, source_target_pairs={{0,8},{4,12},{8,0},{12,4},{16,24},{20,28},{24,16},{28,20},{1,9},{5... | collective-permute-start | bytes 1769480 | tf_op jit(solution)/shard_map/ppermute | solution.py:452
  53.8 19.1 %collective-permute-start.6 = (bf16[392,768]{1,0:T(8,128)(2,1)S(1)}, bf16[392,768]{1,0:T(8,128)(2,1)S(1)}, u32[]{:S(2)}, u32[]{:S(2)}) collective-permute-start(bf16[392,768]{1,0:T(8,128)(2,1)S(1)} %get-tuple-element.154), channel_id=1, source_target_pairs={{0,4},{4,0},{8,12},{12,8},{16,20},{20,16},{24,28},{28,24},{1,5},{5... | collective-permute-start | bytes 1806344 | tf_op jit(solution)/shard_map/ppermute | solution.py:452
  73.8 9.6 %collective-permute-start.8 = (bf16[200,768]{1,0:T(8,128)(2,1)S(1)}, bf16[200,768]{1,0:T(8,128)(2,1)S(1)}, u32[]{:S(2)}, u32[]{:S(2)}) collective-permute-start(bf16[200,768]{1,0:T(8,128)(2,1)S(1)} %get-tuple-element.161), channel_id=1, source_target_pairs={{0,8},{4,12},{8,0},{12,4},{16,24},{20,28},{24,16},{28,20},{1,9},{5... | collective-permute-start | bytes 921608 | tf_op jit(solution)/shard_map/ppermute | solution.py:452
  73.9 9.9 %collective-permute-start.9 = (bf16[192,768]{1,0:T(8,128)(2,1)S(1)}, bf16[192,768]{1,0:T(8,128)(2,1)S(1)}, u32[]{:S(2)}, u32[]{:S(2)}) collective-permute-start(bf16[192,768]{1,0:T(8,128)(2,1)S(1)} %get-tuple-element.164), channel_id=1, source_target_pairs={{0,4},{4,0},{8,12},{12,8},{16,20},{20,16},{24,28},{28,24},{1,5},{5... | collective-permute-start | bytes 884744 | tf_op jit(solution)/shard_map/ppermute | solution.py:452
  79.2 10.0 %collective-permute-start.10 = (bf16[200,768]{1,0:T(8,128)(2,1)S(1)}, bf16[200,768]{1,0:T(8,128)(2,1)S(1)}, u32[]{:S(2)}, u32[]{:S(2)}) collective-permute-start(bf16[200,768]{1,0:T(8,128)(2,1)S(1)} %get-tuple-element.166), channel_id=1, source_target_pairs={{0,4},{4,0},{8,12},{12,8},{16,20},{20,16},{24,28},{28,24},{1,5},{5... | collective-permute-start | bytes 921608 | tf_op jit(solution)/shard_map/ppermute | solution.py:452
  80.4 12.8 %collective-permute-start.11 = (bf16[192,768]{1,0:T(8,128)(2,1)S(1)}, bf16[192,768]{1,0:T(8,128)(2,1)S(1)}, u32[]{:S(2)}, u32[]{:S(2)}) collective-permute-start(bf16[192,768]{1,0:T(8,128)(2,1)S(1)} %get-tuple-element.169), channel_id=1, source_target_pairs={{0,8},{4,12},{8,0},{12,4},{16,24},{20,28},{24,16},{28,20},{1,9},{5... | collective-permute-start | bytes 884744 | tf_op jit(solution)/shard_map/ppermute | solution.py:452
  84.6 17.3 %collective-permute-start.15 = (bf16[200,768]{1,0:T(8,128)(2,1)S(1)}, bf16[200,768]{1,0:T(8,128)(2,1)S(1)}, u32[]{:S(2)}, u32[]{:S(2)}) collective-permute-start(bf16[200,768]{1,0:T(8,128)(2,1)S(1)} %get-tuple-element.185), channel_id=1, source_target_pairs={{0,16},{4,20},{8,24},{12,28},{16,0},{20,4},{24,8},{28,12},{1,17},{... | collective-permute-start | bytes 921608 | tf_op jit(solution)/shard_map/ppermute | solution.py:452
  94.0 7.3 %collective-permute-start.13 = (bf16[104,768]{1,0:T(8,128)(2,1)S(1)}, bf16[104,768]{1,0:T(8,128)(2,1)S(1)}, u32[]{:S(2)}, u32[]{:S(2)}) collective-permute-start(bf16[104,768]{1,0:T(8,128)(2,1)S(1)} %get-tuple-element.180), channel_id=1, source_target_pairs={{0,8},{4,12},{8,0},{12,4},{16,24},{20,28},{24,16},{28,20},{1,9},{5... | collective-permute-start | bytes 479240 | tf_op jit(solution)/shard_map/ppermute | solution.py:452
  102.0 14.9 %collective-permute-start.16 = (bf16[192,768]{1,0:T(8,128)(2,1)S(1)}, bf16[192,768]{1,0:T(8,128)(2,1)S(1)}, u32[]{:S(2)}, u32[]{:S(2)}) collective-permute-start(bf16[192,768]{1,0:T(8,128)(2,1)S(1)} %get-tuple-element.187.mine_ref), channel_id=1, source_target_pairs={{0,16},{4,20},{8,24},{12,28},{16,0},{20,4},{24,8},{28,12},{1,17},{... | collective-permute-start | bytes 884744 | tf_op jit(solution)/shard_map/ppermute | solution.py:452
  104.1 50.1 %collective-permute-start.25 = (bf16[1024,768]{1,0:T(8,128)(2,1)S(1)}, bf16[1024,768]{1,0:T(8,128)(2,1)S(1)}, u32[]{:S(2)}, u32[]{:S(2)}) collective-permute-start(bf16[1024,768]{1,0:T(8,128)(2,1)S(1)} %forward.1), channel_id=1, source_target_pairs={{0,2},{1,3},{2,0},{3,1},{4,6},{5,7},{6,4},{7,5},{8,10},{9,11},{10,... | collective-permute-start | bytes 4718600 | tf_op jit(solution)/shard_map/ppermute | solution.py:452
  117.5 13.8 %collective-permute-start.18 = (bf16[192,768]{1,0:T(8,128)(2,1)S(1)}, bf16[192,768]{1,0:T(8,128)(2,1)S(1)}, u32[]{:S(2)}, u32[]{:S(2)}) collective-permute-start(bf16[192,768]{1,0:T(8,128)(2,1)S(1)} %get-tuple-element.192.ma_ref), channel_id=1, source_target_pairs={{0,8},{4,12},{8,0},{12,4},{16,24},{20,28},{24,16},{28,20},{1,9},{5... | collective-permute-start | bytes 884744 | tf_op jit(solution)/shard_map/ppermute | solution.py:452
  117.6 13.8 %collective-permute-start.19 = (bf16[192,768]{1,0:T(8,128)(2,1)S(1)}, bf16[192,768]{1,0:T(8,128)(2,1)S(1)}, u32[]{:S(2)}, u32[]{:S(2)}) collective-permute-start(bf16[192,768]{1,0:T(8,128)(2,1)S(1)} %get-tuple-element.197.mb_ref), channel_id=1, source_target_pairs={{0,4},{4,0},{8,12},{12,8},{16,20},{20,16},{24,28},{28,24},{1,5},{5... | collective-permute-start | bytes 884744 | tf_op jit(solution)/shard_map/ppermute | solution.py:452
  118.0 9.8 %collective-permute-start.17 = (bf16[104,768]{1,0:T(8,128)(2,1)S(1)}, bf16[104,768]{1,0:T(8,128)(2,1)S(1)}, u32[]{:S(2)}, u32[]{:S(2)}) collective-permute-start(bf16[104,768]{1,0:T(8,128)(2,1)S(1)} %get-tuple-element.193), channel_id=1, source_target_pairs={{0,16},{4,20},{8,24},{12,28},{16,0},{20,4},{24,8},{28,12},{1,17},{... | collective-permute-start | bytes 479240 | tf_op jit(solution)/shard_map/ppermute | solution.py:452
  127.9 11.1 %collective-permute-start.20 = (bf16[96,768]{1,0:T(8,128)(2,1)S(1)}, bf16[96,768]{1,0:T(8,128)(2,1)S(1)}, u32[]{:S(2)}, u32[]{:S(2)}) collective-permute-start(bf16[96,768]{1,0:T(8,128)(2,1)S(1)} %get-tuple-element.195.mine_ref), channel_id=1, source_target_pairs={{0,16},{4,20},{8,24},{12,28},{16,0},{20,4},{24,8},{28,12},{1,17},{... | collective-permute-start | bytes 442376 | tf_op jit(solution)/shard_map/ppermute | solution.py:452
  132.0 25.8 %collective-permute-start.27 = (bf16[384,768]{1,0:T(8,128)(2,1)S(1)}, bf16[384,768]{1,0:T(8,128)(2,1)S(1)}, u32[]{:S(2)}, u32[]{:S(2)}) collective-permute-start(bf16[384,768]{1,0:T(8,128)(2,1)S(1)} %get-tuple-element.215.mb_ref), channel_id=1, source_target_pairs={{0,8},{4,12},{8,0},{12,4},{16,24},{20,28},{24,16},{28,20},{1,9},{5... | collective-permute-start | bytes 1769480 | tf_op jit(solution)/shard_map/ppermute | solution.py:452
  132.1 25.7 %collective-permute-start.26 = (bf16[384,768]{1,0:T(8,128)(2,1)S(1)}, bf16[384,768]{1,0:T(8,128)(2,1)S(1)}, u32[]{:S(2)}, u32[]{:S(2)}) collective-permute-start(bf16[384,768]{1,0:T(8,128)(2,1)S(1)} %get-tuple-element.198.ma_ref), channel_id=1, source_target_pairs={{0,4},{4,0},{8,12},{12,8},{16,20},{20,16},{24,28},{28,24},{1,5},{5... | collective-permute-start | bytes 1769480 | tf_op jit(solution)/shard_map/ppermute | solution.py:452
  132.7 8.1 %collective-permute-start.22 = (f32[4,768]{1,0:T(4,128)S(1)}, f32[4,768]{1,0:T(4,128)S(1)}, u32[]{:S(2)}, u32[]{:S(2)}) collective-permute-start(f32[4,768]{1,0:T(4,128)S(1)} %fusion), channel_id=1, source_target_pairs={{0,2},{1,3},{2,0},{3,1},{4,6},{5,7},{6,4},{7,5},{8,10},{9,11},{10,... | collective-permute-start | bytes 36872 | tf_op jit(solution)/shard_map/ppermute | solution.py:452
  139.7 13.6 %collective-permute-start.23 = (bf16[96,768]{1,0:T(8,128)(2,1)S(1)}, bf16[96,768]{1,0:T(8,128)(2,1)S(1)}, u32[]{:S(2)}, u32[]{:S(2)}) collective-permute-start(bf16[96,768]{1,0:T(8,128)(2,1)S(1)} %get-tuple-element.200.ma_ref), channel_id=1, source_target_pairs={{0,8},{4,12},{8,0},{12,4},{16,24},{20,28},{24,16},{28,20},{1,9},{5... | collective-permute-start | bytes 442376 | tf_op jit(solution)/shard_map/ppermute | solution.py:452
  140.9 12.4 %collective-permute-start.24 = (bf16[96,768]{1,0:T(8,128)(2,1)S(1)}, bf16[96,768]{1,0:T(8,128)(2,1)S(1)}, u32[]{:S(2)}, u32[]{:S(2)}) collective-permute-start(bf16[96,768]{1,0:T(8,128)(2,1)S(1)} %get-tuple-element.206.mb_ref), channel_id=1, source_target_pairs={{0,4},{4,0},{8,12},{12,8},{16,20},{20,16},{24,28},{28,24},{1,5},{5... | collective-permute-start | bytes 442376 | tf_op jit(solution)/shard_map/ppermute | solution.py:452
  153.8 8.3 %collective-permute-start.28 = (bf16[192,768]{1,0:T(8,128)(2,1)S(1)}, bf16[192,768]{1,0:T(8,128)(2,1)S(1)}, u32[]{:S(2)}, u32[]{:S(2)}) collective-permute-start(bf16[192,768]{1,0:T(8,128)(2,1)S(1)} %get-tuple-element.207.ma_ref), channel_id=1, source_target_pairs={{0,4},{4,0},{8,12},{12,8},{16,20},{20,16},{24,28},{28,24},{1,5},{5... | collective-permute-start | bytes 884744 | tf_op jit(solution)/shard_map/ppermute | solution.py:452
  153.9 8.3 %collective-permute-start.29 = (bf16[192,768]{1,0:T(8,128)(2,1)S(1)}, bf16[192,768]{1,0:T(8,128)(2,1)S(1)}, u32[]{:S(2)}, u32[]{:S(2)}) collective-permute-start(bf16[192,768]{1,0:T(8,128)(2,1)S(1)} %get-tuple-element.218.mb_ref), channel_id=1, source_target_pairs={{0,8},{4,12},{8,0},{12,4},{16,24},{20,28},{24,16},{28,20},{1,9},{5... | collective-permute-start | bytes 884744 | tf_op jit(solution)/shard_map/ppermute | solution.py:452
  (23 other events, 168.1 us)

commit v3 on v2

--- a/solution.py
+++ b/solution.py
@@ -21,12 +21,12 @@
 UNIT = 500_000_000
 SEQUENCE = (
     "attend_back", "p1", "qkv_end", "p2", "q1", "sides", "q2", "p3",
-    "forward", "p4", "q3", "p5", "q4", "vectors", "q5", "result",
-    "tokens_grad", "p6", "q6",
+    "forward", "p4", "q3", "p5", "q4", "result", "tokens_grad", "q5",
+    "p6", "vectors", "q6",
 )
 COSTS = {
     "attend": 10, "attend_back": 14, "ff_back": 4, "front": 2, "p3": 150, "p4": 60,
-    "segments": 8,
+    "segments": 8, "tokens_grad": 20,
 }
 ORDER_A, ORDER_B = (0, 1, 2), (1, 0, 2)
 
@@ -528,9 +528,10 @@
     wd_ref[...] = jnp.where(side == 0, got, mine)
 
 
-def vectors_kernel(near_ref, a_ref, c_ref, *out_refs):
+def vectors_kernel(n0_ref, n1_ref, n2_ref, n3_ref, a_ref, c_ref, *out_refs):
+    near = (n0_ref[...] + n1_ref[...]) + (n2_ref[...] + n3_ref[...])
     for i in range(4):
-        out_refs[i][...] = near_ref[i : i + 1, :].reshape(-1)
+        out_refs[i][...] = near[i : i + 1, :].reshape(-1)
     out_refs[4][...] = a_ref[2:3, :].reshape(-1)
     out_refs[5][...] = a_ref[2:3, :].reshape(-1)
     out_refs[6][...] = a_ref[3:4, :].reshape(-1)
@@ -671,8 +672,7 @@
         got[name] = dp_swap(keep[name], dp, ORDER_A[2])
         if len(vectors) == 2:
             near = jnp.concatenate([vectors["q"][:2], vectors["p"][:2]], axis=0)
-            near = near + swap(near, "tensor", tp, 1)
-            made["near"] = near + swap(near, "tensor", tp, 2)
+            made["near"] = [near] + [swap(near, "tensor", tp, k) for k in range(1, tp)]
 
     def far_join(name):
         keep[name] = run(
@@ -761,7 +761,7 @@
     def finish_vectors():
         flat = like((width,), f32)
         made["vectors"] = run(
-            vectors_kernel, "vectors", [made["near"], vectors["p"], vectors["q"]],
+            vectors_kernel, "vectors", [*made["near"], vectors["p"], vectors["q"]],
             [flat] * 7 + [like((wq.shape[0],), f32)], hold=0, flops=cost("vectors"),
         )
 

time: 165 us -> 160 us (0.970)
  waiting for transfers between devices: 51.9 us -> 45.1 us
  starting transfers between devices: 27.5 us -> 30.8 us
    ppermute x30 -> x31, waiting for transfers between devices: 51.9 us -> 45.1 us  [swap(): return lax.ppermute(value, axis, [(i, i ^ distance) for i in range(size)])]
    ppermute x30 -> x31, starting transfers between devices: 27.5 us -> 30.8 us  [swap(): return lax.ppermute(value, axis, [(i, i ^ distance) for i in range(size)])]
  transfers between devices with their start and end apart: 30 -> 31, of which waited for: 14 -> 13; matrix products, arithmetic and copies ran while one was open for 0% -> 0% of each run, Pallas kernels for 45% -> 46%
where the time goes in v3:
time: 160 us
  Pallas kernels  81.6 us (51%)
  waiting for transfers between devices  45.1 us (28%)
  starting transfers between devices  30.8 us (19%)
    pallas_call x27, Pallas kernels, call(): pl.pallas_call(kernel, out_shape=tuple(outs), in_specs=[SMEM if i in smem...  81.6 us
    ppermute x31, waiting for transfers between devices, swap(): return lax.ppermute(value, axis, [(i, i ^ distance) for i in range(size)])  45.1 us
    ppermute x31, starting transfers between devices, swap(): return lax.ppermute(value, axis, [(i, i ^ distance) for i in range(size)])  30.8 us
  transfers between devices with their start and end apart: 31, of which 13 were waited for; matrix products, arithmetic and copies ran while one was open for 0% of the time, Pallas kernels for 46%

profile of v3, /device:TPU:0, one launch (start us, length us, event | category | flops | bytes accessed | tf_op | source)
XLA Modules:
  0.0 159.6 jit_solution(11565787627222045354)
XLA Ops:
  1.4 2.9 %collective-permute-start.2 = (bf16[512,768]{1,0:T(8,128)(2,1)}, bf16[512,768]{1,0:T(8,128)(2,1)}, u32[]{:S(2)}, u32[]{:S(2)}) collective-permute-start(bf16[512,768]{1,0:T(8,128)(2,1)} %bitcast.14), channel_id=1, source_target_pairs={{0,2},{1,3},{2,0},{3,1},{4,6},{5,7},{6,4},{7,5},{8,10},{9,11},{10,... | collective-permute-start | bytes 2359304 | tf_op jit(solution)/shard_map/ppermute | solution.py:452
  6.9 5.1 %front.3 = (bf16[1024,768]{1,0:T(8,128)(2,1)S(1)}, bf16[1024,768]{1,0:T(8,128)(2,1)S(1)}, bf16[1024,768]{1,0:T(8,128)(2,1)S(1)}, bf16[3,3,64,1024]{3,2,1,0:T(8,128)(2,1)S(1)}) custom-call(s32[2]{0:T(128)S(1)} %pad_add_fusion.place_ref, bf16[512,768]{1,0:T(8,128)(2,1)S(1)} %bitcast.15, bf16[512,768]{1,0:T(8,128)(2,1)} %collective-permute-done.refs_1_, ...), custom_call_target="tpu_custom_call" | custom-call | flops 2000000000 | bytes 1000 | tf_op jit(solution)/shard_map/front/pallas_call | solution.py:51
  12.0 8.0 %ff_back.3 = (bf16[1024,768]{1,0:T(8,128)(2,1)S(1)}, bf16[1024,768]{1,0:T(8,128)(2,1)S(1)}, bf16[192,1024]{1,0:T(8,128)(2,1)S(1)}, f32[768,768]{1,0:T(8,128)S(1)...) custom-call(s32[2]{0:T(128)S(1)} %pad_add_fusion.place_ref, bf16[512,768]{1,0:T(8,128)(2,1)S(1)} %bitcast.19, ...), custom_call_target="tpu_custom_call" | custom-call | flops 4000000000 | bytes 1000 | tf_op jit(solution)/shard_map/ff_back/pallas_call | solution.py:51
  20.0 2.4 %collective-permute-done.2.refs_0_ = bf16[512,768]{1,0:T(8,128)(2,1)} collective-permute-done((bf16[512,768]{1,0:T(8,128)(2,1)}, bf16[512,768]{1,0:T(8,128)(2,1)}, u32[]{:S(2)}, u32[]{:S(2)}) %collective-permute-start.2) | collective-permute-done | bytes 786464 | tf_op jit(solution)/shard_map/ppermute | solution.py:452
  24.1 3.0 %front.4 = (bf16[512,768]{1,0:T(8,128)(2,1)S(1)}, bf16[512,768]{1,0:T(8,128)(2,1)S(1)}, bf16[512,768]{1,0:T(8,128)(2,1)S(1)}, bf16[3,3,64,512]{3,2,1,0:T(8,128)(2,1)S(1)}) custom-call(s32[2]{0:T(128)S(1)} %pad_add_fusion.place_ref, bf16[512,768]{1,0:T(8,128)(2,1)} %collective-permute-done.2.refs_0_, bf16[768]{0:T(1024)(128)(2,1)S(1)} %copy-done.6, ...), custom_call_target="tpu_custom_call" | custom-call | flops 1000000000 | bytes 1000 | tf_op jit(solution)/shard_map/front/pallas_call | solution.py:51
  27.1 2.6 %front.5 = (bf16[512,768]{1,0:T(8,128)(2,1)S(1)}, bf16[512,768]{1,0:T(8,128)(2,1)S(1)}, bf16[512,768]{1,0:T(8,128)(2,1)S(1)}, bf16[3,3,64,512]{3,2,1,0:T(8,128)(2,1)S(1)}) custom-call(s32[2]{0:T(128)S(1)} %pad_add_fusion.place_ref, bf16[512,768]{1,0:T(8,128)(2,1)S(1)} %collective-permute-done.3.refs_0_, bf16[768]{0:T(1024)(128)(2,1)S(1)} %copy-done.6, ...), custom_call_target="tpu_custom_call" | custom-call | flops 1000000000 | bytes 1000 | tf_op jit(solution)/shard_map/front/pallas_call | solution.py:51
  29.7 12.7 %attend.1 = (bf16[3,3,64,2048]{3,2,1,0:T(8,128)(2,1)S(1)}, bf16[192,2048]{1,0:T(8,128)(2,1)S(1)}, f32[3,1,2048]{2,1,0:T(1,128)S(1)}) custom-call(s32[2]{0:T(128)S(1)} %pad_add_fusion.place_ref, s32[8]{0:T(128)S(1)} %get-tuple-element.120.lo_ref, s32[1,2048]{1,0:T(1,128)S(1)} %get-tuple-element.121.start_ref, ...), custom_call_target="tpu_custom_call" | custom-call | flops 5000000000 | bytes 1000 | tf_op jit(solution)/shard_map/attend/pallas_call | solution.py:51
  42.7 4.1 %ff_back.4 = (bf16[512,768]{1,0:T(8,128)(2,1)S(1)}, bf16[512,768]{1,0:T(8,128)(2,1)S(1)}, bf16[192,512]{1,0:T(8,128)(2,1)S(1)}, f32[768,768]{1,0:T(8,128)S(1)}, ...) custom-call(s32[2]{0:T(128)S(1)} %pad_add_fusion.place_ref, bf16[512,768]{1,0:T(8,128)(2,1)S(1)} %collective-permute-done.4.refs_0_.dy2_ref, ...), custom_call_target="tpu_custom_call" | custom-call | flops 2000000000 | bytes 1000 | tf_op jit(solution)/shard_map/ff_back/pallas_call | solution.py:51
  46.8 5.5 %ff_back.5 = (bf16[512,768]{1,0:T(8,128)(2,1)S(1)}, bf16[512,768]{1,0:T(8,128)(2,1)S(1)}, bf16[192,512]{1,0:T(8,128)(2,1)S(1)}, bf16[384,768]{1,0:T(8,128)(2,1)S...) custom-call(s32[2]{0:T(128)S(1)} %pad_add_fusion.place_ref, ...), custom_call_target="tpu_custom_call" | custom-call | flops 2000000000 | bytes 1000 | tf_op jit(solution)/shard_map/ff_back/pallas_call | solution.py:51
  55.5 16.2 %attend_back.1.dqkv_ref = bf16[3,3,64,2048]{3,2,1,0:T(8,128)(2,1)S(1)} custom-call(s32[2]{0:T(128)S(1)} %pad_add_fusion.place_ref, s32[8]{0:T(128)S(1)} %get-tuple-element.120.lo_ref, s32[1,2048]{1,0:T(1,128)S(1)} %get-tuple-element.121.start_ref, bf16[3,3,64,2048]{3,2,1,0:T(8,128)(2,1)S(1)} %get-tuple-element.148.qkv_ref, ...), custom_call_target="tpu_custom_call" | custom-call | flops 7000000000 | bytes 1000 | tf_op jit(solution)/shard_map/attend_back/pallas_call | solution.py:51
  73.6 4.4 %qkv_end.1 = (bf16[200,768]{1,0:T(8,128)(2,1)S(1)}, bf16[200,768]{1,0:T(8,128)(2,1)S(1)}, bf16[192,768]{1,0:T(8,128)(2,1)S(1)}, bf16[192,768]{1,0:T(8,128)(2,1)S(1)}) custom-call(s32[2]{0:T(128)S(1)} %pad_add_fusion.place_ref, bf16[3,3,64,2048]{3,2,1,0:T(8,128)(2,1)S(1)} %attend_back.1.dqkv_ref, bf16[1024,768]{1,0:T(8,128)(2,1)S(1)} %get-tuple-element.127.refs_4_.xh0_ref, ...), custom_call_target="tpu_custom_call" | custom-call | flops 1000000 | bytes 1000 | tf_op jit(solution)/shard_map/qkv_end/pallas_call | solution.py:51
  83.7 2.6 %collective-permute-start.15 = (bf16[200,768]{1,0:T(8,128)(2,1)S(1)}, bf16[200,768]{1,0:T(8,128)(2,1)S(1)}, u32[]{:S(2)}, u32[]{:S(2)}) collective-permute-start(bf16[200,768]{1,0:T(8,128)(2,1)S(1)} %get-tuple-element.185), channel_id=1, source_target_pairs={{0,16},{4,20},{8,24},{12,28},{16,0},{20,4},{24,8},{28,12},{1,17},{... | collective-permute-start | bytes 921608 | tf_op jit(solution)/shard_map/ppermute | solution.py:452
  86.4 1.8 %collective-permute-done.10.ga_ref = bf16[200,768]{1,0:T(8,128)(2,1)S(1)} collective-permute-done((bf16[200,768]{1,0:T(8,128)(2,1)S(1)}, bf16[200,768]{1,0:T(8,128)(2,1)S(1)}, u32[]{:S(2)}, u32[]{:S(2)}) %collective-permute-start.10) | collective-permute-done | bytes 307232 | tf_op jit(solution)/shard_map/ppermute | solution.py:452
  88.2 4.5 %collective-permute-done.11.gb_ref = bf16[192,768]{1,0:T(8,128)(2,1)S(1)} collective-permute-done((bf16[192,768]{1,0:T(8,128)(2,1)S(1)}, bf16[192,768]{1,0:T(8,128)(2,1)S(1)}, u32[]{:S(2)}, u32[]{:S(2)}) %collective-permute-start.11) | collective-permute-done | bytes 294944 | tf_op jit(solution)/shard_map/ppermute | solution.py:452
  94.5 3.6 %sides.1 = (f32[512,768]{1,0:T(8,128)S(1)}, f32[512,768]{1,0:T(8,128)S(1)}, f32[512,768]{1,0:T(8,128)S(1)}, f32[512,768]{1,0:T(8,128)S(1)}, bf16[2048,768]{1,0:T(8,128)(2,1)S(1)}) custom-call(bf16[3,3,64,2048]{3,2,1,0:T(8,128)(2,1)S(1)} %attend_back.1.dqkv_ref, bf16[1024,768]{1,0:T(8,128)(2,1)S(1)} %get-tuple-element.172.back0_ref, ...), custom_call_target="tpu_custom_call" | custom-call | flops 1000000 | bytes 1000 | tf_op jit(solution)/shard_map/sides/pallas_call | solution.py:51
  105.6 14.9 %collective-permute-done.16.got_ref = bf16[192,768]{1,0:T(8,128)(2,1)S(1)} collective-permute-done((bf16[192,768]{1,0:T(8,128)(2,1)S(1)}, bf16[192,768]{1,0:T(8,128)(2,1)S(1)}, u32[]{:S(2)}, u32[]{:S(2)}) %collective-permute-start.16) | collective-permute-done | bytes 294944 | tf_op jit(solution)/shard_map/ppermute | solution.py:452
  124.3 7.6 %collective-permute-done.18.ga_ref = bf16[192,768]{1,0:T(8,128)(2,1)S(1)} collective-permute-done((bf16[192,768]{1,0:T(8,128)(2,1)S(1)}, bf16[192,768]{1,0:T(8,128)(2,1)S(1)}, u32[]{:S(2)}, u32[]{:S(2)}) %collective-permute-start.18) | collective-permute-done | bytes 294944 | tf_op jit(solution)/shard_map/ppermute | solution.py:452
  135.3 2.0 %collective-permute-start.25 = (bf16[384,768]{1,0:T(8,128)(2,1)S(1)}, bf16[384,768]{1,0:T(8,128)(2,1)S(1)}, u32[]{:S(2)}, u32[]{:S(2)}) collective-permute-start(bf16[384,768]{1,0:T(8,128)(2,1)S(1)} %get-tuple-element.208.mb_ref), channel_id=1, source_target_pairs={{0,8},{4,12},{8,0},{12,4},{16,24},{20,28},{24,16},{28,20},{1,9},{5... | collective-permute-start | bytes 1769480 | tf_op jit(solution)/shard_map/ppermute | solution.py:452
  137.3 3.3 %collective-permute-done.21.far_ref = bf16[1024,768]{1,0:T(8,128)(2,1)S(1)} collective-permute-done((bf16[1024,768]{1,0:T(8,128)(2,1)S(1)}, bf16[1024,768]{1,0:T(8,128)(2,1)S(1)}, u32[]{:S(2)}, u32[]{:S(2)}) %collective-permute-start.21) | collective-permute-done | bytes 1572896 | tf_op jit(solution)/shard_map/ppermute | solution.py:452
  141.9 2.3 %tokens_grad.1 = f32[512,768]{1,0:T(8,128)} custom-call(bf16[512,768]{1,0:T(8,128)(2,1)S(1)} %bitcast.17, bf16[512,768]{1,0:T(8,128)(2,1)S(1)} %bitcast.22, f32[512,768]{1,0:T(8,128)S(1)} %get-tuple-element.202.keep_ref, bf16[2048,768]{1,0:T(8,128)(2,1)S(1)} %collective-permute-done.12.got_ref, bf16[1024,768]{1,0:T(8,128)(2,1)S(1)} %collective-permute-done.21.far_ref), custom_call_target="tpu_custom_call" | custom-call | flops 10000000000 | bytes 1000 | tf_op jit(solution)/shard_map/tokens_grad/pallas_call | solution.py:51
  144.2 4.6 %collective-permute-done.23.gb_ref = bf16[96,768]{1,0:T(8,128)(2,1)S(1)} collective-permute-done((bf16[96,768]{1,0:T(8,128)(2,1)S(1)}, bf16[96,768]{1,0:T(8,128)(2,1)S(1)}, u32[]{:S(2)}, u32[]{:S(2)}) %collective-permute-start.23) | collective-permute-done | bytes 147488 | tf_op jit(solution)/shard_map/ppermute | solution.py:452
  150.4 2.0 %collective-permute-done.25.gb_ref = bf16[384,768]{1,0:T(8,128)(2,1)S(1)} collective-permute-done((bf16[384,768]{1,0:T(8,128)(2,1)S(1)}, bf16[384,768]{1,0:T(8,128)(2,1)S(1)}, u32[]{:S(2)}, u32[]{:S(2)}) %collective-permute-start.25) | collective-permute-done | bytes 589856 | tf_op jit(solution)/shard_map/ppermute | solution.py:452
  153.9 3.0 %grads.1 = (f32[768,768]{1,0:T(8,128)}, f32[768,768]{1,0:T(8,128)}) custom-call(s32[2]{0:T(128)S(1)} %pad_add_fusion.place_ref, bf16[384,768]{1,0:T(8,128)(2,1)S(1)} %get-tuple-element.198.ma_ref, bf16[384,768]{1,0:T(8,128)(2,1)S(1)} %collective-permute-done.24.ga_ref, bf16[384,768]{1,0:T(8,128)(2,1)S(1)} %get-tuple-element.208.mb_ref, ...), custom_call_target="tpu_custom_call" | custom-call | flops 1000000 | bytes 1000 | tf_op jit(solution)/shard_map/grads/pallas_call | solution.py:51
  157.5 2.1 %spread.1 = (f32[576,768]{1,0:T(8,128)}, f32[192,768]{1,0:T(8,128)}) custom-call(s32[2]{0:T(128)S(1)} %pad_add_fusion.place_ref, bf16[192,768]{1,0:T(8,128)(2,1)S(1)} %get-tuple-element.206.ma_ref, bf16[192,768]{1,0:T(8,128)(2,1)S(1)} %collective-permute-done.29.ga_ref, bf16[192,768]{1,0:T(8,128)(2,1)S(1)} %get-tuple-element.218.mb_ref, ...), custom_call_target="tpu_custom_call" | custom-call | flops 1000000 | bytes 1000 | tf_op jit(solution)/shard_map/spread/pallas_call | solution.py:51
  (104 shorter events, 37.4 us)
Async XLA Ops:
  0.6 6.1 %collective-permute-start = (bf16[512,768]{1,0:T(8,128)(2,1)}, bf16[512,768]{1,0:T(8,128)(2,1)}, u32[]{:S(2)}, u32[]{:S(2)}) collective-permute-start(bf16[512,768]{1,0:T(8,128)(2,1)} %bitcast.13), channel_id=1, source_target_pairs={{0,1},{1,0},{2,3},{3,2},{4,5},{5,4},{6,7},{7,6},{8,9},{9,8},{10,11... | collective-permute-start | bytes 2359304 | tf_op jit(solution)/shard_map/ppermute | solution.py:452
  1.2 10.7 %collective-permute-start.1 = (bf16[512,768]{1,0:T(8,128)(2,1)}, bf16[512,768]{1,0:T(8,128)(2,1)}, u32[]{:S(2)}, u32[]{:S(2)}) collective-permute-start(bf16[512,768]{1,0:T(8,128)(2,1)} %bitcast.18), channel_id=1, source_target_pairs={{0,1},{1,0},{2,3},{3,2},{4,5},{5,4},{6,7},{7,6},{8,9},{9,8},{10,11... | collective-permute-start | bytes 2359304 | tf_op jit(solution)/shard_map/ppermute | solution.py:452
  1.4 21.0 %collective-permute-start.2 = (bf16[512,768]{1,0:T(8,128)(2,1)}, bf16[512,768]{1,0:T(8,128)(2,1)}, u32[]{:S(2)}, u32[]{:S(2)}) collective-permute-start(bf16[512,768]{1,0:T(8,128)(2,1)} %bitcast.14), channel_id=1, source_target_pairs={{0,2},{1,3},{2,0},{3,1},{4,6},{5,7},{6,4},{7,5},{8,10},{9,11},{10,... | collective-permute-start | bytes 2359304 | tf_op jit(solution)/shard_map/ppermute | solution.py:452
  22.4 20.0 %collective-permute-start.4 = (bf16[512,768]{1,0:T(8,128)(2,1)S(1)}, bf16[512,768]{1,0:T(8,128)(2,1)S(1)}, u32[]{:S(2)}, u32[]{:S(2)}) collective-permute-start(bf16[512,768]{1,0:T(8,128)(2,1)S(1)} %bitcast.20), channel_id=1, source_target_pairs={{0,2},{1,3},{2,0},{3,1},{4,6},{5,7},{6,4},{7,5},{8,10},{9,11},{10,... | collective-permute-start | bytes 2359304 | tf_op jit(solution)/shard_map/ppermute | solution.py:452
  52.3 19.4 %collective-permute-start.7 = (bf16[384,768]{1,0:T(8,128)(2,1)S(1)}, bf16[384,768]{1,0:T(8,128)(2,1)S(1)}, u32[]{:S(2)}, u32[]{:S(2)}) collective-permute-start(bf16[384,768]{1,0:T(8,128)(2,1)S(1)} %get-tuple-element.157), channel_id=1, source_target_pairs={{0,8},{4,12},{8,0},{12,4},{16,24},{20,28},{24,16},{28,20},{1,9},{5... | collective-permute-start | bytes 1769480 | tf_op jit(solution)/shard_map/ppermute | solution.py:452
  54.0 17.7 %collective-permute-start.6 = (bf16[392,768]{1,0:T(8,128)(2,1)S(1)}, bf16[392,768]{1,0:T(8,128)(2,1)S(1)}, u32[]{:S(2)}, u32[]{:S(2)}) collective-permute-start(bf16[392,768]{1,0:T(8,128)(2,1)S(1)} %get-tuple-element.154), channel_id=1, source_target_pairs={{0,4},{4,0},{8,12},{12,8},{16,20},{20,16},{24,28},{28,24},{1,5},{5... | collective-permute-start | bytes 1806344 | tf_op jit(solution)/shard_map/ppermute | solution.py:452
  72.6 9.6 %collective-permute-start.8 = (bf16[200,768]{1,0:T(8,128)(2,1)S(1)}, bf16[200,768]{1,0:T(8,128)(2,1)S(1)}, u32[]{:S(2)}, u32[]{:S(2)}) collective-permute-start(bf16[200,768]{1,0:T(8,128)(2,1)S(1)} %get-tuple-element.161), channel_id=1, source_target_pairs={{0,8},{4,12},{8,0},{12,4},{16,24},{20,28},{24,16},{28,20},{1,9},{5... | collective-permute-start | bytes 921608 | tf_op jit(solution)/shard_map/ppermute | solution.py:452
  73.2 9.9 %collective-permute-start.9 = (bf16[192,768]{1,0:T(8,128)(2,1)S(1)}, bf16[192,768]{1,0:T(8,128)(2,1)S(1)}, u32[]{:S(2)}, u32[]{:S(2)}) collective-permute-start(bf16[192,768]{1,0:T(8,128)(2,1)S(1)} %get-tuple-element.164), channel_id=1, source_target_pairs={{0,4},{4,0},{8,12},{12,8},{16,20},{20,16},{24,28},{28,24},{1,5},{5... | collective-permute-start | bytes 884744 | tf_op jit(solution)/shard_map/ppermute | solution.py:452
  78.0 10.2 %collective-permute-start.10 = (bf16[200,768]{1,0:T(8,128)(2,1)S(1)}, bf16[200,768]{1,0:T(8,128)(2,1)S(1)}, u32[]{:S(2)}, u32[]{:S(2)}) collective-permute-start(bf16[200,768]{1,0:T(8,128)(2,1)S(1)} %get-tuple-element.166), channel_id=1, source_target_pairs={{0,4},{4,0},{8,12},{12,8},{16,20},{20,16},{24,28},{28,24},{1,5},{5... | collective-permute-start | bytes 921608 | tf_op jit(solution)/shard_map/ppermute | solution.py:452
  79.6 13.0 %collective-permute-start.11 = (bf16[192,768]{1,0:T(8,128)(2,1)S(1)}, bf16[192,768]{1,0:T(8,128)(2,1)S(1)}, u32[]{:S(2)}, u32[]{:S(2)}) collective-permute-start(bf16[192,768]{1,0:T(8,128)(2,1)S(1)} %get-tuple-element.169), channel_id=1, source_target_pairs={{0,8},{4,12},{8,0},{12,4},{16,24},{20,28},{24,16},{28,20},{1,9},{5... | collective-permute-start | bytes 884744 | tf_op jit(solution)/shard_map/ppermute | solution.py:452
  83.7 16.3 %collective-permute-start.15 = (bf16[200,768]{1,0:T(8,128)(2,1)S(1)}, bf16[200,768]{1,0:T(8,128)(2,1)S(1)}, u32[]{:S(2)}, u32[]{:S(2)}) collective-permute-start(bf16[200,768]{1,0:T(8,128)(2,1)S(1)} %get-tuple-element.185), channel_id=1, source_target_pairs={{0,16},{4,20},{8,24},{12,28},{16,0},{20,4},{24,8},{28,12},{1,17},{... | collective-permute-start | bytes 921608 | tf_op jit(solution)/shard_map/ppermute | solution.py:452
  100.1 20.4 %collective-permute-start.16 = (bf16[192,768]{1,0:T(8,128)(2,1)S(1)}, bf16[192,768]{1,0:T(8,128)(2,1)S(1)}, u32[]{:S(2)}, u32[]{:S(2)}) collective-permute-start(bf16[192,768]{1,0:T(8,128)(2,1)S(1)} %get-tuple-element.187.mine_ref), channel_id=1, source_target_pairs={{0,16},{4,20},{8,24},{12,28},{16,0},{20,4},{24,8},{28,12},{1,17},{... | collective-permute-start | bytes 884744 | tf_op jit(solution)/shard_map/ppermute | solution.py:452
  101.4 21.1 %collective-permute-start.17 = (bf16[104,768]{1,0:T(8,128)(2,1)S(1)}, bf16[104,768]{1,0:T(8,128)(2,1)S(1)}, u32[]{:S(2)}, u32[]{:S(2)}) collective-permute-start(bf16[104,768]{1,0:T(8,128)(2,1)S(1)} %get-tuple-element.193), channel_id=1, source_target_pairs={{0,16},{4,20},{8,24},{12,28},{16,0},{20,4},{24,8},{28,12},{1,17},{... | collective-permute-start | bytes 479240 | tf_op jit(solution)/shard_map/ppermute | solution.py:452
  104.1 36.5 %collective-permute-start.21 = (bf16[1024,768]{1,0:T(8,128)(2,1)S(1)}, bf16[1024,768]{1,0:T(8,128)(2,1)S(1)}, u32[]{:S(2)}, u32[]{:S(2)}) collective-permute-start(bf16[1024,768]{1,0:T(8,128)(2,1)S(1)} %forward.1), channel_id=1, source_target_pairs={{0,2},{1,3},{2,0},{3,1},{4,6},{5,7},{6,4},{7,5},{8,10},{9,11},{10,... | collective-permute-start | bytes 4718600 | tf_op jit(solution)/shard_map/ppermute | solution.py:452
  121.1 10.8 %collective-permute-start.18 = (bf16[192,768]{1,0:T(8,128)(2,1)S(1)}, bf16[192,768]{1,0:T(8,128)(2,1)S(1)}, u32[]{:S(2)}, u32[]{:S(2)}) collective-permute-start(bf16[192,768]{1,0:T(8,128)(2,1)S(1)} %get-tuple-element.192.ma_ref), channel_id=1, source_target_pairs={{0,8},{4,12},{8,0},{12,4},{16,24},{20,28},{24,16},{28,20},{1,9},{5... | collective-permute-start | bytes 884744 | tf_op jit(solution)/shard_map/ppermute | solution.py:452
  121.2 10.7 %collective-permute-start.19 = (bf16[192,768]{1,0:T(8,128)(2,1)S(1)}, bf16[192,768]{1,0:T(8,128)(2,1)S(1)}, u32[]{:S(2)}, u32[]{:S(2)}) collective-permute-start(bf16[192,768]{1,0:T(8,128)(2,1)S(1)} %get-tuple-element.197.mb_ref), channel_id=1, source_target_pairs={{0,4},{4,0},{8,12},{12,8},{16,20},{20,16},{24,28},{28,24},{1,5},{5... | collective-permute-start | bytes 884744 | tf_op jit(solution)/shard_map/ppermute | solution.py:452
  122.6 11.1 %collective-permute-start.20 = (bf16[96,768]{1,0:T(8,128)(2,1)S(1)}, bf16[96,768]{1,0:T(8,128)(2,1)S(1)}, u32[]{:S(2)}, u32[]{:S(2)}) collective-permute-start(bf16[96,768]{1,0:T(8,128)(2,1)S(1)} %get-tuple-element.195.mine_ref), channel_id=1, source_target_pairs={{0,16},{4,20},{8,24},{12,28},{16,0},{20,4},{24,8},{28,12},{1,17},{... | collective-permute-start | bytes 442376 | tf_op jit(solution)/shard_map/ppermute | solution.py:452
  132.5 21.4 %collective-permute-start.24 = (bf16[384,768]{1,0:T(8,128)(2,1)S(1)}, bf16[384,768]{1,0:T(8,128)(2,1)S(1)}, u32[]{:S(2)}, u32[]{:S(2)}) collective-permute-start(bf16[384,768]{1,0:T(8,128)(2,1)S(1)} %get-tuple-element.198.ma_ref), channel_id=1, source_target_pairs={{0,4},{4,0},{8,12},{12,8},{16,20},{20,16},{24,28},{28,24},{1,5},{5... | collective-permute-start | bytes 1769480 | tf_op jit(solution)/shard_map/ppermute | solution.py:452
  134.2 14.6 %collective-permute-start.23 = (bf16[96,768]{1,0:T(8,128)(2,1)S(1)}, bf16[96,768]{1,0:T(8,128)(2,1)S(1)}, u32[]{:S(2)}, u32[]{:S(2)}) collective-permute-start(bf16[96,768]{1,0:T(8,128)(2,1)S(1)} %get-tuple-element.205.mb_ref), channel_id=1, source_target_pairs={{0,4},{4,0},{8,12},{12,8},{16,20},{20,16},{24,28},{28,24},{1,5},{5... | collective-permute-start | bytes 442376 | tf_op jit(solution)/shard_map/ppermute | solution.py:452
  135.3 9.0 %collective-permute-start.22 = (bf16[96,768]{1,0:T(8,128)(2,1)S(1)}, bf16[96,768]{1,0:T(8,128)(2,1)S(1)}, u32[]{:S(2)}, u32[]{:S(2)}) collective-permute-start(bf16[96,768]{1,0:T(8,128)(2,1)S(1)} %get-tuple-element.200.ma_ref), channel_id=1, source_target_pairs={{0,8},{4,12},{8,0},{12,4},{16,24},{20,28},{24,16},{28,20},{1,9},{5... | collective-permute-start | bytes 442376 | tf_op jit(solution)/shard_map/ppermute | solution.py:452
  135.3 17.2 %collective-permute-start.25 = (bf16[384,768]{1,0:T(8,128)(2,1)S(1)}, bf16[384,768]{1,0:T(8,128)(2,1)S(1)}, u32[]{:S(2)}, u32[]{:S(2)}) collective-permute-start(bf16[384,768]{1,0:T(8,128)(2,1)S(1)} %get-tuple-element.208.mb_ref), channel_id=1, source_target_pairs={{0,8},{4,12},{8,0},{12,4},{16,24},{20,28},{24,16},{28,20},{1,9},{5... | collective-permute-start | bytes 1769480 | tf_op jit(solution)/shard_map/ppermute | solution.py:452
  149.4 8.1 %collective-permute-start.29 = (bf16[192,768]{1,0:T(8,128)(2,1)S(1)}, bf16[192,768]{1,0:T(8,128)(2,1)S(1)}, u32[]{:S(2)}, u32[]{:S(2)}) collective-permute-start(bf16[192,768]{1,0:T(8,128)(2,1)S(1)} %get-tuple-element.206.ma_ref), channel_id=1, source_target_pairs={{0,4},{4,0},{8,12},{12,8},{16,20},{20,16},{24,28},{28,24},{1,5},{5... | collective-permute-start | bytes 884744 | tf_op jit(solution)/shard_map/ppermute | solution.py:452
  150.3 7.2 %collective-permute-start.30 = (bf16[192,768]{1,0:T(8,128)(2,1)S(1)}, bf16[192,768]{1,0:T(8,128)(2,1)S(1)}, u32[]{:S(2)}, u32[]{:S(2)}) collective-permute-start(bf16[192,768]{1,0:T(8,128)(2,1)S(1)} %get-tuple-element.218.mb_ref), channel_id=1, source_target_pairs={{0,8},{4,12},{8,0},{12,4},{16,24},{20,28},{24,16},{28,20},{1,9},{5... | collective-permute-start | bytes 884744 | tf_op jit(solution)/shard_map/ppermute | solution.py:452
  150.3 6.5 %collective-permute-start.28 = (f32[4,768]{1,0:T(4,128)S(1)}, f32[4,768]{1,0:T(4,128)S(1)}, u32[]{:S(2)}, u32[]{:S(2)}) collective-permute-start(f32[4,768]{1,0:T(4,128)S(1)} %pad_maximum_fusion.n0_ref), channel_id=1, source_target_pairs={{0,3},{1,2},{2,1},{3,0},{4,7},{5,6},{6,5},{7,4},{8,11},{9,10},{10,... | collective-permute-start | bytes 36872 | tf_op jit(solution)/shard_map/ppermute | solution.py:452
  (24 other events, 135.1 us)

commit v4 on v3

--- a/solution.py
+++ b/solution.py
@@ -21,8 +21,8 @@
 UNIT = 500_000_000
 SEQUENCE = (
     "attend_back", "p1", "qkv_end", "p2", "q1", "sides", "q2", "p3",
-    "forward", "p4", "q3", "p5", "q4", "result", "tokens_grad", "q5",
-    "p6", "vectors", "q6",
+    "forward", "p4", "q3", "p5", "q4", "result", "tokens_grad", "vectors",
+    "q5", "p6", "q6",
 )
 COSTS = {
     "attend": 10, "attend_back": 14, "ff_back": 4, "front": 2, "p3": 150, "p4": 60,
@@ -528,8 +528,8 @@
     wd_ref[...] = jnp.where(side == 0, got, mine)
 
 
-def vectors_kernel(n0_ref, n1_ref, n2_ref, n3_ref, a_ref, c_ref, *out_refs):
-    near = (n0_ref[...] + n1_ref[...]) + (n2_ref[...] + n3_ref[...])
+def vectors_kernel(near_ref, a_ref, c_ref, *out_refs):
+    near = (near_ref[0] + near_ref[1]) + (near_ref[2] + near_ref[3])
     for i in range(4):
         out_refs[i][...] = near[i : i + 1, :].reshape(-1)
     out_refs[4][...] = a_ref[2:3, :].reshape(-1)
@@ -672,7 +672,7 @@
         got[name] = dp_swap(keep[name], dp, ORDER_A[2])
         if len(vectors) == 2:
             near = jnp.concatenate([vectors["q"][:2], vectors["p"][:2]], axis=0)
-            made["near"] = [near] + [swap(near, "tensor", tp, k) for k in range(1, tp)]
+            made["near"] = lax.all_to_all(jnp.broadcast_to(near, (tp, *near.shape)), "tensor", 0, 0)
 
     def far_join(name):
         keep[name] = run(
@@ -761,7 +761,7 @@
     def finish_vectors():
         flat = like((width,), f32)
         made["vectors"] = run(
-            vectors_kernel, "vectors", [*made["near"], vectors["p"], vectors["q"]],
+            vectors_kernel, "vectors", [made["near"], vectors["p"], vectors["q"]],
             [flat] * 7 + [like((wq.shape[0],), f32)], hold=0, flops=cost("vectors"),
         )
 

time: 160 us -> 164 us (1.025)
  waiting for transfers between devices: 45.1 us -> 37.1 us
  starting transfers between devices: 30.8 us -> 36.3 us
  Pallas kernels: 81.6 us -> 85.7 us
  local copies, waits for them, and re-layouts: 0.91 us -> 2.97 us
    ppermute x31 -> x28, waiting for transfers between devices: 45.1 us -> 37.1 us  [swap(): return lax.ppermute(value, axis, [(i, i ^ distance) for i in range(size)])]
    pallas_call x27, Pallas kernels: 81.6 us -> 85.7 us  [call(): pl.pallas_call(kernel, out_shape=tuple(outs), in_specs=[SMEM if i in smem...]
    all_to_all x0 -> x1, starting transfers between devices: none -> 3.27 us  [complete(): lax.all_to_all(jnp.broadcast_to(near, (tp, *near.shape)), 'tensor', 0, 0)]
    ppermute x31 -> x28, starting transfers between devices: 30.8 us -> 33 us  [swap(): return lax.ppermute(value, axis, [(i, i ^ distance) for i in range(size)])]
  transfers between devices with their start and end apart: 31 -> 29, of which waited for: 13 -> 14; matrix products, arithmetic and copies ran while one was open for 0% -> 1% of each run, Pallas kernels for 46% -> 47%
where the time goes in v4:
time: 164 us; the launch traced here: 163 us
  Pallas kernels  85.7 us (52%)
  waiting for transfers between devices  37.1 us (23%)
  starting transfers between devices  36.3 us (22%)
  local copies, waits for them, and re-layouts  2.97 us (2%)
    pallas_call x27, Pallas kernels, call(): pl.pallas_call(kernel, out_shape=tuple(outs), in_specs=[SMEM if i in smem...  85.7 us
    ppermute x28, waiting for transfers between devices, swap(): return lax.ppermute(value, axis, [(i, i ^ distance) for i in range(size)])  37.1 us
    ppermute x28, starting transfers between devices, swap(): return lax.ppermute(value, axis, [(i, i ^ distance) for i in range(size)])  33 us
  transfers between devices with their start and end apart: 29, of which 14 were waited for; matrix products, arithmetic and copies ran while one was open for 1% of the time, Pallas kernels for 47%

profile of v4, /device:TPU:0, one launch (start us, length us, event | category | flops | bytes accessed | tf_op | source)
XLA Modules:
  0.0 163.3 jit_solution(2070616255698556691)
XLA Ops:
  1.4 2.9 %collective-permute-start.2 = (bf16[512,768]{1,0:T(8,128)(2,1)}, bf16[512,768]{1,0:T(8,128)(2,1)}, u32[]{:S(2)}, u32[]{:S(2)}) collective-permute-start(bf16[512,768]{1,0:T(8,128)(2,1)} %bitcast.14), channel_id=1, source_target_pairs={{0,2},{1,3},{2,0},{3,1},{4,6},{5,7},{6,4},{7,5},{8,10},{9,11},{10,... | collective-permute-start | bytes 2359304 | tf_op jit(solution)/shard_map/ppermute | solution.py:452
  6.9 5.1 %front.3 = (bf16[1024,768]{1,0:T(8,128)(2,1)S(1)}, bf16[1024,768]{1,0:T(8,128)(2,1)S(1)}, bf16[1024,768]{1,0:T(8,128)(2,1)S(1)}, bf16[3,3,64,1024]{3,2,1,0:T(8,128)(2,1)S(1)}) custom-call(s32[2]{0:T(128)S(1)} %pad_add_fusion.place_ref, bf16[512,768]{1,0:T(8,128)(2,1)S(1)} %bitcast.15, bf16[512,768]{1,0:T(8,128)(2,1)} %collective-permute-done.refs_1_, ...), custom_call_target="tpu_custom_call" | custom-call | flops 2000000000 | bytes 1000 | tf_op jit(solution)/shard_map/front/pallas_call | solution.py:51
  12.0 8.0 %ff_back.3 = (bf16[1024,768]{1,0:T(8,128)(2,1)S(1)}, bf16[1024,768]{1,0:T(8,128)(2,1)S(1)}, bf16[192,1024]{1,0:T(8,128)(2,1)S(1)}, f32[768,768]{1,0:T(8,128)S(1)...) custom-call(s32[2]{0:T(128)S(1)} %pad_add_fusion.place_ref, bf16[512,768]{1,0:T(8,128)(2,1)S(1)} %bitcast.19, ...), custom_call_target="tpu_custom_call" | custom-call | flops 4000000000 | bytes 1000 | tf_op jit(solution)/shard_map/ff_back/pallas_call | solution.py:51
  20.0 2.4 %collective-permute-done.2.refs_0_ = bf16[512,768]{1,0:T(8,128)(2,1)} collective-permute-done((bf16[512,768]{1,0:T(8,128)(2,1)}, bf16[512,768]{1,0:T(8,128)(2,1)}, u32[]{:S(2)}, u32[]{:S(2)}) %collective-permute-start.2) | collective-permute-done | bytes 786464 | tf_op jit(solution)/shard_map/ppermute | solution.py:452
  24.1 3.0 %front.4 = (bf16[512,768]{1,0:T(8,128)(2,1)S(1)}, bf16[512,768]{1,0:T(8,128)(2,1)S(1)}, bf16[512,768]{1,0:T(8,128)(2,1)S(1)}, bf16[3,3,64,512]{3,2,1,0:T(8,128)(2,1)S(1)}) custom-call(s32[2]{0:T(128)S(1)} %pad_add_fusion.place_ref, bf16[512,768]{1,0:T(8,128)(2,1)} %collective-permute-done.2.refs_0_, bf16[768]{0:T(1024)(128)(2,1)S(1)} %copy-done.10, ...), custom_call_target="tpu_custom_call" | custom-call | flops 1000000000 | bytes 1000 | tf_op jit(solution)/shard_map/front/pallas_call | solution.py:51
  27.1 2.6 %front.5 = (bf16[512,768]{1,0:T(8,128)(2,1)S(1)}, bf16[512,768]{1,0:T(8,128)(2,1)S(1)}, bf16[512,768]{1,0:T(8,128)(2,1)S(1)}, bf16[3,3,64,512]{3,2,1,0:T(8,128)(2,1)S(1)}) custom-call(s32[2]{0:T(128)S(1)} %pad_add_fusion.place_ref, bf16[512,768]{1,0:T(8,128)(2,1)S(1)} %collective-permute-done.3.refs_0_, bf16[768]{0:T(1024)(128)(2,1)S(1)} %copy-done.10, ...), custom_call_target="tpu_custom_call" | custom-call | flops 1000000000 | bytes 1000 | tf_op jit(solution)/shard_map/front/pallas_call | solution.py:51
  29.7 10.5 %attend.1 = (bf16[3,3,64,2048]{3,2,1,0:T(8,128)(2,1)S(1)}, bf16[192,2048]{1,0:T(8,128)(2,1)S(1)}, f32[3,1,2048]{2,1,0:T(1,128)S(1)}) custom-call(s32[2]{0:T(128)S(1)} %pad_add_fusion.place_ref, s32[8]{0:T(128)S(1)} %get-tuple-element.120.lo_ref, s32[1,2048]{1,0:T(1,128)S(1)} %get-tuple-element.121.start_ref, ...), custom_call_target="tpu_custom_call" | custom-call | flops 5000000000 | bytes 1000 | tf_op jit(solution)/shard_map/attend/pallas_call | solution.py:51
  40.2 2.1 %collective-permute-done.4.refs_0_.dy2_ref = bf16[512,768]{1,0:T(8,128)(2,1)S(1)} collective-permute-done((bf16[512,768]{1,0:T(8,128)(2,1)S(1)}, bf16[512,768]{1,0:T(8,128)(2,1)S(1)}, u32[]{:S(2)}, u32[]{:S(2)}) %collective-permute-start.4) | collective-permute-done | bytes 786464 | tf_op jit(solution)/shard_map/ppermute | solution.py:452
  42.4 4.1 %ff_back.4 = (bf16[512,768]{1,0:T(8,128)(2,1)S(1)}, bf16[512,768]{1,0:T(8,128)(2,1)S(1)}, bf16[192,512]{1,0:T(8,128)(2,1)S(1)}, f32[768,768]{1,0:T(8,128)S(1)}, ...) custom-call(s32[2]{0:T(128)S(1)} %pad_add_fusion.place_ref, bf16[512,768]{1,0:T(8,128)(2,1)S(1)} %collective-permute-done.4.refs_0_.dy2_ref, ...), custom_call_target="tpu_custom_call" | custom-call | flops 2000000000 | bytes 1000 | tf_op jit(solution)/shard_map/ff_back/pallas_call | solution.py:51
  46.5 5.5 %ff_back.5 = (bf16[512,768]{1,0:T(8,128)(2,1)S(1)}, bf16[512,768]{1,0:T(8,128)(2,1)S(1)}, bf16[192,512]{1,0:T(8,128)(2,1)S(1)}, bf16[384,768]{1,0:T(8,128)(2,1)S...) custom-call(s32[2]{0:T(128)S(1)} %pad_add_fusion.place_ref, ...), custom_call_target="tpu_custom_call" | custom-call | flops 2000000000 | bytes 1000 | tf_op jit(solution)/shard_map/ff_back/pallas_call | solution.py:51
  56.1 13.6 %attend_back.1.dqkv_ref = bf16[3,3,64,2048]{3,2,1,0:T(8,128)(2,1)S(1)} custom-call(s32[2]{0:T(128)S(1)} %pad_add_fusion.place_ref, s32[8]{0:T(128)S(1)} %get-tuple-element.120.lo_ref, s32[1,2048]{1,0:T(1,128)S(1)} %get-tuple-element.121.start_ref, bf16[3,3,64,2048]{3,2,1,0:T(8,128)(2,1)S(1)} %get-tuple-element.148.qkv_ref, ...), custom_call_target="tpu_custom_call" | custom-call | flops 7000000000 | bytes 1000 | tf_op jit(solution)/shard_map/attend_back/pallas_call | solution.py:51
  70.7 2.7 %collective-permute-start.8 = (bf16[200,768]{1,0:T(8,128)(2,1)S(1)}, bf16[200,768]{1,0:T(8,128)(2,1)S(1)}, u32[]{:S(2)}, u32[]{:S(2)}) collective-permute-start(bf16[200,768]{1,0:T(8,128)(2,1)S(1)} %get-tuple-element.161), channel_id=1, source_target_pairs={{0,8},{4,12},{8,0},{12,4},{16,24},{20,28},{24,16},{28,20},{1,9},{5... | collective-permute-start | bytes 921608 | tf_op jit(solution)/shard_map/ppermute | solution.py:452
  74.0 4.4 %qkv_end.1 = (bf16[200,768]{1,0:T(8,128)(2,1)S(1)}, bf16[200,768]{1,0:T(8,128)(2,1)S(1)}, bf16[192,768]{1,0:T(8,128)(2,1)S(1)}, bf16[192,768]{1,0:T(8,128)(2,1)S(1)}) custom-call(s32[2]{0:T(128)S(1)} %pad_add_fusion.place_ref, bf16[3,3,64,2048]{3,2,1,0:T(8,128)(2,1)S(1)} %attend_back.1.dqkv_ref, bf16[1024,768]{1,0:T(8,128)(2,1)S(1)} %get-tuple-element.127.refs_4_.xh0_ref, ...), custom_call_target="tpu_custom_call" | custom-call | flops 1000000 | bytes 1000 | tf_op jit(solution)/shard_map/qkv_end/pallas_call | solution.py:51
  80.8 2.4 %collective-permute-done.9.gb_ref = bf16[192,768]{1,0:T(8,128)(2,1)S(1)} collective-permute-done((bf16[192,768]{1,0:T(8,128)(2,1)S(1)}, bf16[192,768]{1,0:T(8,128)(2,1)S(1)}, u32[]{:S(2)}, u32[]{:S(2)}) %collective-permute-start.9) | collective-permute-done | bytes 294944 | tf_op jit(solution)/shard_map/ppermute | solution.py:452
  83.9 2.6 %collective-permute-start.15 = (bf16[200,768]{1,0:T(8,128)(2,1)S(1)}, bf16[200,768]{1,0:T(8,128)(2,1)S(1)}, u32[]{:S(2)}, u32[]{:S(2)}) collective-permute-start(bf16[200,768]{1,0:T(8,128)(2,1)S(1)} %get-tuple-element.185), channel_id=1, source_target_pairs={{0,16},{4,20},{8,24},{12,28},{16,0},{20,4},{24,8},{28,12},{1,17},{... | collective-permute-start | bytes 921608 | tf_op jit(solution)/shard_map/ppermute | solution.py:452
  88.6 4.4 %collective-permute-done.11.gb_ref = bf16[192,768]{1,0:T(8,128)(2,1)S(1)} collective-permute-done((bf16[192,768]{1,0:T(8,128)(2,1)S(1)}, bf16[192,768]{1,0:T(8,128)(2,1)S(1)}, u32[]{:S(2)}, u32[]{:S(2)}) %collective-permute-start.11) | collective-permute-done | bytes 294944 | tf_op jit(solution)/shard_map/ppermute | solution.py:452
  93.9 3.6 %sides.1 = (f32[512,768]{1,0:T(8,128)S(1)}, f32[512,768]{1,0:T(8,128)S(1)}, f32[512,768]{1,0:T(8,128)S(1)}, f32[512,768]{1,0:T(8,128)S(1)}, bf16[2048,768]{1,0:T(8,128)(2,1)S(1)}) custom-call(bf16[3,3,64,2048]{3,2,1,0:T(8,128)(2,1)S(1)} %attend_back.1.dqkv_ref, bf16[1024,768]{1,0:T(8,128)(2,1)S(1)} %get-tuple-element.172.back0_ref, ...), custom_call_target="tpu_custom_call" | custom-call | flops 1000000 | bytes 1000 | tf_op jit(solution)/shard_map/sides/pallas_call | solution.py:51
  106.5 13.4 %collective-permute-done.16.got_ref = bf16[192,768]{1,0:T(8,128)(2,1)S(1)} collective-permute-done((bf16[192,768]{1,0:T(8,128)(2,1)S(1)}, bf16[192,768]{1,0:T(8,128)(2,1)S(1)}, u32[]{:S(2)}, u32[]{:S(2)}) %collective-permute-start.16) | collective-permute-done | bytes 294944 | tf_op jit(solution)/shard_map/ppermute | solution.py:452
  125.8 3.3 %all-to-all-start = ((f32[4,4,768]{2,1,0:T(4,128)}), f32[4,4,768]{2,1,0:T(4,128)S(1)}, u32[]{:S(2)}, u32[]{:S(2)}) async-start(f32[4,4,768]{2,1,0:T(4,128)} %broadcast_in_dim.18), calls=%async_computation | async-start | bytes 98304 | tf_op jit(solution)/shard_map/all_to_all | solution.py:675
  131.3 2.2 %join.2 = (bf16[384,768]{1,0:T(8,128)(2,1)}, bf16[384,768]{1,0:T(8,128)(2,1)}) custom-call(s32[2]{0:T(128)S(1)} %pad_add_fusion.place_ref, bf16[192,768]{1,0:T(8,128)(2,1)S(1)} %get-tuple-element.192.ma_ref, bf16[192,768]{1,0:T(8,128)(2,1)} %collective-permute-done.18.ga_ref, bf16[192,768]{1,0:T(8,128)(2,1)} %get-tuple-element.197.mb_ref, ...), custom_call_target="tpu_custom_call" | custom-call | flops 1000000 | bytes 1000 | tf_op jit(solution)/shard_map/join/pallas_call | solution.py:51
  138.7 3.1 %collective-permute-done.21.far_ref = bf16[1024,768]{1,0:T(8,128)(2,1)} collective-permute-done((bf16[1024,768]{1,0:T(8,128)(2,1)}, bf16[1024,768]{1,0:T(8,128)(2,1)}, u32[]{:S(2)}, u32[]{:S(2)}) %collective-permute-start.21) | collective-permute-done | bytes 1572896 | tf_op jit(solution)/shard_map/ppermute | solution.py:452
  143.2 2.8 %result.1 = bf16[512,768]{1,0:T(8,128)(2,1)} custom-call(bf16[512,768]{1,0:T(8,128)(2,1)S(1)} %bitcast.16, f32[512,768]{1,0:T(8,128)S(1)} %copy-done.5, bf16[2048,768]{1,0:T(8,128)(2,1)S(1)} %collective-permute-done.12.got_ref, bf16[1024,768]{1,0:T(8,128)(2,1)} %collective-permute-done.21.far_ref, bf16[768]{0:T(1024)(128)(2,1)S(1)} %copy-done.14, ...), custom_call_target="tpu_custom_call" | custom-call | flops 1000000 | bytes 1000 | tf_op jit(solution)/shard_map/result/pallas_call | solution.py:51
  146.1 3.7 %tokens_grad.1 = f32[512,768]{1,0:T(8,128)} custom-call(bf16[512,768]{1,0:T(8,128)(2,1)S(1)} %bitcast.17, bf16[512,768]{1,0:T(8,128)(2,1)S(1)} %bitcast.22, f32[512,768]{1,0:T(8,128)S(1)} %copy-done.17, bf16[2048,768]{1,0:T(8,128)(2,1)S(1)} %collective-permute-done.12.got_ref, bf16[1024,768]{1,0:T(8,128)(2,1)} %collective-permute-done.21.far_ref), custom_call_target="tpu_custom_call" | custom-call | flops 10000000000 | bytes 1000 | tf_op jit(solution)/shard_map/tokens_grad/pallas_call | solution.py:51
  155.3 4.0 %grads.1 = (f32[768,768]{1,0:T(8,128)}, f32[768,768]{1,0:T(8,128)}) custom-call(s32[2]{0:T(128)S(1)} %pad_add_fusion.place_ref, bf16[384,768]{1,0:T(8,128)(2,1)} %get-tuple-element.198.ma_ref, bf16[384,768]{1,0:T(8,128)(2,1)} %collective-permute-done.24.ga_ref, bf16[384,768]{1,0:T(8,128)(2,1)} %get-tuple-element.215.mb_ref, ...), custom_call_target="tpu_custom_call" | custom-call | flops 1000000 | bytes 1000 | tf_op jit(solution)/shard_map/grads/pallas_call | solution.py:51
  (117 shorter events, 49.9 us)
Async XLA Ops:
  0.7 6.1 %collective-permute-start = (bf16[512,768]{1,0:T(8,128)(2,1)}, bf16[512,768]{1,0:T(8,128)(2,1)}, u32[]{:S(2)}, u32[]{:S(2)}) collective-permute-start(bf16[512,768]{1,0:T(8,128)(2,1)} %bitcast.13), channel_id=1, source_target_pairs={{0,1},{1,0},{2,3},{3,2},{4,5},{5,4},{6,7},{7,6},{8,9},{9,8},{10,11... | collective-permute-start | bytes 2359304 | tf_op jit(solution)/shard_map/ppermute | solution.py:452
  1.2 10.7 %collective-permute-start.1 = (bf16[512,768]{1,0:T(8,128)(2,1)}, bf16[512,768]{1,0:T(8,128)(2,1)}, u32[]{:S(2)}, u32[]{:S(2)}) collective-permute-start(bf16[512,768]{1,0:T(8,128)(2,1)} %bitcast.18), channel_id=1, source_target_pairs={{0,1},{1,0},{2,3},{3,2},{4,5},{5,4},{6,7},{7,6},{8,9},{9,8},{10,11... | collective-permute-start | bytes 2359304 | tf_op jit(solution)/shard_map/ppermute | solution.py:452
  1.4 21.0 %collective-permute-start.2 = (bf16[512,768]{1,0:T(8,128)(2,1)}, bf16[512,768]{1,0:T(8,128)(2,1)}, u32[]{:S(2)}, u32[]{:S(2)}) collective-permute-start(bf16[512,768]{1,0:T(8,128)(2,1)} %bitcast.14), channel_id=1, source_target_pairs={{0,2},{1,3},{2,0},{3,1},{4,6},{5,7},{6,4},{7,5},{8,10},{9,11},{10,... | collective-permute-start | bytes 2359304 | tf_op jit(solution)/shard_map/ppermute | solution.py:452
  22.4 20.0 %collective-permute-start.4 = (bf16[512,768]{1,0:T(8,128)(2,1)S(1)}, bf16[512,768]{1,0:T(8,128)(2,1)S(1)}, u32[]{:S(2)}, u32[]{:S(2)}) collective-permute-start(bf16[512,768]{1,0:T(8,128)(2,1)S(1)} %bitcast.20), channel_id=1, source_target_pairs={{0,2},{1,3},{2,0},{3,1},{4,6},{5,7},{6,4},{7,5},{8,10},{9,11},{10,... | collective-permute-start | bytes 2359304 | tf_op jit(solution)/shard_map/ppermute | solution.py:452
  52.0 17.9 %collective-permute-start.7 = (bf16[384,768]{1,0:T(8,128)(2,1)S(1)}, bf16[384,768]{1,0:T(8,128)(2,1)S(1)}, u32[]{:S(2)}, u32[]{:S(2)}) collective-permute-start(bf16[384,768]{1,0:T(8,128)(2,1)S(1)} %get-tuple-element.157), channel_id=1, source_target_pairs={{0,8},{4,12},{8,0},{12,4},{16,24},{20,28},{24,16},{28,20},{1,9},{5... | collective-permute-start | bytes 1769480 | tf_op jit(solution)/shard_map/ppermute | solution.py:452
  54.0 15.8 %collective-permute-start.6 = (bf16[392,768]{1,0:T(8,128)(2,1)S(1)}, bf16[392,768]{1,0:T(8,128)(2,1)S(1)}, u32[]{:S(2)}, u32[]{:S(2)}) collective-permute-start(bf16[392,768]{1,0:T(8,128)(2,1)S(1)} %get-tuple-element.154), channel_id=1, source_target_pairs={{0,4},{4,0},{8,12},{12,8},{16,20},{20,16},{24,28},{28,24},{1,5},{5... | collective-permute-start | bytes 1806344 | tf_op jit(solution)/shard_map/ppermute | solution.py:452
  70.7 10.1 %collective-permute-start.8 = (bf16[200,768]{1,0:T(8,128)(2,1)S(1)}, bf16[200,768]{1,0:T(8,128)(2,1)S(1)}, u32[]{:S(2)}, u32[]{:S(2)}) collective-permute-start(bf16[200,768]{1,0:T(8,128)(2,1)S(1)} %get-tuple-element.161), channel_id=1, source_target_pairs={{0,8},{4,12},{8,0},{12,4},{16,24},{20,28},{24,16},{28,20},{1,9},{5... | collective-permute-start | bytes 921608 | tf_op jit(solution)/shard_map/ppermute | solution.py:452
  73.4 9.8 %collective-permute-start.9 = (bf16[192,768]{1,0:T(8,128)(2,1)S(1)}, bf16[192,768]{1,0:T(8,128)(2,1)S(1)}, u32[]{:S(2)}, u32[]{:S(2)}) collective-permute-start(bf16[192,768]{1,0:T(8,128)(2,1)S(1)} %get-tuple-element.164), channel_id=1, source_target_pairs={{0,4},{4,0},{8,12},{12,8},{16,20},{20,16},{24,28},{28,24},{1,5},{5... | collective-permute-start | bytes 884744 | tf_op jit(solution)/shard_map/ppermute | solution.py:452
  78.4 10.2 %collective-permute-start.10 = (bf16[200,768]{1,0:T(8,128)(2,1)S(1)}, bf16[200,768]{1,0:T(8,128)(2,1)S(1)}, u32[]{:S(2)}, u32[]{:S(2)}) collective-permute-start(bf16[200,768]{1,0:T(8,128)(2,1)S(1)} %get-tuple-element.166), channel_id=1, source_target_pairs={{0,4},{4,0},{8,12},{12,8},{16,20},{20,16},{24,28},{28,24},{1,5},{5... | collective-permute-start | bytes 921608 | tf_op jit(solution)/shard_map/ppermute | solution.py:452
  79.9 13.1 %collective-permute-start.11 = (bf16[192,768]{1,0:T(8,128)(2,1)S(1)}, bf16[192,768]{1,0:T(8,128)(2,1)S(1)}, u32[]{:S(2)}, u32[]{:S(2)}) collective-permute-start(bf16[192,768]{1,0:T(8,128)(2,1)S(1)} %get-tuple-element.169), channel_id=1, source_target_pairs={{0,8},{4,12},{8,0},{12,4},{16,24},{20,28},{24,16},{28,20},{1,9},{5... | collective-permute-start | bytes 884744 | tf_op jit(solution)/shard_map/ppermute | solution.py:452
  83.9 16.3 %collective-permute-start.15 = (bf16[200,768]{1,0:T(8,128)(2,1)S(1)}, bf16[200,768]{1,0:T(8,128)(2,1)S(1)}, u32[]{:S(2)}, u32[]{:S(2)}) collective-permute-start(bf16[200,768]{1,0:T(8,128)(2,1)S(1)} %get-tuple-element.185), channel_id=1, source_target_pairs={{0,16},{4,20},{8,24},{12,28},{16,0},{20,4},{24,8},{28,12},{1,17},{... | collective-permute-start | bytes 921608 | tf_op jit(solution)/shard_map/ppermute | solution.py:452
  100.3 19.7 %collective-permute-start.16 = (bf16[192,768]{1,0:T(8,128)(2,1)S(1)}, bf16[192,768]{1,0:T(8,128)(2,1)S(1)}, u32[]{:S(2)}, u32[]{:S(2)}) collective-permute-start(bf16[192,768]{1,0:T(8,128)(2,1)S(1)} %get-tuple-element.187.mine_ref), channel_id=1, source_target_pairs={{0,16},{4,20},{8,24},{12,28},{16,0},{20,4},{24,8},{28,12},{1,17},{... | collective-permute-start | bytes 884744 | tf_op jit(solution)/shard_map/ppermute | solution.py:452
  101.8 21.5 %collective-permute-start.17 = (bf16[104,768]{1,0:T(8,128)(2,1)S(1)}, bf16[104,768]{1,0:T(8,128)(2,1)S(1)}, u32[]{:S(2)}, u32[]{:S(2)}) collective-permute-start(bf16[104,768]{1,0:T(8,128)(2,1)S(1)} %get-tuple-element.193), channel_id=1, source_target_pairs={{0,16},{4,20},{8,24},{12,28},{16,0},{20,4},{24,8},{28,12},{1,17},{... | collective-permute-start | bytes 479240 | tf_op jit(solution)/shard_map/ppermute | solution.py:452
  104.8 37.0 %collective-permute-start.21 = (bf16[1024,768]{1,0:T(8,128)(2,1)}, bf16[1024,768]{1,0:T(8,128)(2,1)}, u32[]{:S(2)}, u32[]{:S(2)}) collective-permute-start(bf16[1024,768]{1,0:T(8,128)(2,1)} %forward.1), channel_id=1, source_target_pairs={{0,2},{1,3},{2,0},{3,1},{4,6},{5,7},{6,4},{7,5},{8,10},{9,11},{10,... | collective-permute-start | bytes 4718600 | tf_op jit(solution)/shard_map/ppermute | solution.py:452
  121.3 10.0 %collective-permute-start.18 = (bf16[192,768]{1,0:T(8,128)(2,1)S(1)}, bf16[192,768]{1,0:T(8,128)(2,1)}, u32[]{:S(2)}, u32[]{:S(2)}) collective-permute-start(bf16[192,768]{1,0:T(8,128)(2,1)S(1)} %get-tuple-element.192.ma_ref), channel_id=1, source_target_pairs={{0,8},{4,12},{8,0},{12,4},{16,24},{20,28},{24,16},{28,20},{1,9},{5... | collective-permute-start | bytes 884744 | tf_op jit(solution)/shard_map/ppermute | solution.py:452
  121.3 10.0 %collective-permute-start.19 = (bf16[192,768]{1,0:T(8,128)(2,1)}, bf16[192,768]{1,0:T(8,128)(2,1)}, u32[]{:S(2)}, u32[]{:S(2)}) collective-permute-start(bf16[192,768]{1,0:T(8,128)(2,1)} %get-tuple-element.197.mb_ref), channel_id=1, source_target_pairs={{0,4},{4,0},{8,12},{12,8},{16,20},{20,16},{24,28},{28,24},{1,5},{5... | collective-permute-start | bytes 884744 | tf_op jit(solution)/shard_map/ppermute | solution.py:452
  123.9 11.6 %collective-permute-start.20 = (bf16[96,768]{1,0:T(8,128)(2,1)}, bf16[96,768]{1,0:T(8,128)(2,1)}, u32[]{:S(2)}, u32[]{:S(2)}) collective-permute-start(bf16[96,768]{1,0:T(8,128)(2,1)} %get-tuple-element.195.mine_ref), channel_id=1, source_target_pairs={{0,16},{4,20},{8,24},{12,28},{16,0},{20,4},{24,8},{28,12},{1,17},{... | collective-permute-start | bytes 442376 | tf_op jit(solution)/shard_map/ppermute | solution.py:452
  125.8 23.9 %all-to-all-start = ((f32[4,4,768]{2,1,0:T(4,128)}), f32[4,4,768]{2,1,0:T(4,128)S(1)}, u32[]{:S(2)}, u32[]{:S(2)}) async-start(f32[4,4,768]{2,1,0:T(4,128)} %broadcast_in_dim.18), calls=%async_computation | async-start | bytes 98304 | tf_op jit(solution)/shard_map/all_to_all | solution.py:675
  133.5 21.8 %collective-permute-start.24 = (bf16[384,768]{1,0:T(8,128)(2,1)}, bf16[384,768]{1,0:T(8,128)(2,1)}, u32[]{:S(2)}, u32[]{:S(2)}) collective-permute-start(bf16[384,768]{1,0:T(8,128)(2,1)} %get-tuple-element.198.ma_ref), channel_id=1, source_target_pairs={{0,4},{4,0},{8,12},{12,8},{16,20},{20,16},{24,28},{28,24},{1,5},{5... | collective-permute-start | bytes 1769480 | tf_op jit(solution)/shard_map/ppermute | solution.py:452
  136.6 14.1 %collective-permute-start.23 = (bf16[96,768]{1,0:T(8,128)(2,1)S(1)}, bf16[96,768]{1,0:T(8,128)(2,1)}, u32[]{:S(2)}, u32[]{:S(2)}) collective-permute-start(bf16[96,768]{1,0:T(8,128)(2,1)S(1)} %get-tuple-element.212.mb_ref), channel_id=1, source_target_pairs={{0,4},{4,0},{8,12},{12,8},{16,20},{20,16},{24,28},{28,24},{1,5},{5... | collective-permute-start | bytes 442376 | tf_op jit(solution)/shard_map/ppermute | solution.py:452
  136.7 13.7 %collective-permute-start.22 = (bf16[96,768]{1,0:T(8,128)(2,1)S(1)}, bf16[96,768]{1,0:T(8,128)(2,1)}, u32[]{:S(2)}, u32[]{:S(2)}) collective-permute-start(bf16[96,768]{1,0:T(8,128)(2,1)S(1)} %get-tuple-element.200.ma_ref), channel_id=1, source_target_pairs={{0,8},{4,12},{8,0},{12,4},{16,24},{20,28},{24,16},{28,20},{1,9},{5... | collective-permute-start | bytes 442376 | tf_op jit(solution)/shard_map/ppermute | solution.py:452
  136.7 18.6 %collective-permute-start.25 = (bf16[384,768]{1,0:T(8,128)(2,1)}, bf16[384,768]{1,0:T(8,128)(2,1)}, u32[]{:S(2)}, u32[]{:S(2)}) collective-permute-start(bf16[384,768]{1,0:T(8,128)(2,1)} %get-tuple-element.215.mb_ref), channel_id=1, source_target_pairs={{0,8},{4,12},{8,0},{12,4},{16,24},{20,28},{24,16},{28,20},{1,9},{5... | collective-permute-start | bytes 1769480 | tf_op jit(solution)/shard_map/ppermute | solution.py:452
  151.7 7.9 %collective-permute-start.26 = (bf16[192,768]{1,0:T(8,128)(2,1)S(1)}, bf16[192,768]{1,0:T(8,128)(2,1)S(1)}, u32[]{:S(2)}, u32[]{:S(2)}) collective-permute-start(bf16[192,768]{1,0:T(8,128)(2,1)S(1)} %get-tuple-element.213.ma_ref), channel_id=1, source_target_pairs={{0,4},{4,0},{8,12},{12,8},{16,20},{20,16},{24,28},{28,24},{1,5},{5... | collective-permute-start | bytes 884744 | tf_op jit(solution)/shard_map/ppermute | solution.py:452
  153.3 7.9 %collective-permute-start.27 = (bf16[192,768]{1,0:T(8,128)(2,1)S(1)}, bf16[192,768]{1,0:T(8,128)(2,1)S(1)}, u32[]{:S(2)}, u32[]{:S(2)}) collective-permute-start(bf16[192,768]{1,0:T(8,128)(2,1)S(1)} %get-tuple-element.218.mb_ref), channel_id=1, source_target_pairs={{0,8},{4,12},{8,0},{12,4},{16,24},{20,28},{24,16},{28,20},{1,9},{5... | collective-permute-start | bytes 884744 | tf_op jit(solution)/shard_map/ppermute | solution.py:452
  (30 other events, 173.7 us)

commit v5 on v3

--- a/solution.py
+++ b/solution.py
@@ -22,7 +22,7 @@
 SEQUENCE = (
     "attend_back", "p1", "qkv_end", "p2", "q1", "sides", "q2", "p3",
     "forward", "p4", "q3", "p5", "q4", "result", "tokens_grad", "q5",
-    "p6", "vectors", "q6",
+    "p6", "q6", "vectors",
 )
 COSTS = {
     "attend": 10, "attend_back": 14, "ff_back": 4, "front": 2, "p3": 150, "p4": 60,

time: 160 us -> 162 us (1.012)
  transfers between devices with their start and end apart: 31 -> 31, of which waited for: 13 -> 13; matrix products, arithmetic and copies ran while one was open for 0% -> 0% of each run, Pallas kernels for 46% -> 47%
where the time goes in v5:
time: 162 us; the launch traced here: 161 us
  Pallas kernels  82.9 us (51%)
  waiting for transfers between devices  46.2 us (29%)
  starting transfers between devices  30.3 us (19%)
    pallas_call x27, Pallas kernels, call(): pl.pallas_call(kernel, out_shape=tuple(outs), in_specs=[SMEM if i in smem...  82.9 us
    ppermute x31, waiting for transfers between devices, swap(): return lax.ppermute(value, axis, [(i, i ^ distance) for i in range(size)])  46.2 us
    ppermute x31, starting transfers between devices, swap(): return lax.ppermute(value, axis, [(i, i ^ distance) for i in range(size)])  30.3 us
  transfers between devices with their start and end apart: 31, of which 13 were waited for; matrix products, arithmetic and copies ran while one was open for 0% of the time, Pallas kernels for 47%

profile of v5, /device:TPU:0, one launch (start us, length us, event | category | flops | bytes accessed | tf_op | source)
XLA Modules:
  0.0 161.4 jit_solution(15984590888901036138)
XLA Ops:
  1.4 2.9 %collective-permute-start.2 = (bf16[512,768]{1,0:T(8,128)(2,1)}, bf16[512,768]{1,0:T(8,128)(2,1)}, u32[]{:S(2)}, u32[]{:S(2)}) collective-permute-start(bf16[512,768]{1,0:T(8,128)(2,1)} %bitcast.14), channel_id=1, source_target_pairs={{0,2},{1,3},{2,0},{3,1},{4,6},{5,7},{6,4},{7,5},{8,10},{9,11},{10,... | collective-permute-start | bytes 2359304 | tf_op jit(solution)/shard_map/ppermute | solution.py:452
  6.9 5.1 %front.3 = (bf16[1024,768]{1,0:T(8,128)(2,1)S(1)}, bf16[1024,768]{1,0:T(8,128)(2,1)S(1)}, bf16[1024,768]{1,0:T(8,128)(2,1)S(1)}, bf16[3,3,64,1024]{3,2,1,0:T(8,128)(2,1)S(1)}) custom-call(s32[2]{0:T(128)S(1)} %pad_add_fusion.place_ref, bf16[512,768]{1,0:T(8,128)(2,1)S(1)} %bitcast.15, bf16[512,768]{1,0:T(8,128)(2,1)} %collective-permute-done.refs_1_, ...), custom_call_target="tpu_custom_call" | custom-call | flops 2000000000 | bytes 1000 | tf_op jit(solution)/shard_map/front/pallas_call | solution.py:51
  12.0 8.0 %ff_back.3 = (bf16[1024,768]{1,0:T(8,128)(2,1)S(1)}, bf16[1024,768]{1,0:T(8,128)(2,1)S(1)}, bf16[192,1024]{1,0:T(8,128)(2,1)S(1)}, f32[768,768]{1,0:T(8,128)S(1)...) custom-call(s32[2]{0:T(128)S(1)} %pad_add_fusion.place_ref, bf16[512,768]{1,0:T(8,128)(2,1)S(1)} %bitcast.19, ...), custom_call_target="tpu_custom_call" | custom-call | flops 4000000000 | bytes 1000 | tf_op jit(solution)/shard_map/ff_back/pallas_call | solution.py:51
  20.0 2.4 %collective-permute-done.2.refs_0_ = bf16[512,768]{1,0:T(8,128)(2,1)} collective-permute-done((bf16[512,768]{1,0:T(8,128)(2,1)}, bf16[512,768]{1,0:T(8,128)(2,1)}, u32[]{:S(2)}, u32[]{:S(2)}) %collective-permute-start.2) | collective-permute-done | bytes 786464 | tf_op jit(solution)/shard_map/ppermute | solution.py:452
  24.1 3.0 %front.4 = (bf16[512,768]{1,0:T(8,128)(2,1)S(1)}, bf16[512,768]{1,0:T(8,128)(2,1)S(1)}, bf16[512,768]{1,0:T(8,128)(2,1)S(1)}, bf16[3,3,64,512]{3,2,1,0:T(8,128)(2,1)S(1)}) custom-call(s32[2]{0:T(128)S(1)} %pad_add_fusion.place_ref, bf16[512,768]{1,0:T(8,128)(2,1)} %collective-permute-done.2.refs_0_, bf16[768]{0:T(1024)(128)(2,1)S(1)} %copy-done.6, ...), custom_call_target="tpu_custom_call" | custom-call | flops 1000000000 | bytes 1000 | tf_op jit(solution)/shard_map/front/pallas_call | solution.py:51
  27.1 2.6 %front.5 = (bf16[512,768]{1,0:T(8,128)(2,1)S(1)}, bf16[512,768]{1,0:T(8,128)(2,1)S(1)}, bf16[512,768]{1,0:T(8,128)(2,1)S(1)}, bf16[3,3,64,512]{3,2,1,0:T(8,128)(2,1)S(1)}) custom-call(s32[2]{0:T(128)S(1)} %pad_add_fusion.place_ref, bf16[512,768]{1,0:T(8,128)(2,1)S(1)} %collective-permute-done.3.refs_0_, bf16[768]{0:T(1024)(128)(2,1)S(1)} %copy-done.6, ...), custom_call_target="tpu_custom_call" | custom-call | flops 1000000000 | bytes 1000 | tf_op jit(solution)/shard_map/front/pallas_call | solution.py:51
  29.7 13.3 %attend.1 = (bf16[3,3,64,2048]{3,2,1,0:T(8,128)(2,1)S(1)}, bf16[192,2048]{1,0:T(8,128)(2,1)S(1)}, f32[3,1,2048]{2,1,0:T(1,128)S(1)}) custom-call(s32[2]{0:T(128)S(1)} %pad_add_fusion.place_ref, s32[8]{0:T(128)S(1)} %get-tuple-element.120.lo_ref, s32[1,2048]{1,0:T(1,128)S(1)} %get-tuple-element.121.start_ref, ...), custom_call_target="tpu_custom_call" | custom-call | flops 5000000000 | bytes 1000 | tf_op jit(solution)/shard_map/attend/pallas_call | solution.py:51
  43.3 4.1 %ff_back.4 = (bf16[512,768]{1,0:T(8,128)(2,1)S(1)}, bf16[512,768]{1,0:T(8,128)(2,1)S(1)}, bf16[192,512]{1,0:T(8,128)(2,1)S(1)}, f32[768,768]{1,0:T(8,128)S(1)}, ...) custom-call(s32[2]{0:T(128)S(1)} %pad_add_fusion.place_ref, bf16[512,768]{1,0:T(8,128)(2,1)S(1)} %collective-permute-done.4.refs_0_.dy2_ref, ...), custom_call_target="tpu_custom_call" | custom-call | flops 2000000000 | bytes 1000 | tf_op jit(solution)/shard_map/ff_back/pallas_call | solution.py:51
  47.4 5.5 %ff_back.5 = (bf16[512,768]{1,0:T(8,128)(2,1)S(1)}, bf16[512,768]{1,0:T(8,128)(2,1)S(1)}, bf16[192,512]{1,0:T(8,128)(2,1)S(1)}, bf16[384,768]{1,0:T(8,128)(2,1)S...) custom-call(s32[2]{0:T(128)S(1)} %pad_add_fusion.place_ref, ...), custom_call_target="tpu_custom_call" | custom-call | flops 2000000000 | bytes 1000 | tf_op jit(solution)/shard_map/ff_back/pallas_call | solution.py:51
  55.5 16.9 %attend_back.1.dqkv_ref = bf16[3,3,64,2048]{3,2,1,0:T(8,128)(2,1)S(1)} custom-call(s32[2]{0:T(128)S(1)} %pad_add_fusion.place_ref, s32[8]{0:T(128)S(1)} %get-tuple-element.120.lo_ref, s32[1,2048]{1,0:T(1,128)S(1)} %get-tuple-element.121.start_ref, bf16[3,3,64,2048]{3,2,1,0:T(8,128)(2,1)S(1)} %get-tuple-element.148.qkv_ref, ...), custom_call_target="tpu_custom_call" | custom-call | flops 7000000000 | bytes 1000 | tf_op jit(solution)/shard_map/attend_back/pallas_call | solution.py:51
  74.2 4.4 %qkv_end.1 = (bf16[200,768]{1,0:T(8,128)(2,1)S(1)}, bf16[200,768]{1,0:T(8,128)(2,1)S(1)}, bf16[192,768]{1,0:T(8,128)(2,1)S(1)}, bf16[192,768]{1,0:T(8,128)(2,1)S(1)}) custom-call(s32[2]{0:T(128)S(1)} %pad_add_fusion.place_ref, bf16[3,3,64,2048]{3,2,1,0:T(8,128)(2,1)S(1)} %attend_back.1.dqkv_ref, bf16[1024,768]{1,0:T(8,128)(2,1)S(1)} %get-tuple-element.127.refs_4_.xh0_ref, ...), custom_call_target="tpu_custom_call" | custom-call | flops 1000000 | bytes 1000 | tf_op jit(solution)/shard_map/qkv_end/pallas_call | solution.py:51
  84.1 2.5 %collective-permute-start.15 = (bf16[200,768]{1,0:T(8,128)(2,1)S(1)}, bf16[200,768]{1,0:T(8,128)(2,1)S(1)}, u32[]{:S(2)}, u32[]{:S(2)}) collective-permute-start(bf16[200,768]{1,0:T(8,128)(2,1)S(1)} %get-tuple-element.185), channel_id=1, source_target_pairs={{0,16},{4,20},{8,24},{12,28},{16,0},{20,4},{24,8},{28,12},{1,17},{... | collective-permute-start | bytes 921608 | tf_op jit(solution)/shard_map/ppermute | solution.py:452
  86.6 2.2 %collective-permute-done.10.ga_ref = bf16[200,768]{1,0:T(8,128)(2,1)S(1)} collective-permute-done((bf16[200,768]{1,0:T(8,128)(2,1)S(1)}, bf16[200,768]{1,0:T(8,128)(2,1)S(1)}, u32[]{:S(2)}, u32[]{:S(2)}) %collective-permute-start.10) | collective-permute-done | bytes 307232 | tf_op jit(solution)/shard_map/ppermute | solution.py:452
  88.7 5.0 %collective-permute-done.11.gb_ref = bf16[192,768]{1,0:T(8,128)(2,1)S(1)} collective-permute-done((bf16[192,768]{1,0:T(8,128)(2,1)S(1)}, bf16[192,768]{1,0:T(8,128)(2,1)S(1)}, u32[]{:S(2)}, u32[]{:S(2)}) %collective-permute-start.11) | collective-permute-done | bytes 294944 | tf_op jit(solution)/shard_map/ppermute | solution.py:452
  94.6 3.6 %sides.1 = (f32[512,768]{1,0:T(8,128)S(1)}, f32[512,768]{1,0:T(8,128)S(1)}, f32[512,768]{1,0:T(8,128)S(1)}, f32[512,768]{1,0:T(8,128)S(1)}, bf16[2048,768]{1,0:T(8,128)(2,1)S(1)}) custom-call(bf16[3,3,64,2048]{3,2,1,0:T(8,128)(2,1)S(1)} %attend_back.1.dqkv_ref, bf16[1024,768]{1,0:T(8,128)(2,1)S(1)} %get-tuple-element.172.back0_ref, ...), custom_call_target="tpu_custom_call" | custom-call | flops 1000000 | bytes 1000 | tf_op jit(solution)/shard_map/sides/pallas_call | solution.py:51
  98.3 2.6 %collective-permute-done.13.ga_ref = bf16[104,768]{1,0:T(8,128)(2,1)S(1)} collective-permute-done((bf16[104,768]{1,0:T(8,128)(2,1)S(1)}, bf16[104,768]{1,0:T(8,128)(2,1)S(1)}, u32[]{:S(2)}, u32[]{:S(2)}) %collective-permute-start.13) | collective-permute-done | bytes 159776 | tf_op jit(solution)/shard_map/ppermute | solution.py:452
  106.7 13.9 %collective-permute-done.16.got_ref = bf16[192,768]{1,0:T(8,128)(2,1)S(1)} collective-permute-done((bf16[192,768]{1,0:T(8,128)(2,1)S(1)}, bf16[192,768]{1,0:T(8,128)(2,1)S(1)}, u32[]{:S(2)}, u32[]{:S(2)}) %collective-permute-start.16) | collective-permute-done | bytes 294944 | tf_op jit(solution)/shard_map/ppermute | solution.py:452
  124.7 7.0 %collective-permute-done.18.ga_ref = bf16[192,768]{1,0:T(8,128)(2,1)S(1)} collective-permute-done((bf16[192,768]{1,0:T(8,128)(2,1)S(1)}, bf16[192,768]{1,0:T(8,128)(2,1)S(1)}, u32[]{:S(2)}, u32[]{:S(2)}) %collective-permute-start.18) | collective-permute-done | bytes 294944 | tf_op jit(solution)/shard_map/ppermute | solution.py:452
  137.1 3.6 %collective-permute-done.21.far_ref = bf16[1024,768]{1,0:T(8,128)(2,1)S(1)} collective-permute-done((bf16[1024,768]{1,0:T(8,128)(2,1)S(1)}, bf16[1024,768]{1,0:T(8,128)(2,1)S(1)}, u32[]{:S(2)}, u32[]{:S(2)}) %collective-permute-start.21) | collective-permute-done | bytes 1572896 | tf_op jit(solution)/shard_map/ppermute | solution.py:452
  142.0 2.3 %tokens_grad.1 = f32[512,768]{1,0:T(8,128)} custom-call(bf16[512,768]{1,0:T(8,128)(2,1)S(1)} %bitcast.17, bf16[512,768]{1,0:T(8,128)(2,1)S(1)} %bitcast.22, f32[512,768]{1,0:T(8,128)S(1)} %get-tuple-element.202.keep_ref, bf16[2048,768]{1,0:T(8,128)(2,1)S(1)} %collective-permute-done.12.got_ref, bf16[1024,768]{1,0:T(8,128)(2,1)S(1)} %collective-permute-done.21.far_ref), custom_call_target="tpu_custom_call" | custom-call | flops 10000000000 | bytes 1000 | tf_op jit(solution)/shard_map/tokens_grad/pallas_call | solution.py:51
  144.4 5.3 %collective-permute-done.23.gb_ref = bf16[96,768]{1,0:T(8,128)(2,1)S(1)} collective-permute-done((bf16[96,768]{1,0:T(8,128)(2,1)S(1)}, bf16[96,768]{1,0:T(8,128)(2,1)S(1)}, u32[]{:S(2)}, u32[]{:S(2)}) %collective-permute-start.23) | collective-permute-done | bytes 147488 | tf_op jit(solution)/shard_map/ppermute | solution.py:452
  152.1 2.1 %collective-permute-start.29 = (f32[4,768]{1,0:T(4,128)S(1)}, f32[4,768]{1,0:T(4,128)S(1)}, u32[]{:S(2)}, u32[]{:S(2)}) collective-permute-start(f32[4,768]{1,0:T(4,128)S(1)} %pad_maximum_fusion.n0_ref), channel_id=1, source_target_pairs={{0,2},{1,3},{2,0},{3,1},{4,6},{5,7},{6,4},{7,5},{8,10},{9,11},{10,... | collective-permute-start | bytes 36872 | tf_op jit(solution)/shard_map/ppermute | solution.py:452
  154.2 3.0 %grads.1 = (f32[768,768]{1,0:T(8,128)}, f32[768,768]{1,0:T(8,128)}) custom-call(s32[2]{0:T(128)S(1)} %pad_add_fusion.place_ref, bf16[384,768]{1,0:T(8,128)(2,1)S(1)} %get-tuple-element.198.ma_ref, bf16[384,768]{1,0:T(8,128)(2,1)S(1)} %collective-permute-done.24.ga_ref, bf16[384,768]{1,0:T(8,128)(2,1)S(1)} %get-tuple-element.208.mb_ref, ...), custom_call_target="tpu_custom_call" | custom-call | flops 1000000 | bytes 1000 | tf_op jit(solution)/shard_map/grads/pallas_call | solution.py:51
  158.7 2.1 %spread.1 = (f32[576,768]{1,0:T(8,128)}, f32[192,768]{1,0:T(8,128)}) custom-call(s32[2]{0:T(128)S(1)} %pad_add_fusion.place_ref, bf16[192,768]{1,0:T(8,128)(2,1)S(1)} %get-tuple-element.206.ma_ref, bf16[192,768]{1,0:T(8,128)(2,1)S(1)} %collective-permute-done.26.ga_ref, bf16[192,768]{1,0:T(8,128)(2,1)S(1)} %get-tuple-element.211.mb_ref, ...), custom_call_target="tpu_custom_call" | custom-call | flops 1000000 | bytes 1000 | tf_op jit(solution)/shard_map/spread/pallas_call | solution.py:51
  (104 shorter events, 36.9 us)
Async XLA Ops:
  1.2 10.7 %collective-permute-start.1 = (bf16[512,768]{1,0:T(8,128)(2,1)}, bf16[512,768]{1,0:T(8,128)(2,1)}, u32[]{:S(2)}, u32[]{:S(2)}) collective-permute-start(bf16[512,768]{1,0:T(8,128)(2,1)} %bitcast.18), channel_id=1, source_target_pairs={{0,1},{1,0},{2,3},{3,2},{4,5},{5,4},{6,7},{7,6},{8,9},{9,8},{10,11... | collective-permute-start | bytes 2359304 | tf_op jit(solution)/shard_map/ppermute | solution.py:452
  1.4 21.0 %collective-permute-start.2 = (bf16[512,768]{1,0:T(8,128)(2,1)}, bf16[512,768]{1,0:T(8,128)(2,1)}, u32[]{:S(2)}, u32[]{:S(2)}) collective-permute-start(bf16[512,768]{1,0:T(8,128)(2,1)} %bitcast.14), channel_id=1, source_target_pairs={{0,2},{1,3},{2,0},{3,1},{4,6},{5,7},{6,4},{7,5},{8,10},{9,11},{10,... | collective-permute-start | bytes 2359304 | tf_op jit(solution)/shard_map/ppermute | solution.py:452
  22.4 20.6 %collective-permute-start.4 = (bf16[512,768]{1,0:T(8,128)(2,1)S(1)}, bf16[512,768]{1,0:T(8,128)(2,1)S(1)}, u32[]{:S(2)}, u32[]{:S(2)}) collective-permute-start(bf16[512,768]{1,0:T(8,128)(2,1)S(1)} %bitcast.20), channel_id=1, source_target_pairs={{0,2},{1,3},{2,0},{3,1},{4,6},{5,7},{6,4},{7,5},{8,10},{9,11},{10,... | collective-permute-start | bytes 2359304 | tf_op jit(solution)/shard_map/ppermute | solution.py:452
  52.9 19.6 %collective-permute-start.7 = (bf16[384,768]{1,0:T(8,128)(2,1)S(1)}, bf16[384,768]{1,0:T(8,128)(2,1)S(1)}, u32[]{:S(2)}, u32[]{:S(2)}) collective-permute-start(bf16[384,768]{1,0:T(8,128)(2,1)S(1)} %get-tuple-element.157), channel_id=1, source_target_pairs={{0,8},{4,12},{8,0},{12,4},{16,24},{20,28},{24,16},{28,20},{1,9},{5... | collective-permute-start | bytes 1769480 | tf_op jit(solution)/shard_map/ppermute | solution.py:452
  53.9 18.6 %collective-permute-start.6 = (bf16[392,768]{1,0:T(8,128)(2,1)S(1)}, bf16[392,768]{1,0:T(8,128)(2,1)S(1)}, u32[]{:S(2)}, u32[]{:S(2)}) collective-permute-start(bf16[392,768]{1,0:T(8,128)(2,1)S(1)} %get-tuple-element.154), channel_id=1, source_target_pairs={{0,4},{4,0},{8,12},{12,8},{16,20},{20,16},{24,28},{28,24},{1,5},{5... | collective-permute-start | bytes 1806344 | tf_op jit(solution)/shard_map/ppermute | solution.py:452
  73.3 9.6 %collective-permute-start.8 = (bf16[200,768]{1,0:T(8,128)(2,1)S(1)}, bf16[200,768]{1,0:T(8,128)(2,1)S(1)}, u32[]{:S(2)}, u32[]{:S(2)}) collective-permute-start(bf16[200,768]{1,0:T(8,128)(2,1)S(1)} %get-tuple-element.161), channel_id=1, source_target_pairs={{0,8},{4,12},{8,0},{12,4},{16,24},{20,28},{24,16},{28,20},{1,9},{5... | collective-permute-start | bytes 921608 | tf_op jit(solution)/shard_map/ppermute | solution.py:452
  73.4 9.9 %collective-permute-start.9 = (bf16[192,768]{1,0:T(8,128)(2,1)S(1)}, bf16[192,768]{1,0:T(8,128)(2,1)S(1)}, u32[]{:S(2)}, u32[]{:S(2)}) collective-permute-start(bf16[192,768]{1,0:T(8,128)(2,1)S(1)} %get-tuple-element.164), channel_id=1, source_target_pairs={{0,4},{4,0},{8,12},{12,8},{16,20},{20,16},{24,28},{28,24},{1,5},{5... | collective-permute-start | bytes 884744 | tf_op jit(solution)/shard_map/ppermute | solution.py:452
  78.6 10.2 %collective-permute-start.10 = (bf16[200,768]{1,0:T(8,128)(2,1)S(1)}, bf16[200,768]{1,0:T(8,128)(2,1)S(1)}, u32[]{:S(2)}, u32[]{:S(2)}) collective-permute-start(bf16[200,768]{1,0:T(8,128)(2,1)S(1)} %get-tuple-element.166), channel_id=1, source_target_pairs={{0,4},{4,0},{8,12},{12,8},{16,20},{20,16},{24,28},{28,24},{1,5},{5... | collective-permute-start | bytes 921608 | tf_op jit(solution)/shard_map/ppermute | solution.py:452
  80.0 13.8 %collective-permute-start.11 = (bf16[192,768]{1,0:T(8,128)(2,1)S(1)}, bf16[192,768]{1,0:T(8,128)(2,1)S(1)}, u32[]{:S(2)}, u32[]{:S(2)}) collective-permute-start(bf16[192,768]{1,0:T(8,128)(2,1)S(1)} %get-tuple-element.169), channel_id=1, source_target_pairs={{0,8},{4,12},{8,0},{12,4},{16,24},{20,28},{24,16},{28,20},{1,9},{5... | collective-permute-start | bytes 884744 | tf_op jit(solution)/shard_map/ppermute | solution.py:452
  84.1 17.5 %collective-permute-start.15 = (bf16[200,768]{1,0:T(8,128)(2,1)S(1)}, bf16[200,768]{1,0:T(8,128)(2,1)S(1)}, u32[]{:S(2)}, u32[]{:S(2)}) collective-permute-start(bf16[200,768]{1,0:T(8,128)(2,1)S(1)} %get-tuple-element.185), channel_id=1, source_target_pairs={{0,16},{4,20},{8,24},{12,28},{16,0},{20,4},{24,8},{28,12},{1,17},{... | collective-permute-start | bytes 921608 | tf_op jit(solution)/shard_map/ppermute | solution.py:452
  101.7 18.9 %collective-permute-start.16 = (bf16[192,768]{1,0:T(8,128)(2,1)S(1)}, bf16[192,768]{1,0:T(8,128)(2,1)S(1)}, u32[]{:S(2)}, u32[]{:S(2)}) collective-permute-start(bf16[192,768]{1,0:T(8,128)(2,1)S(1)} %get-tuple-element.187.mine_ref), channel_id=1, source_target_pairs={{0,16},{4,20},{8,24},{12,28},{16,0},{20,4},{24,8},{28,12},{1,17},{... | collective-permute-start | bytes 884744 | tf_op jit(solution)/shard_map/ppermute | solution.py:452
  102.7 21.0 %collective-permute-start.17 = (bf16[104,768]{1,0:T(8,128)(2,1)S(1)}, bf16[104,768]{1,0:T(8,128)(2,1)S(1)}, u32[]{:S(2)}, u32[]{:S(2)}) collective-permute-start(bf16[104,768]{1,0:T(8,128)(2,1)S(1)} %get-tuple-element.193), channel_id=1, source_target_pairs={{0,16},{4,20},{8,24},{12,28},{16,0},{20,4},{24,8},{28,12},{1,17},{... | collective-permute-start | bytes 479240 | tf_op jit(solution)/shard_map/ppermute | solution.py:452
  105.0 35.8 %collective-permute-start.21 = (bf16[1024,768]{1,0:T(8,128)(2,1)S(1)}, bf16[1024,768]{1,0:T(8,128)(2,1)S(1)}, u32[]{:S(2)}, u32[]{:S(2)}) collective-permute-start(bf16[1024,768]{1,0:T(8,128)(2,1)S(1)} %forward.1), channel_id=1, source_target_pairs={{0,2},{1,3},{2,0},{3,1},{4,6},{5,7},{6,4},{7,5},{8,10},{9,11},{10,... | collective-permute-start | bytes 4718600 | tf_op jit(solution)/shard_map/ppermute | solution.py:452
  121.2 10.5 %collective-permute-start.18 = (bf16[192,768]{1,0:T(8,128)(2,1)S(1)}, bf16[192,768]{1,0:T(8,128)(2,1)S(1)}, u32[]{:S(2)}, u32[]{:S(2)}) collective-permute-start(bf16[192,768]{1,0:T(8,128)(2,1)S(1)} %get-tuple-element.192.ma_ref), channel_id=1, source_target_pairs={{0,8},{4,12},{8,0},{12,4},{16,24},{20,28},{24,16},{28,20},{1,9},{5... | collective-permute-start | bytes 884744 | tf_op jit(solution)/shard_map/ppermute | solution.py:452
  121.3 10.4 %collective-permute-start.19 = (bf16[192,768]{1,0:T(8,128)(2,1)S(1)}, bf16[192,768]{1,0:T(8,128)(2,1)S(1)}, u32[]{:S(2)}, u32[]{:S(2)}) collective-permute-start(bf16[192,768]{1,0:T(8,128)(2,1)S(1)} %get-tuple-element.197.mb_ref), channel_id=1, source_target_pairs={{0,4},{4,0},{8,12},{12,8},{16,20},{20,16},{24,28},{28,24},{1,5},{5... | collective-permute-start | bytes 884744 | tf_op jit(solution)/shard_map/ppermute | solution.py:452
  123.7 10.6 %collective-permute-start.20 = (bf16[96,768]{1,0:T(8,128)(2,1)S(1)}, bf16[96,768]{1,0:T(8,128)(2,1)S(1)}, u32[]{:S(2)}, u32[]{:S(2)}) collective-permute-start(bf16[96,768]{1,0:T(8,128)(2,1)S(1)} %get-tuple-element.195.mine_ref), channel_id=1, source_target_pairs={{0,16},{4,20},{8,24},{12,28},{16,0},{20,4},{24,8},{28,12},{1,17},{... | collective-permute-start | bytes 442376 | tf_op jit(solution)/shard_map/ppermute | solution.py:452
  132.4 21.9 %collective-permute-start.24 = (bf16[384,768]{1,0:T(8,128)(2,1)S(1)}, bf16[384,768]{1,0:T(8,128)(2,1)S(1)}, u32[]{:S(2)}, u32[]{:S(2)}) collective-permute-start(bf16[384,768]{1,0:T(8,128)(2,1)S(1)} %get-tuple-element.198.ma_ref), channel_id=1, source_target_pairs={{0,4},{4,0},{8,12},{12,8},{16,20},{20,16},{24,28},{28,24},{1,5},{5... | collective-permute-start | bytes 1769480 | tf_op jit(solution)/shard_map/ppermute | solution.py:452
  134.8 14.9 %collective-permute-start.23 = (bf16[96,768]{1,0:T(8,128)(2,1)S(1)}, bf16[96,768]{1,0:T(8,128)(2,1)S(1)}, u32[]{:S(2)}, u32[]{:S(2)}) collective-permute-start(bf16[96,768]{1,0:T(8,128)(2,1)S(1)} %get-tuple-element.205.mb_ref), channel_id=1, source_target_pairs={{0,4},{4,0},{8,12},{12,8},{16,20},{20,16},{24,28},{28,24},{1,5},{5... | collective-permute-start | bytes 442376 | tf_op jit(solution)/shard_map/ppermute | solution.py:452
  135.1 9.3 %collective-permute-start.22 = (bf16[96,768]{1,0:T(8,128)(2,1)S(1)}, bf16[96,768]{1,0:T(8,128)(2,1)S(1)}, u32[]{:S(2)}, u32[]{:S(2)}) collective-permute-start(bf16[96,768]{1,0:T(8,128)(2,1)S(1)} %get-tuple-element.200.ma_ref), channel_id=1, source_target_pairs={{0,8},{4,12},{8,0},{12,4},{16,24},{20,28},{24,16},{28,20},{1,9},{5... | collective-permute-start | bytes 442376 | tf_op jit(solution)/shard_map/ppermute | solution.py:452
  135.1 17.0 %collective-permute-start.25 = (bf16[384,768]{1,0:T(8,128)(2,1)S(1)}, bf16[384,768]{1,0:T(8,128)(2,1)S(1)}, u32[]{:S(2)}, u32[]{:S(2)}) collective-permute-start(bf16[384,768]{1,0:T(8,128)(2,1)S(1)} %get-tuple-element.208.mb_ref), channel_id=1, source_target_pairs={{0,8},{4,12},{8,0},{12,4},{16,24},{20,28},{24,16},{28,20},{1,9},{5... | collective-permute-start | bytes 1769480 | tf_op jit(solution)/shard_map/ppermute | solution.py:452
  150.3 7.0 %collective-permute-start.26 = (bf16[192,768]{1,0:T(8,128)(2,1)S(1)}, bf16[192,768]{1,0:T(8,128)(2,1)S(1)}, u32[]{:S(2)}, u32[]{:S(2)}) collective-permute-start(bf16[192,768]{1,0:T(8,128)(2,1)S(1)} %get-tuple-element.206.ma_ref), channel_id=1, source_target_pairs={{0,4},{4,0},{8,12},{12,8},{16,20},{20,16},{24,28},{28,24},{1,5},{5... | collective-permute-start | bytes 884744 | tf_op jit(solution)/shard_map/ppermute | solution.py:452
  152.0 6.7 %collective-permute-start.27 = (bf16[192,768]{1,0:T(8,128)(2,1)S(1)}, bf16[192,768]{1,0:T(8,128)(2,1)S(1)}, u32[]{:S(2)}, u32[]{:S(2)}) collective-permute-start(bf16[192,768]{1,0:T(8,128)(2,1)S(1)} %get-tuple-element.211.mb_ref), channel_id=1, source_target_pairs={{0,8},{4,12},{8,0},{12,4},{16,24},{20,28},{24,16},{28,20},{1,9},{5... | collective-permute-start | bytes 884744 | tf_op jit(solution)/shard_map/ppermute | solution.py:452
  152.0 8.8 %collective-permute-start.30 = (f32[4,768]{1,0:T(4,128)S(1)}, f32[4,768]{1,0:T(4,128)S(1)}, u32[]{:S(2)}, u32[]{:S(2)}) collective-permute-start(f32[4,768]{1,0:T(4,128)S(1)} %pad_maximum_fusion.n0_ref), channel_id=1, source_target_pairs={{0,3},{1,2},{2,1},{3,0},{4,7},{5,6},{6,5},{7,4},{8,11},{9,10},{10,... | collective-permute-start | bytes 36872 | tf_op jit(solution)/shard_map/ppermute | solution.py:452
  152.1 8.7 %collective-permute-start.29 = (f32[4,768]{1,0:T(4,128)S(1)}, f32[4,768]{1,0:T(4,128)S(1)}, u32[]{:S(2)}, u32[]{:S(2)}) collective-permute-start(f32[4,768]{1,0:T(4,128)S(1)} %pad_maximum_fusion.n0_ref), channel_id=1, source_target_pairs={{0,2},{1,3},{2,0},{3,1},{4,6},{5,7},{6,4},{7,5},{8,10},{9,11},{10,... | collective-permute-start | bytes 36872 | tf_op jit(solution)/shard_map/ppermute | solution.py:452
  (24 other events, 142.0 us)
